TPU v7x, 128 devices: a whole 4x4x4 slice. The times are simulated.
128 devices in a mesh: seq: 32 (over x, y, z_hi), tp: 4 (over z_lo, core).
Axes of the slice: x: 4, y: 4, z: 4 (z_hi: 2, z_lo: 2; z = z_hi * 2 + z_lo), core: 2. Of those that a mesh axis runs over, the one named last changes fastest.
Arguments:
- queries: bfloat16 [16384, 4096], P('seq', 'tp'), may hold values from -6 to 6
- token_keys: bfloat16 [16384, 4096], P('seq', 'tp'), may hold values from -6 to 6
- token_values: bfloat16 [16384, 4096], P('seq', 'tp'), may hold values from -6 to 6
- out_weight: bfloat16 [4096, 4096], P('tp'), may hold values from -0.09375 to 0.09375
- out_grad: bfloat16 [16384, 4096], P('seq'), may hold values from -6 to 6
Outputs:
- layer_out: bfloat16 [16384, 4096], P('seq', 'tp')
- query_grad: bfloat16 [16384, 4096], P('seq', 'tp')
- key_grad: bfloat16 [16384, 4096], P('seq', 'tp')
- value_grad: bfloat16 [16384, 4096], P('seq', 'tp')
- weight_grad: float32 [4096, 4096], P('tp', 'seq')
All inputs are finite; a program needn't handle non-finite values.
Results may differ from a plain program's by a relative error of at most 0.024.
Values may be sent and summed in bfloat16 or wider, within the bound.
No kernel may reach another device: no remote copies, remote signals or barrier semaphores. Data moves between devices by JAX's collectives and lax.ppermute only.
A program may use at most 256 MiB of HBM per device.

v0:
```python
import math

import jax
import jax.numpy as jnp
from jax import lax
from jax.sharding import PartitionSpec as P

DH = 128
FB = 128
P1 = 16
P2 = 256


def with_halo(cells, sides, width):
    for axis, dim in sides:
        count = lax.axis_size(axis)
        ends = count - 1
        head = lax.slice_in_dim(cells, 0, width, axis=dim)
        tail = lax.slice_in_dim(cells, cells.shape[dim] - width, cells.shape[dim], axis=dim)
        cells = jnp.concatenate(
            [
                lax.ppermute(tail, axis, [(i, (i + 1) % count) for i in range(ends)]),
                cells,
                lax.ppermute(head, axis, [((i + 1) % count, i) for i in range(ends)]),
            ],
            axis=dim,
        )
    return cells


def joined_along(tiles, dim):
    tiles = jnp.moveaxis(tiles, 0, dim)
    lengths = tiles.shape
    return tiles.reshape(*lengths[:dim], lengths[dim] * lengths[dim + 1], *lengths[dim + 2 :])


def copy_for_each(x, axis):
    copies = jnp.broadcast_to(x, (lax.axis_size(axis), *x.shape))
    return lax.all_to_all(copies, axis, split_axis=0, concat_axis=0, tiled=True)


def gathered_copies(x, axis, dim):
    return joined_along(copy_for_each(x, axis), dim)


def cut_along(x, dim, peers):
    before, after = (x.shape[:dim], x.shape[dim + 1 :])
    return jnp.moveaxis(x.reshape(*before, peers, -1, *after), dim, 0)


def summed_on_arrival(x, axis, dim):
    peers = lax.axis_size(axis)
    tiles = lax.all_to_all(cut_along(x, dim, peers), axis, 0, 0, tiled=True)
    return jnp.sum(tiles, axis=0)


def product(form, left, right):
    return jnp.einsum(form, left, right, preferred_element_type=jnp.float32)


def pooled(stacked, group_size):
    count_rows = stacked.shape[1] // group_size
    summed = (
        stacked.astype(jnp.float32)
        .reshape(stacked.shape[0], count_rows, group_size, stacked.shape[2])
        .sum(axis=2)
    )
    return (summed / group_size).astype(jnp.bfloat16)


def expand_rows(grad_parts, group_size):
    shaped = jnp.broadcast_to(
        grad_parts[:, :, None, :] / group_size,
        (grad_parts.shape[0], grad_parts.shape[1], group_size, grad_parts.shape[2]),
    )
    return shaped.reshape(
        grad_parts.shape[0], grad_parts.shape[1] * group_size, grad_parts.shape[2]
    )


def fold_windows(window_grad, blocks):
    leading = window_grad.shape[0]
    split_grad = window_grad.reshape(leading, blocks, 3, FB, -1)
    first_part = jnp.pad(split_grad[:, :, 0], ((0, 0), (0, 2), (0, 0), (0, 0)))
    middle = jnp.pad(split_grad[:, :, 1], ((0, 0), (1, 1), (0, 0), (0, 0)))
    last_part = jnp.pad(split_grad[:, :, 2], ((0, 0), (2, 0), (0, 0), (0, 0)))
    return (first_part + middle + last_part).reshape(leading, (blocks + 2) * FB, -1)


def attend(query_rows, extended, extended_pooled, coarse_rows, grad_rows, position, seq_count):
    tokens_here, features = query_rows.shape
    head_count = features // DH
    blocks = tokens_here // FB
    pooled_rows = extended_pooled.shape[1] // 3
    coarse_count = coarse_rows.shape[1]
    scaling = 1.0 / math.sqrt(DH)
    query_blocks = query_rows.reshape(blocks, FB, head_count, DH)
    token_blocks = extended.reshape(2, blocks + 2, FB, head_count, DH)
    windows = jnp.concatenate(
        [token_blocks[:, offset : offset + blocks] for offset in range(3)], axis=2
    )
    coarse_all = jnp.concatenate([extended_pooled, coarse_rows], axis=1).reshape(
        2, 3 * pooled_rows + coarse_count, head_count, DH
    )
    block_ids = jnp.arange(blocks, dtype=jnp.int32)[:, None]
    window_rows = block_ids * FB + jnp.arange(3 * FB, dtype=jnp.int32)[None, :]
    first_dev = position == 0
    last_dev = position == seq_count - 1
    fine_mask = jnp.logical_not(
        jnp.logical_or(
            jnp.logical_and(window_rows < FB, first_dev),
            jnp.logical_and(window_rows >= tokens_here + FB, last_dev),
        )
    )
    group_ids = jnp.arange(3 * pooled_rows, dtype=jnp.int32)
    group_dev = group_ids // pooled_rows
    present = jnp.logical_not(
        jnp.logical_or(
            jnp.logical_and(group_dev == 0, first_dev), jnp.logical_and(group_dev == 2, last_dev)
        )
    )
    distance = group_ids[None, :] * P1 // FB - blocks - block_ids
    near_mask = jnp.logical_and(present[None, :], jnp.abs(distance) > 1)
    coarse_dev = jnp.arange(coarse_count, dtype=jnp.int32) * P2 // tokens_here
    far_mask = jnp.abs(coarse_dev - position) > 1
    coarse_mask = jnp.concatenate(
        [near_mask, jnp.broadcast_to(far_mask[None, :], (blocks, coarse_count))], axis=1
    )
    level_bias = jnp.concatenate(
        [
            jnp.full((3 * pooled_rows,), math.log(P1), jnp.float32),
            jnp.full((coarse_count,), math.log(P2), jnp.float32),
        ]
    )
    fine_scores = jnp.where(
        fine_mask[None, :, None, :],
        product("bqhd,bkhd->hbqk", query_blocks, windows[0]) * scaling,
        -jnp.inf,
    )
    coarse_scores = jnp.where(
        coarse_mask[None, :, None, :],
        product("bqhd,khd->hbqk", query_blocks, coarse_all[0]) * scaling + level_bias,
        -jnp.inf,
    )
    row_peak = jnp.maximum(fine_scores.max(axis=-1), coarse_scores.max(axis=-1))
    row_total = jnp.exp(fine_scores - row_peak[..., None]).sum(axis=-1) + jnp.exp(
        coarse_scores - row_peak[..., None]
    ).sum(axis=-1)
    log_total = row_peak + jnp.log(row_total)
    fine_prob = jnp.exp(fine_scores - log_total[..., None])
    coarse_prob = jnp.exp(coarse_scores - log_total[..., None])
    fine_round = fine_prob.astype(jnp.bfloat16)
    coarse_round = coarse_prob.astype(jnp.bfloat16)
    attention = (
        product("hbqk,bkhd->bqhd", fine_round, windows[1])
        + product("hbqk,khd->bqhd", coarse_round, coarse_all[1])
    ).astype(jnp.bfloat16)
    grad_blocks = grad_rows.reshape(blocks, FB, head_count, DH)
    row_delta = product("bqhd,bqhd->hbq", grad_blocks, attention)
    fine_ds = (
        fine_prob * (product("bqhd,bkhd->hbqk", grad_blocks, windows[1]) - row_delta[..., None])
    ).astype(jnp.bfloat16)
    coarse_ds = (
        coarse_prob * (product("bqhd,khd->hbqk", grad_blocks, coarse_all[1]) - row_delta[..., None])
    ).astype(jnp.bfloat16)
    query_grad = (
        (
            product("hbqk,bkhd->bqhd", fine_ds, windows[0])
            + product("hbqk,khd->bqhd", coarse_ds, coarse_all[0])
        )
        * scaling
    ).astype(jnp.bfloat16)
    window_grad = jnp.stack(
        [
            product("hbqk,bqhd->bkhd", fine_ds, query_blocks) * scaling,
            product("hbqk,bqhd->bkhd", fine_round, grad_blocks),
        ]
    )
    coarse_grad = jnp.stack(
        [
            product("hbqk,bqhd->khd", coarse_ds, query_blocks) * scaling,
            product("hbqk,bqhd->khd", coarse_round, grad_blocks),
        ]
    )
    coarse_grad = coarse_grad.reshape(2, 3 * pooled_rows + coarse_count, features)
    extended_grad = fold_windows(window_grad.reshape(2, blocks, 3 * FB, features), blocks)
    return (
        attention.reshape(tokens_here, features),
        query_grad.reshape(tokens_here, features),
        extended_grad,
        coarse_grad[:, : 3 * pooled_rows],
        coarse_grad[:, 3 * pooled_rows :],
    )


def shards(queries, token_keys, token_values, out_weight, out_grad):
    position = lax.axis_index("seq")
    seq_count = lax.axis_size("seq")
    tokens_here, features = queries.shape
    grad_scale = 1.0 / math.sqrt(tokens_here * seq_count)
    pooled_rows = tokens_here // P1
    reach = FB + pooled_rows
    stacked = jnp.stack([token_keys, token_values])
    near_rows = pooled(stacked, P1)
    far_rows = pooled(stacked, P2)
    extended = with_halo(stacked, (("seq", 1),), FB)
    extended_pooled = with_halo(near_rows, (("seq", 1),), pooled_rows)
    coarse_rows = gathered_copies(far_rows, "seq", 1)
    attn_grad = lax.dot_general(
        out_grad, out_weight, (((1,), (1,)), ((), ())), preferred_element_type=jnp.float32
    ).astype(jnp.bfloat16)
    attention, query_grad, extended_grad, near_grad, far_grad = attend(
        queries, extended, extended_pooled, coarse_rows, attn_grad, position, seq_count
    )
    head_part = jnp.dot(attention, out_weight, preferred_element_type=jnp.float32)
    layer_out = lax.psum_scatter(head_part, "tp", scatter_dimension=1, tiled=True).astype(
        jnp.bfloat16
    )
    outgoing = jnp.concatenate(
        [
            extended_grad[:, :FB],
            near_grad[:, :pooled_rows],
            near_grad[:, 2 * pooled_rows :],
            extended_grad[:, tokens_here + FB :],
        ],
        axis=1,
    )
    received = with_halo(outgoing, (("seq", 1),), FB + pooled_rows)
    left_back = received[:, :reach]
    right_back = received[:, received.shape[1] - reach :]
    fine_total = (
        extended_grad[:, FB : FB + tokens_here]
        + jnp.pad(left_back[:, pooled_rows:], ((0, 0), (0, tokens_here - FB), (0, 0)))
        + jnp.pad(right_back[:, :FB], ((0, 0), (tokens_here - FB, 0), (0, 0)))
    )
    near_total = (
        near_grad[:, pooled_rows : 2 * pooled_rows]
        + left_back[:, :pooled_rows]
        + right_back[:, FB:]
    )
    far_total = summed_on_arrival(far_grad, "seq", 1)
    columns = lax.all_to_all(out_grad, "seq", split_axis=1, concat_axis=0, tiled=True)
    weight_sum = lax.dot_general(
        lax.all_gather(attention, "seq", axis=0, tiled=True),
        columns,
        (((0,), (0,)), ((), ())),
        preferred_element_type=jnp.float32,
    )
    weight_grad = weight_sum * grad_scale
    grand = fine_total + expand_rows(near_total, P1) + expand_rows(far_total, P2)
    return (
        layer_out,
        query_grad,
        grand[0].astype(jnp.bfloat16),
        grand[1].astype(jnp.bfloat16),
        weight_grad,
    )


def solution(mesh):
    return jax.shard_map(
        shards,
        mesh=mesh,
        in_specs=(P("seq", "tp"), P("seq", "tp"), P("seq", "tp"), P("tp", None), P("seq", None)),
        out_specs=(P("seq", "tp"), P("seq", "tp"), P("seq", "tp"), P("seq", "tp"), P("tp", "seq")),
        check_vma=False,
    )
```

profile of v0, /device:TPU:0, one launch (start us, length us, event | category | flops | bytes accessed | tf_op | source)
XLA Modules:
  0.0 497.8 jit_solution(9888094884265164346)
XLA Ops:
  8.0 2.6 convert_reduce_fusion.1
  10.6 5.9 %collective-permute-start.2 = (bf16[2,32,1024]{2,1,0:T(8,128)(2,1)S(1)}, bf16[2,32,1024]{2,1,0:T(8,128)(2,1)S(1)}, u32[]{:S(2)}, u32[]{:S(2)}) collective-permute-start(bf16[2,32,1024]{2,1,0:T(8,128)(2,1)S(1)} %multiply_convert_fusion.2), channel_id=1, source_target_pairs={{0,4},{4,8},{8,12},{12,16},{16,20},{20,24},{24,28},{28,32},{32,36}... | collective-permute-start | bytes 393224 | tf_op jit(solution)/shard_map/ppermute | solution.py:22
  18.9 6.8 %collective-permute-start = (bf16[2,128,1024]{2,1,0:T(8,128)(2,1)}, bf16[2,128,1024]{2,1,0:T(8,128)(2,1)}, u32[]{:S(2)}, u32[]{:S(2)}) collective-permute-start(bf16[2,128,1024]{2,1,0:T(8,128)(2,1)} %get-tuple-element.19), channel_id=1, source_target_pairs={{0,4},{4,8},{8,12},{12,16},{16,20},{20,24},{24,28},{28,32},{32,36}... | collective-permute-start | bytes 1572872 | tf_op jit(solution)/shard_map/ppermute | solution.py:22
  28.3 10.5 %all-to-all-start = ((bf16[32,2,2,1024]{3,1,2,0:T(2,128)(2,1)}), bf16[32,2,2,1024]{3,1,2,0:T(2,128)(2,1)S(1)}, u32[]{:S(2)}, u32[]{:S(2)}) async-start(bf16[32,2,2,1024]{3,1,2,0:T(2,128)(2,1)} %broadcast_in_dim.36), calls=%async_computation | async-start | bytes 524288 | tf_op jit(solution)/shard_map/all_to_all | solution.py:39
  38.9 9.2 %fusion.27 = bf16[64,8,8,128]{3,1,2,0:T(8,128)(2,1)S(1)} fusion(bf16[512,4096]{1,0:T(8,128)(2,1)} %param.9, bf16[1024,4096]{1,0:T(8,128)(2,1)} %param.8), kind=kOutput, calls=%fused_computation.50 | convolution fusion | flops 4295491584 | bytes 13631488 | tf_op jit(solution)/shard_map/dot_general | solution.py:209
  54.3 2.7 slice_reduce_fusion
  72.2 2.8 fusion.10
  76.9 2.6 copy.154
  79.4 11.5 %fusion.54 = f32[512,4096]{1,0:T(8,128)} fusion(bf16[1024,4096]{1,0:T(8,128)(2,1)} %param.8, bf16[64,8,8,128]{3,2,1,0:T(8,128)(2,1)} %bitcast.195), kind=kOutput, calls=%fused_computation.123 | convolution fusion | flops 4294967296 | bytes 17825792 | tf_op jit(solution)/shard_map/dot_general | solution.py:215
  91.0 2.5 copy.285
  93.5 6.5 %copy.177 = bf16[512,4096]{0,1:T(8,128)(2,1)} copy(bf16[512,4096]{1,0:T(8,128)(2,1)} %param.9) | data formatting | bytes 8388608 | tf_op args[4]
  115.9 10.2 %all-to-all-start.1 = ((f32[32,2,2,1024]{3,2,1,0:T(2,128)}), f32[32,2,2,1024]{3,2,1,0:T(2,128)S(1)}, u32[]{:S(2)}, u32[]{:S(2)}) async-start(f32[32,2,2,1024]{3,2,1,0:T(2,128)} %bitcast.200), calls=%async_computation.2 | async-start | bytes 1048576 | tf_op jit(solution)/shard_map/all_to_all | solution.py:53
  126.1 8.1 %multiply_convert_fusion = bf16[8,4,128,384]{2,3,1,0:T(8,128)(2,1)} fusion(f32[8,4,384,128]{3,2,1,0:T(8,128)} %copy-done.2, f32[8,4,128]{2,1,0:T(4,128)S(1)} %copy.189, f32[8,4,128]{2,1,0:T(4,128)S(1)} %bitcast.209, pred[4,384]{1,0:T(4,128)(4,1)S(1)} %fusion.51, bf16[4,128,8,128]{3,2,1,0:T(8,128)(2,1)S(1)} %bitcast.173, ...), kind=kOutput, calls=%fused_computation.8 | convolution fusion | flops 412090368 | bytes 13665792 | tf_op jit(solution)/shard_map/bqhd,bkhd->hbqk/dot_general | solution.py:58
  134.2 7.4 %fusion.18 = f32[4,384,8,128]{1,3,2,0:T(8,128)} fusion(bf16[4,128,8,128]{3,2,1,0:T(8,128)(2,1)S(1)} %bitcast.174, f32[8,4,384,128]{3,2,1,0:T(8,128)} %copy-done.2, f32[8,4,128]{2,1,0:T(4,128)S(1)} %bitcast.210, pred[4,384]{1,0:T(4,128)(4,1)S(1)} %fusion.51), kind=kOutput, calls=%fused_computation.34 | convolution fusion | flops 408944640 | bytes 13649408 | tf_op jit(solution)/shard_map/hbqk,bqhd->bkhd/dot_general | solution.py:58
  141.6 7.1 %copy.169 = f32[4,384,8,128]{3,2,1,0:T(8,128)} copy(f32[4,384,8,128]{1,3,2,0:T(8,128)} %fusion.18) | data formatting | bytes 12582912 | tf_op jit(solution)/shard_map/hbqk,bqhd->bkhd/transpose | solution.py:58
  148.7 7.4 %stack.49 = f32[1,4,3,128,1024]{4,3,2,1,0:T(8,128)} reshape(f32[4,384,8,128]{3,2,1,0:T(8,128)} %copy.169) | data formatting | bytes 12582912 | tf_op jit(solution)/shard_map/stack | solution.py:173
  156.1 2.9 multiply_bitcast_fusion
  159.1 6.3 %copy.166 = f32[4,384,8,128]{3,2,1,0:T(8,128)} copy(f32[4,384,8,128]{3,1,2,0:T(8,128)S(1)} %multiply_bitcast_fusion) | data formatting | bytes 12582912 | tf_op jit(solution)/shard_map/mul | solution.py:175
  165.3 7.1 %stack.48 = f32[1,4,3,128,1024]{4,3,2,1,0:T(8,128)} reshape(f32[4,384,8,128]{3,2,1,0:T(8,128)} %copy.166) | data formatting | bytes 12582912 | tf_op jit(solution)/shard_map/stack | solution.py:173
  172.4 10.2 %all-to-all-start.2 = ((bf16[512,32,128]{0,2,1:T(8,128)(2,1)}), bf16[512,32,128]{0,2,1:T(8,128)(2,1)}, u32[]{:S(2)}, u32[]{:S(2)}) async-start(bf16[512,32,128]{0,2,1:T(8,128)(2,1)} %bitcast.179), calls=%async_computation.3 | async-start | bytes 8388608 | tf_op jit(solution)/shard_map/all_to_all | solution.py:242
  183.4 7.0 %constant_dynamic-update-slice_fusion.1 = f32[2,4,3,128,1024]{4,3,2,1,0:T(8,128)} fusion(f32[1,4,3,128,1024]{4,3,2,1,0:T(8,128)} %stack.48), kind=kLoop, calls=%fused_computation.91 | loop fusion | bytes 12582912
  190.4 3.1 constant_dynamic-update-slice_fusion
  193.5 10.1 %slice_bitcast_fusion.2 = (f32[2,4,128,1024]{3,2,1,0:T(8,128)S(1)}, f32[2,4,128,1024]{3,2,1,0:T(8,128)}, f32[2,4,128,1024]{3,2,1,0:T(8,128)}) fusion(f32[2,4,3,128,1024]{4,3,2,1,0:T(8,128)} %constant_dynamic-update-slice_fusion), kind=kLoop, calls=%fused_computation.18 | loop fusion | bytes 25165824 | tf_op jit(solution)/shard_map/squeeze | solution.py:84
  203.7 5.2 %pad_add_fusion = f32[2,6,128,1024]{3,2,1,0:T(8,128)S(1)} fusion(f32[2,4,128,1024]{3,2,1,0:T(8,128)} %get-tuple-element.8, f32[2,4,128,1024]{3,2,1,0:T(8,128)} %get-tuple-element.9, f32[2,4,128,1024]{3,2,1,0:T(8,128)S(1)} %get-tuple-element.7), kind=kLoop, calls=%fused_computation.6 | loop fusion | flops 3145728 | bytes 18874368 | tf_op jit(solution)/shard_map/add | solution.py:87
  212.7 6.7 %collective-permute-start.4 = (f32[2,160,1024]{2,1,0:T(8,128)}, f32[2,160,1024]{2,1,0:T(8,128)}, u32[]{:S(2)}, u32[]{:S(2)}) collective-permute-start(f32[2,160,1024]{2,1,0:T(8,128)} %pad_maximum_fusion.1), channel_id=1, source_target_pairs={{0,4},{4,8},{8,12},{12,16},{16,20},{20,24},{24,28},{28,32},{32,36}... | collective-permute-start | bytes 3932168 | tf_op jit(solution)/shard_map/ppermute | solution.py:22
  226.1 91.8 %collective-permute-done.4 = f32[2,160,1024]{2,1,0:T(8,128)} collective-permute-done((f32[2,160,1024]{2,1,0:T(8,128)}, f32[2,160,1024]{2,1,0:T(8,128)}, u32[]{:S(2)}, u32[]{:S(2)}) %collective-permute-start.4) | collective-permute-done | bytes 1310752 | tf_op jit(solution)/shard_map/ppermute | solution.py:22
  321.7 3.3 fusion.7
  326.6 6.5 %copy.178 = bf16[32,512,128]{2,1,0:T(8,128)(2,1)} copy(bf16[32,512,128]{1,2,0:T(8,128)(2,1)} %bitcast.40) | data formatting | bytes 8388608 | tf_op jit(solution)/shard_map/all_to_all | solution.py:242
  333.0 103.6 %reduce-scatter.2.cloned.1.call-done = f32[512,1024]{1,0:T(8,128)} async-done(((f32[512,4096]{1,0:T(8,128)}), f32[512,1024]{1,0:T(8,128)}) %reduce-scatter.2.cloned.1.call-update) | async-done | bytes 2097168 | tf_op jit(solution)/shard_map/reduce_scatter | solution.py:216
  436.6 2.7 convert_element_type.63
  439.4 33.9 %all-gather.2.cloned.1.call-done = bf16[16384,1024]{1,0:T(8,128)(2,1)} async-done(((bf16[512,1024]{1,0:T(8,128)(2,1)}), bf16[16384,1024]{1,0:T(8,128)(2,1)}) %all-gather.2.cloned.1.call-update) | async-done | bytes 33554448 | tf_op jit(solution)/shard_map/all_gather | solution.py:244
  473.2 17.0 %convolution_multiply_fusion = f32[1024,128]{1,0:T(8,128)} fusion(bf16[16384,1024]{1,0:T(8,128)(2,1)} %all-gather.2.cloned.1.call-done, bf16[16384,128]{1,0:T(8,128)(2,1)} %bitcast.193), kind=kOutput, calls=%fused_computation.59 | convolution fusion | flops 4295098368 | bytes 38273024 | tf_op jit(solution)/shard_map/dot_general | solution.py:243
  (127 shorter events, 60.4 us)
Async XLA Ops:
  8.0 9.8 %copy-start.6 = (bf16[512,1024]{1,0:T(8,128)(2,1)S(1)}, bf16[512,1024]{1,0:T(8,128)(2,1)}, u32[]{:S(2)}) copy-start(bf16[512,1024]{1,0:T(8,128)(2,1)} %param.6) | copy-start | bytes 3145732
  8.0 9.8 %copy-start.4 = (bf16[512,1024]{1,0:T(8,128)(2,1)S(1)}, bf16[512,1024]{1,0:T(8,128)(2,1)}, u32[]{:S(2)}) copy-start(bf16[512,1024]{1,0:T(8,128)(2,1)} %param.7) | copy-start | bytes 3145732
  10.6 42.4 %collective-permute-start.2 = (bf16[2,32,1024]{2,1,0:T(8,128)(2,1)S(1)}, bf16[2,32,1024]{2,1,0:T(8,128)(2,1)S(1)}, u32[]{:S(2)}, u32[]{:S(2)}) collective-permute-start(bf16[2,32,1024]{2,1,0:T(8,128)(2,1)S(1)} %multiply_convert_fusion.2), channel_id=1, source_target_pairs={{0,4},{4,8},{8,12},{12,16},{16,20},{20,24},{24,28},{28,32},{32,36}... | collective-permute-start | bytes 393224 | tf_op jit(solution)/shard_map/ppermute | solution.py:22
  16.5 36.7 %collective-permute-start.3 = (bf16[2,32,1024]{2,1,0:T(8,128)(2,1)S(1)}, bf16[2,32,1024]{2,1,0:T(8,128)(2,1)S(1)}, u32[]{:S(2)}, u32[]{:S(2)}) collective-permute-start(bf16[2,32,1024]{2,1,0:T(8,128)(2,1)S(1)} %multiply_convert_fusion.2), channel_id=1, source_target_pairs={{4,0},{8,4},{12,8},{16,12},{20,16},{24,20},{28,24},{32,28},{36,32}... | collective-permute-start | bytes 393224 | tf_op jit(solution)/shard_map/ppermute | solution.py:24
  18.9 40.4 %collective-permute-start = (bf16[2,128,1024]{2,1,0:T(8,128)(2,1)}, bf16[2,128,1024]{2,1,0:T(8,128)(2,1)}, u32[]{:S(2)}, u32[]{:S(2)}) collective-permute-start(bf16[2,128,1024]{2,1,0:T(8,128)(2,1)} %get-tuple-element.19), channel_id=1, source_target_pairs={{0,4},{4,8},{8,12},{12,16},{16,20},{20,24},{24,28},{28,32},{32,36}... | collective-permute-start | bytes 1572872 | tf_op jit(solution)/shard_map/ppermute | solution.py:22
  25.7 33.6 %collective-permute-start.1 = (bf16[2,128,1024]{2,1,0:T(8,128)(2,1)}, bf16[2,128,1024]{2,1,0:T(8,128)(2,1)}, u32[]{:S(2)}, u32[]{:S(2)}) collective-permute-start(bf16[2,128,1024]{2,1,0:T(8,128)(2,1)} %get-tuple-element.20), channel_id=1, source_target_pairs={{4,0},{8,4},{12,8},{16,12},{20,16},{24,20},{28,24},{32,28},{36,32}... | collective-permute-start | bytes 1572872 | tf_op jit(solution)/shard_map/ppermute | solution.py:24
  28.3 25.1 %all-to-all-start = ((bf16[32,2,2,1024]{3,1,2,0:T(2,128)(2,1)}), bf16[32,2,2,1024]{3,1,2,0:T(2,128)(2,1)S(1)}, u32[]{:S(2)}, u32[]{:S(2)}) async-start(bf16[32,2,2,1024]{3,1,2,0:T(2,128)(2,1)} %broadcast_in_dim.36), calls=%async_computation | async-start | bytes 524288 | tf_op jit(solution)/shard_map/all_to_all | solution.py:39
  38.8 397.9 %reduce-scatter.2.cloned.1.call-start = ((), (), s32[]{:S(2)}) async-start(), calls=%async_computation.4 | async-start | bytes 10485760 | tf_op jit(solution)/shard_map/reduce_scatter | solution.py:216
  48.1 1.6 copy-start.18
  52.9 4.2 copy-start.20
  57.1 2.2 copy-start.5
  57.1 2.2 copy-start.7
  64.8 3.5 copy-start.8
  64.8 3.5 copy-start.12
  69.6 2.6 copy-start.2
  72.2 2.8 copy-start.9
  91.0 382.2 %all-gather.2.cloned.1.call-start = ((), (), s32[]{:S(2)}) async-start(), calls=%async_computation.5 | async-start | bytes 34603008 | tf_op jit(solution)/shard_map/all_gather | solution.py:244
  100.0 3.2 copy-start.13
  110.4 15.7 %copy-start.1 = (bf16[64,8,8,128]{3,2,1,0:T(8,128)(2,1)S(1)}, bf16[64,8,8,128]{3,2,1,0:T(8,128)(2,1)}, u32[]{:S(2)}) copy-start(bf16[64,8,8,128]{3,2,1,0:T(8,128)(2,1)} %copy-done) | copy-start | bytes 3145732
  112.8 69.8 %copy-start.17 = (f32[2,160,1024]{2,1,0:T(8,128)}, f32[2,160,1024]{2,1,0:T(8,128)S(1)}, u32[]{:S(2)}) copy-start(f32[2,160,1024]{2,1,0:T(8,128)S(1)} %constant_dynamic-update-slice_fusion.2) | copy-start | bytes 3932164
  115.9 56.5 %all-to-all-start.1 = ((f32[32,2,2,1024]{3,2,1,0:T(2,128)}), f32[32,2,2,1024]{3,2,1,0:T(2,128)S(1)}, u32[]{:S(2)}, u32[]{:S(2)}) async-start(f32[32,2,2,1024]{3,2,1,0:T(2,128)} %bitcast.200), calls=%async_computation.2 | async-start | bytes 1048576 | tf_op jit(solution)/shard_map/all_to_all | solution.py:53
  148.7 7.4 %copy-start.14 = (bf16[64,8,8,128]{3,2,1,0:T(8,128)(2,1)S(1)}, bf16[64,8,8,128]{3,2,1,0:T(8,128)(2,1)}, u32[]{:S(2)}) copy-start(bf16[64,8,8,128]{3,2,1,0:T(8,128)(2,1)} %copy.213) | copy-start | bytes 3145732
  172.4 154.2 %all-to-all-start.2 = ((bf16[512,32,128]{0,2,1:T(8,128)(2,1)}), bf16[512,32,128]{0,2,1:T(8,128)(2,1)}, u32[]{:S(2)}, u32[]{:S(2)}) async-start(bf16[512,32,128]{0,2,1:T(8,128)(2,1)} %bitcast.179), calls=%async_computation.3 | async-start | bytes 8388608 | tf_op jit(solution)/shard_map/all_to_all | solution.py:242
  182.6 7.8 %slice-start = ((s8[6291456]{0:T(1024)(128)(4,1)}), s8[4194304]{0:T(1024)(128)(4,1)S(1)}, s32[]{:S(2)}) async-start(s8[6291456]{0:T(1024)(128)(4,1)} %bitcast.175), calls=%async_computation.6 | async-start | bytes 8388608
  183.4 7.0 %slice-start.1 = ((s8[6291456]{0:T(1024)(128)(4,1)}), s8[2097152]{0:T(1024)(128)(4,1)S(1)}, s32[]{:S(2)}) async-start(s8[6291456]{0:T(1024)(128)(4,1)} %bitcast.175), calls=%async_computation.7 | async-start | bytes 4194304
  208.9 3.8 copy-start.3
  208.9 1.1 copy-start.19
  208.9 12.9 %copy-start.16 = (bf16[8,4,128,384]{2,3,1,0:T(8,128)(2,1)S(1)}, bf16[8,4,128,384]{2,3,1,0:T(8,128)(2,1)}, u32[]{:S(2)}) copy-start(bf16[8,4,128,384]{2,3,1,0:T(8,128)(2,1)} %multiply_convert_fusion) | copy-start | bytes 9437188
  209.0 12.8 %copy-start.15 = (bf16[4,384,8,128]{3,1,0,2:T(8,128)(2,1)S(1)}, bf16[4,384,8,128]{3,1,0,2:T(8,128)(2,1)}, u32[]{:S(2)}) copy-start(bf16[4,384,8,128]{3,1,0,2:T(8,128)(2,1)} %get-tuple-element.12) | copy-start | bytes 9437188
  212.7 105.2 %collective-permute-start.4 = (f32[2,160,1024]{2,1,0:T(8,128)}, f32[2,160,1024]{2,1,0:T(8,128)}, u32[]{:S(2)}, u32[]{:S(2)}) collective-permute-start(f32[2,160,1024]{2,1,0:T(8,128)} %pad_maximum_fusion.1), channel_id=1, source_target_pairs={{0,4},{4,8},{8,12},{12,16},{16,20},{20,24},{24,28},{28,32},{32,36}... | collective-permute-start | bytes 3932168 | tf_op jit(solution)/shard_map/ppermute | solution.py:22
  220.5 98.7 %collective-permute-start.5 = (f32[2,160,1024]{2,1,0:T(8,128)}, f32[2,160,1024]{2,1,0:T(8,128)}, u32[]{:S(2)}, u32[]{:S(2)}) collective-permute-start(f32[2,160,1024]{2,1,0:T(8,128)} %pad_maximum_fusion.2), channel_id=1, source_target_pairs={{4,0},{8,4},{12,8},{16,12},{20,16},{24,20},{28,24},{32,28},{36,32}... | collective-permute-start | bytes 3932168 | tf_op jit(solution)/shard_map/ppermute | solution.py:24
  221.8 1.3 copy-start.11
  (2 other events, 2.0 us)
Sparse Core Ops, SparseCore 0:
  91.1 345.4 reduce-scatter.1
Sparse Core Ops, SparseCore 1:
  94.5 378.7 all-gather.1
where the time goes:
time: 505 us; the launch traced here: 498 us
  waiting for transfers between devices  229 us (45%)
  local copies, waits for them, and re-layouts  104 us (21%)
  matrix products  70.5 us (14%)
  starting transfers between devices  54.2 us (11%)
  other arithmetic  23.6 us (5%)
  between operations  16.4 us (3%)
    reduce_scatter x1, waiting for transfers between devices, shards(): lax.psum_scatter(head_part, 'tp', scatter_dimension=1, tiled=True)  104 us
    ppermute x3, waiting for transfers between devices, with_halo(): lax.ppermute(tail, axis, [(i, (i + 1) % count) for i in range(ends)])  91.8 us
    all_gather x1, waiting for transfers between devices, shards(): lax.all_gather(attention, 'seq', axis=0, tiled=True)  33.9 us
    dot_general x12, matrix products, product(): return jnp.einsum(form, left, right, preferred_element_type=jnp.float32)  32.8 us
    unnamed x59, local copies, waits for them, and re-layouts  30.7 us
    ppermute x3, starting transfers between devices, with_halo(): lax.ppermute(tail, axis, [(i, (i + 1) % count) for i in range(ends)])  19.4 us
    another operation x3, local copies, waits for them, and re-layouts, attend(): jnp.stack([product('hbqk,bqhd->bkhd', fine_ds, query_blocks) * scaling, p...  17.6 us
    dot_general x1, matrix products, shards(): lax.dot_general(lax.all_gather(attention, 'seq', axis=0, tiled=True), col...  17 us
  transfers between devices with their start and end apart: 11, of which 3 were waited for; matrix products, arithmetic and copies ran while one was open for 29% of the time, Pallas kernels for 0%

commit v1 on v0

v1 whole, which is shorter than its diff:
```python
import functools
import math

import jax
import jax.numpy as jnp
from jax import lax
from jax.experimental import pallas as pl
from jax.experimental.pallas import tpu as pltpu
from jax.sharding import PartitionSpec as P

DH = 128
FB = 128
P1 = 16
P2 = 256
BF = jnp.bfloat16
F32 = jnp.float32
NEG = -1e30
LOG2E = math.log2(math.e)
MB = 1024 * 1024


def dot(a, b, ca, cb):
    return lax.dot_general(a, b, (((ca,), (cb,)), ((), ())), preferred_element_type=F32)


def params(limit):
    return pltpu.CompilerParams(vmem_limit_bytes=limit * MB)


def pool_kernel(k_ref, v_ref, near_ref, far_ref, left_ref, right_ref):
    rows = k_ref.shape[0]
    for i, ref in enumerate((k_ref, v_ref)):
        x = ref[...].astype(F32)
        s16 = x.reshape(rows // P1, P1, x.shape[1]).sum(axis=1)
        near = (s16 * (1.0 / P1)).astype(BF)
        far = s16.reshape(rows // P2, P2 // P1, x.shape[1]).sum(axis=1) * (1.0 / P2)
        near_ref[i] = near
        far_ref[i] = far.astype(BF)
        left_ref[i, :FB] = ref[:FB]
        right_ref[i, :FB] = ref[rows - FB :]
        left_ref[i, FB:] = near
        right_ref[i, FB:] = near


def pool(k, v):
    rows, feats = k.shape
    nr, fr = rows // P1, rows // P2
    cols = 256
    blk = lambda r: pl.BlockSpec((2, r, cols), lambda j: (0, 0, j))
    out = lambda r: jax.ShapeDtypeStruct((2, r, feats), BF)
    return pl.pallas_call(
        pool_kernel,
        grid=(feats // cols,),
        in_specs=[pl.BlockSpec((rows, cols), lambda j: (0, j))] * 2,
        out_specs=[blk(nr), blk(fr), blk(FB + nr), blk(FB + nr)],
        out_shape=[out(nr), out(fr), out(FB + nr), out(FB + nr)],
        compiler_params=params(24),
        name="pool",
    )(k, v)


def level_bias(position, blocks, pooled_rows, coarse_count, tokens_here, seq_count):
    group_ids = jnp.arange(3 * pooled_rows, dtype=jnp.int32)
    group_dev = group_ids // pooled_rows
    absent = ((group_dev == 0) & (position == 0)) | ((group_dev == 2) & (position == seq_count - 1))
    block_ids = jnp.arange(blocks, dtype=jnp.int32)[:, None]
    distance = group_ids[None, :] * P1 // FB - blocks - block_ids
    near = jnp.where(absent[None, :] | (jnp.abs(distance) <= 1), NEG, math.log(P1) * LOG2E)
    coarse_dev = jnp.arange(coarse_count, dtype=jnp.int32) * P2 // tokens_here
    far = jnp.where(jnp.abs(coarse_dev - position) > 1, math.log(P2) * LOG2E, NEG)
    far = jnp.broadcast_to(far[None, :], (blocks, coarse_count))
    bias = jnp.concatenate([near, far], axis=1).astype(F32)
    return jnp.broadcast_to(bias[:, :, None], (*bias.shape, FB))


def gathered(i, left_ref, own_ref, right_ref, near_ref, far_ref):
    keys = jnp.concatenate([left_ref[i, :FB], own_ref[...], right_ref[i, :FB]], axis=0)
    coarse = jnp.concatenate([left_ref[i, FB:], near_ref[i], right_ref[i, FB:], far_ref[i]], axis=0)
    return keys, coarse


def scores(b, blocks, pos_ref, seq_count, q, keys, coarse_scores, bias_ref):
    scale = LOG2E / math.sqrt(DH)
    qb = q[b * FB : (b + 1) * FB]
    fine = dot(keys[b * FB : (b + 3) * FB], qb, 1, 1) * scale
    if b == 0:
        edge = jnp.where(pos_ref[0] == 0, NEG, 0.0).astype(F32)
        fine = jnp.concatenate([fine[:FB] + edge, fine[FB:]], axis=0)
    if b == blocks - 1:
        edge = jnp.where(pos_ref[0] == seq_count - 1, NEG, 0.0).astype(F32)
        fine = jnp.concatenate([fine[: 2 * FB], fine[2 * FB :] + edge], axis=0)
    coarse = coarse_scores[:, b * FB : (b + 1) * FB] * scale + bias_ref[b]
    return fine, coarse


def fwd_kernel(seq_count, pos_ref, q_ref, k_ref, v_ref, left_ref, right_ref, near_ref, far_ref, bias_ref, att_ref, attt_ref, lse_ref):
    blocks = q_ref.shape[0] // FB
    q = q_ref[...]
    keys, ckeys = gathered(0, left_ref, k_ref, right_ref, near_ref, far_ref)
    vals, cvals = gathered(1, left_ref, v_ref, right_ref, near_ref, far_ref)
    vals_t, cvals_t = vals.T, cvals.T
    csc = dot(ckeys, q, 1, 1)
    for b in range(blocks):
        fine, coarse = scores(b, blocks, pos_ref, seq_count, q, keys, csc, bias_ref)
        peak = jnp.maximum(fine.max(axis=0, keepdims=True), coarse.max(axis=0, keepdims=True))
        pf = jnp.exp2(fine - peak)
        pc = jnp.exp2(coarse - peak)
        total = pf.sum(axis=0, keepdims=True) + pc.sum(axis=0, keepdims=True)
        lse_ref[0, :, b * FB : (b + 1) * FB] = peak + jnp.log2(total)
        out_t = dot(vals_t[:, b * FB : (b + 3) * FB], pf.astype(BF), 1, 0) + dot(cvals_t, pc.astype(BF), 1, 0)
        out_t = (out_t * (1.0 / total)).astype(BF)
        attt_ref[:, b * FB : (b + 1) * FB] = out_t
        att_ref[b * FB : (b + 1) * FB, :] = out_t.T


def bwd_kernel(
    seq_count, pos_ref, q_ref, k_ref, v_ref, left_ref, right_ref, near_ref, far_ref, bias_ref, do_ref, att_ref, lse_ref,
    dq_ref, gk_ref, gv_ref, sl_ref, sr_ref, gfar_ref, p_ref, ds_ref, cp_ref, cds_ref,
):
    blocks = q_ref.shape[0] // FB
    own = blocks * FB
    inv = 1.0 / math.sqrt(DH)
    q, do = q_ref[...], do_ref[...]
    keys, ckeys = gathered(0, left_ref, k_ref, right_ref, near_ref, far_ref)
    vals, cvals = gathered(1, left_ref, v_ref, right_ref, near_ref, far_ref)
    keys_t, ckeys_t = keys.T, ckeys.T
    csc = dot(ckeys, q, 1, 1)
    cdp = dot(cvals, do, 1, 1)
    delta_all = (do.astype(F32) * att_ref[...].astype(F32)).T.sum(axis=0, keepdims=True)
    for b in range(blocks):
        cols = slice(b * FB, (b + 1) * FB)
        fine, coarse = scores(b, blocks, pos_ref, seq_count, q, keys, csc, bias_ref)
        lse = lse_ref[0, :, cols]
        delta = delta_all[:, cols]
        pf = jnp.exp2(fine - lse)
        pc = jnp.exp2(coarse - lse)
        dpf = dot(vals[b * FB : (b + 3) * FB], do[cols], 1, 1)
        dsf = (pf * (dpf - delta)).astype(BF)
        dsc = (pc * (cdp[:, cols] - delta)).astype(BF)
        p_ref[b * FB : (b + 3) * FB, cols] = pf.astype(BF)
        ds_ref[b * FB : (b + 3) * FB, cols] = dsf
        cp_ref[:, cols] = pc.astype(BF)
        cds_ref[:, cols] = dsc
        dq_t = dot(keys_t[:, b * FB : (b + 3) * FB], dsf, 1, 0) + dot(ckeys_t, dsc, 1, 0)
        dq_ref[cols, :] = (dq_t * inv).astype(BF).T
    nr = near_ref.shape[1]
    for i, (src, csrc, rhs, mul, g_ref) in enumerate(((ds_ref, cds_ref, q, inv, gk_ref), (p_ref, cp_ref, do, 1.0, gv_ref))):
        cg = dot(csrc[...], rhs, 1, 0) * mul
        sl_ref[i, FB:] = cg[:nr].astype(BF)
        sr_ref[i, FB:] = cg[2 * nr : 3 * nr].astype(BF)
        gfar_ref[i] = cg[3 * nr :]
        mine = cg[nr : 2 * nr] * (1.0 / P1)
        for c in range(blocks + 2):
            lo, hi = max(0, c - 2), min(blocks, c + 1)
            part = dot(src[c * FB : (c + 1) * FB, lo * FB : hi * FB], rhs[lo * FB : hi * FB], 1, 0) * mul
            if c == 0:
                sl_ref[i, :FB] = part.astype(BF)
            elif c == blocks + 1:
                sr_ref[i, :FB] = part.astype(BF)
            else:
                r = c - 1
                per = FB // P1
                spread = jnp.broadcast_to(mine[r * per : (r + 1) * per, None, :], (per, P1, DH)).reshape(FB, DH)
                g_ref[r * FB : (r + 1) * FB, :] = part + spread


def attention_specs(tokens, halo, nr, fr, blocks):
    tok = pl.BlockSpec((tokens, DH), lambda h, *_: (0, h))
    lev = lambda r: pl.BlockSpec((2, r, DH), lambda h, *_: (0, 0, h))
    bias = pl.BlockSpec((blocks, 3 * nr + fr, FB), lambda h, *_: (0, 0, 0))
    return tok, [tok, tok, tok, lev(halo), lev(halo), lev(nr), lev(fr), bias], lev


def forward(seq_count, pos, q, k, v, left, right, near, far, bias):
    tokens, feats = q.shape
    heads = feats // DH
    tok, specs, _ = attention_specs(tokens, left.shape[1], near.shape[1], far.shape[1], tokens // FB)
    return pl.pallas_call(
        functools.partial(fwd_kernel, seq_count),
        grid_spec=pltpu.PrefetchScalarGridSpec(
            num_scalar_prefetch=1,
            grid=(heads,),
            in_specs=specs,
            out_specs=[tok, pl.BlockSpec((DH, tokens), lambda h, *_: (h, 0)), pl.BlockSpec((1, 1, tokens), lambda h, *_: (h, 0, 0))],
        ),
        out_shape=[
            jax.ShapeDtypeStruct((tokens, feats), BF),
            jax.ShapeDtypeStruct((feats, tokens), BF),
            jax.ShapeDtypeStruct((heads, 1, tokens), F32),
        ],
        compiler_params=params(32),
        name="attend",
    )(pos, q, k, v, left, right, near, far, bias)


def backward(seq_count, pos, q, k, v, left, right, near, far, bias, do, att, lse):
    tokens, feats = q.shape
    heads = feats // DH
    halo, nr, fr = left.shape[1], near.shape[1], far.shape[1]
    tok, specs, lev = attention_specs(tokens, halo, nr, fr, tokens // FB)
    coarse = 3 * nr + fr
    return pl.pallas_call(
        functools.partial(bwd_kernel, seq_count),
        grid_spec=pltpu.PrefetchScalarGridSpec(
            num_scalar_prefetch=1,
            grid=(heads,),
            in_specs=[*specs, tok, tok, pl.BlockSpec((1, 1, tokens), lambda h, *_: (h, 0, 0))],
            out_specs=[tok, tok, tok, lev(halo), lev(halo), lev(fr)],
            scratch_shapes=[
                pltpu.VMEM((tokens + 2 * FB, tokens), BF),
                pltpu.VMEM((tokens + 2 * FB, tokens), BF),
                pltpu.VMEM((coarse, tokens), BF),
                pltpu.VMEM((coarse, tokens), BF),
            ],
        ),
        out_shape=[
            jax.ShapeDtypeStruct((tokens, feats), BF),
            jax.ShapeDtypeStruct((tokens, feats), F32),
            jax.ShapeDtypeStruct((tokens, feats), F32),
            jax.ShapeDtypeStruct((2, halo, feats), BF),
            jax.ShapeDtypeStruct((2, halo, feats), BF),
            jax.ShapeDtypeStruct((2, fr, feats), F32),
        ],
        compiler_params=params(40),
        name="attend_grad",
    )(pos, q, k, v, left, right, near, far, bias, do, att, lse)


def combine_kernel(gk_ref, gv_ref, left_ref, right_ref, far_ref, ok_ref, ov_ref):
    rows, width = gk_ref.shape
    for i, (g_ref, o_ref) in enumerate(((gk_ref, ok_ref), (gv_ref, ov_ref))):
        near = (left_ref[i, FB:].astype(F32) + right_ref[i, FB:].astype(F32)) * (1.0 / P1)
        per = FB // P1
        for r in range(rows // FB):
            part = g_ref[r * FB : (r + 1) * FB]
            part += jnp.broadcast_to(near[r * per : (r + 1) * per, None, :], (per, P1, width)).reshape(FB, width)
            g = r * FB // P2
            part += far_ref[i, g : g + 1] * (1.0 / P2)
            if r == 0:
                part += left_ref[i, :FB].astype(F32)
            if r == rows // FB - 1:
                part += right_ref[i, :FB].astype(F32)
            o_ref[r * FB : (r + 1) * FB] = part.astype(BF)


def combine(gk, gv, from_left, from_right, far):
    rows, feats = gk.shape
    cols = 256
    tok = pl.BlockSpec((rows, cols), lambda j: (0, j))
    lev = lambda r: pl.BlockSpec((2, r, cols), lambda j: (0, 0, j))
    halo = from_left.shape[1]
    return pl.pallas_call(
        combine_kernel,
        grid=(feats // cols,),
        in_specs=[tok, tok, lev(halo), lev(halo), lev(far.shape[1])],
        out_specs=[tok, tok],
        out_shape=[jax.ShapeDtypeStruct((rows, feats), BF)] * 2,
        compiler_params=params(32),
        name="combine",
    )(gk, gv, from_left, from_right, far)


UNITS = 4
ROUTE = ((0, 1, 3), (0, 3, 1), (1, 1, 3), (1, 3, 1))


def weight_kernel(cols_ref, attt_ref, og_ref, *out_refs):
    j = pl.program_id(0)
    width = out_refs[0].shape[-1]
    rows = attt_ref.shape[0] // UNITS
    for u, o_ref in enumerate(out_refs):
        at = pl.multiple_of(cols_ref[u, j] * (2 * width), 2 * width)
        res = dot(attt_ref[u * rows : (u + 1) * rows, :], og_ref[:, pl.ds(at, 2 * width)], 1, 0).astype(BF)
        o_ref[0, 0] = res[:, :width]
        o_ref[0, 1] = res[:, width:]


def weight_parts(cols, attt, og, width):
    feats, tokens = attt.shape
    steps = cols.shape[1]
    rows = feats // UNITS
    whole = lambda a: pl.BlockSpec(a.shape, lambda j, *_: (0, 0))
    return pl.pallas_call(
        weight_kernel,
        grid_spec=pltpu.PrefetchScalarGridSpec(
            num_scalar_prefetch=1,
            grid=(steps,),
            in_specs=[whole(attt), whole(og)],
            out_specs=[pl.BlockSpec((1, 2, rows, width), lambda j, *_: (j, 0, 0, 0))] * UNITS,
        ),
        out_shape=[jax.ShapeDtypeStruct((steps, 2, rows, width), BF)] * UNITS,
        compiler_params=params(40),
        name="weight_parts",
    )(cols, attt, og)


def layer_kernel(cols_ref, att_ref, w_ref, o_ref):
    o_ref[0] = dot(att_ref[...], w_ref[...], 1, 0).astype(BF)


def layer_parts(cols, att, w, width):
    tokens, feats = att.shape
    steps = cols.shape[0]
    sub = 2
    n = width // sub
    return pl.pallas_call(
        layer_kernel,
        grid_spec=pltpu.PrefetchScalarGridSpec(
            num_scalar_prefetch=1,
            grid=(steps, sub),
            in_specs=[
                pl.BlockSpec((tokens, feats), lambda j, s, *_: (0, 0)),
                pl.BlockSpec((feats, n), lambda j, s, c: (0, c[j] * sub + s)),
            ],
            out_specs=pl.BlockSpec((1, tokens, n), lambda j, s, *_: (j, 0, s)),
        ),
        out_shape=jax.ShapeDtypeStruct((steps, tokens, width), BF),
        compiler_params=params(40),
        name="layer_parts",
    )(cols, att, w)


def swap(x, axis, bits):
    n = lax.axis_size(axis)
    return lax.ppermute(x, axis, [(i, i ^ bits) for i in range(n)])


def add(a, b):
    return (a.astype(F32) + b.astype(F32)).astype(BF)


def shards(queries, token_keys, token_values, out_weight, out_grad):
    pos = lax.axis_index("seq").astype(jnp.int32)
    tp = lax.axis_index("tp").astype(jnp.int32)
    seq_count, tp_count = lax.axis_size("seq"), lax.axis_size("tp")
    tokens, feats = queries.shape
    width = out_weight.shape[1]
    pos1 = pos[None]
    right_perm = [(i, i + 1) for i in range(seq_count - 1)]
    left_perm = [(i + 1, i) for i in range(seq_count - 1)]

    near, far_own, to_left, to_right = pool(token_keys, token_values)
    from_left = lax.ppermute(to_right, "seq", right_perm)
    from_right = lax.ppermute(to_left, "seq", left_perm)
    far = lax.all_gather(far_own, "seq", axis=1, tiled=True)
    attn_grad = dot(out_grad, out_weight, 1, 1).astype(BF)
    bias = level_bias(pos, tokens // FB, near.shape[1], far.shape[1], tokens, seq_count)
    args = (seq_count, pos1, queries, token_keys, token_values, from_left, from_right, near, far, bias)
    att, attt, lse = forward(*args)

    part = width // seq_count
    shift = (3, 1)
    coord = ((pos >> 3) & 3, (pos >> 1) & 3)
    rows = []
    for axis, k1, k2 in ROUTE:
        rel = jnp.array([0, k2, k1, k1 ^ k2], jnp.int32)
        first = coord[axis] ^ rel
        second = coord[1 - axis] ^ rel
        xs, ys = (first[:, None], second[None, :]) if axis == 0 else (second[None, :], first[:, None])
        rows.append((xs * 4 + ys).reshape(-1))
    cols = jnp.stack(rows).astype(jnp.int32)
    send = weight_parts(cols[:, 8:], attt, out_grad, part)
    got = [swap(s, "seq", k1 << shift[axis]) for s, (axis, k1, k2) in zip(send, ROUTE)]
    keep = weight_parts(cols[:, :8], attt, out_grad, part)

    c, zl = tp & 1, tp >> 1
    mine = jnp.stack([zl, zl ^ 1]) * 2
    lwidth = width // tp_count
    lsend = layer_parts(mine + (c ^ 1), att, out_weight, lwidth)
    lgot = swap(lsend, "tp", 1)
    lkeep = layer_parts(mine + c, att, out_weight, lwidth)
    lgot2 = swap(add(lkeep[1], lgot[1]), "tp", 2)
    layer_out = (lkeep[0].astype(F32) + lgot[0].astype(F32) + lgot2.astype(F32)).astype(BF)

    dq, gk, gv, sl, sr, gfar = backward(*args, attn_grad, att, lse)
    back_left = lax.ppermute(sr, "seq", right_perm)
    back_right = lax.ppermute(sl, "seq", left_perm)
    far_sum = lax.psum_scatter(gfar, "seq", scatter_dimension=1, tiled=True)

    nxt = []
    for k, r, (axis, k1, k2) in zip(keep, got, ROUTE):
        s2 = add(k[4:], r[4:])
        nxt.append((add(k[:4], r[:4]), swap(s2, "seq", k2 << shift[axis])))
    halves = []
    for p in (0, 2):
        axis = ROUTE[p][0]
        a = [add(k, r) for k, r in nxt[p : p + 2]]
        outs = []
        for unit, x in zip(ROUTE[p : p + 2], a):
            _, k1, k2 = unit
            o = shift[1 - axis]
            x = add(x[:2], swap(x[2:], "seq", k1 << o))
            x = add(x[:1], swap(x[1:], "seq", k2 << o))
            outs.append(x[0])
        halves.append(jnp.concatenate(outs, axis=1))
    wsum = jnp.concatenate(halves, axis=1)
    zh = pos & 1
    wkeep = lax.dynamic_index_in_dim(wsum, zh, 0, keepdims=False)
    wsend = lax.dynamic_index_in_dim(wsum, zh ^ 1, 0, keepdims=False)
    wgot = swap(wsend, "seq", 1)
    weight_grad = (wkeep.astype(F32) + wgot.astype(F32)) * (1.0 / math.sqrt(tokens * seq_count))

    key_grad, value_grad = combine(gk, gv, back_left, back_right, far_sum)
    return layer_out, dq, key_grad, value_grad, weight_grad


def solution(mesh):
    return jax.shard_map(
        shards,
        mesh=mesh,
        in_specs=(P("seq", "tp"), P("seq", "tp"), P("seq", "tp"), P("tp", None), P("seq", None)),
        out_specs=(P("seq", "tp"), P("seq", "tp"), P("seq", "tp"), P("seq", "tp"), P("tp", "seq")),
        check_vma=False,
    )
```

time: 505 us -> 568 us (1.12); the launches traced: 498 us -> 567 us
  blocking collectives: 0 us -> 110 us
  waiting for transfers between devices: 229 us -> 306 us
  local copies, waits for them, and re-layouts: 104 us -> 31.3 us
  matrix products: 70.5 us -> 5.54 us
  Pallas kernels: 0 us -> 53.9 us
  starting transfers between devices: 54.2 us -> 28.6 us
  other arithmetic: 23.6 us -> 16 us
    unnamed x2, waiting for transfers between devices: 0.03 us -> 267 us
    all_gather x0 -> x1, blocking collectives: none -> 110 us  [shards(): far = lax.all_gather(far_own, 'seq', axis=1, tiled=True)]
    reduce_scatter x1 -> x0, waiting for transfers between devices: 104 us -> none  [shards(): lax.psum_scatter(head_part, 'tp', scatter_dimension=1, tiled=True)]
    dot_general x15 -> x1, matrix products: 70.5 us -> 5.54 us  [dot(): lax.dot_general(a, b, (((ca,), (cb,)), ((), ())), preferred_element_type=...]
    pallas_call x0 -> x8, Pallas kernels: none -> 53.9 us  [the longest x1 15.5 us: backward(): pl.pallas_call(functools.partial(bwd_kernel, seq_count), grid_spec=pltpu....]
    ppermute x6 -> x23, waiting for transfers between devices: 91.8 us -> 39.1 us  [the longest x19 39.1 us: swap(): return lax.ppermute(x, axis, [(i, i ^ bits) for i in range(n)])]
    all_gather x1 -> x0, waiting for transfers between devices: 33.9 us -> none  [shards(): lax.all_gather(attention, 'seq', axis=0, tiled=True)]
    all_to_all x3 -> x0, starting transfers between devices: 30.9 us -> none  [the longest x1 10.5 us: copy_for_each(): return lax.all_to_all(copies, axis, split_axis=0, concat_axis=0, tiled=True)]
  transfers between devices with their start and end apart: 11 -> 24, of which waited for: 3 -> 12; matrix products, arithmetic and copies ran while one was open for 29% -> 4% of each run, Pallas kernels for 0% -> 6%
where the time goes in v1:
time: 568 us; the launch traced here: 567 us
  waiting for transfers between devices  306 us (54%)
  blocking collectives  110 us (19%)
  Pallas kernels  53.9 us (9%)
  local copies, waits for them, and re-layouts  31.3 us (6%)
  starting transfers between devices  28.6 us (5%)
  other arithmetic  16 us (3%)
  between operations  15.3 us (3%)
    unnamed x2, waiting for transfers between devices  267 us
    all_gather x1, blocking collectives, shards(): far = lax.all_gather(far_own, 'seq', axis=1, tiled=True)  110 us
    ppermute x19, waiting for transfers between devices, swap(): return lax.ppermute(x, axis, [(i, i ^ bits) for i in range(n)])  39.1 us
    unnamed x86, local copies, waits for them, and re-layouts  30.5 us
    ppermute x19, starting transfers between devices, swap(): return lax.ppermute(x, axis, [(i, i ^ bits) for i in range(n)])  15.9 us
    pallas_call x1, Pallas kernels, backward(): pl.pallas_call(functools.partial(bwd_kernel, seq_count), grid_spec=pltpu....  15.5 us
    pallas_call x1, Pallas kernels, forward(): pl.pallas_call(functools.partial(fwd_kernel, seq_count), grid_spec=pltpu....  14.1 us
    convert_element_type x13, other arithmetic, add(): return (a.astype(F32) + b.astype(F32)).astype(BF)  11.8 us
  transfers between devices with their start and end apart: 24, of which 12 were waited for; matrix products, arithmetic and copies ran while one was open for 4% of the time, Pallas kernels for 6%

profile of v1, /device:TPU:0, one launch (start us, length us, event | category | flops | bytes accessed | tf_op | source)
XLA Modules:
  0.0 567.1 jit_solution(4622335718170252643)
XLA Ops:
  9.7 2.5 pool.1
  12.8 5.9 %collective-permute-start = (bf16[2,160,1024]{2,1,0:T(8,128)(2,1)}, bf16[2,160,1024]{2,1,0:T(8,128)(2,1)S(1)}, u32[]{:S(2)}, u32[]{:S(2)}) collective-permute-start(bf16[2,160,1024]{2,1,0:T(8,128)(2,1)} %get-tuple-element.28), channel_id=1, source_target_pairs={{0,4},{4,8},{8,12},{12,16},{16,20},{20,24},{24,28},{28,32},{32,36}... | collective-permute-start | bytes 1966088 | tf_op jit(solution)/shard_map/ppermute | solution.py:343
  20.6 110.0 %all_gather.3 = bf16[2,64,1024]{2,0,1:T(2,128)(2,1)S(1)} all-gather(bf16[2,2,1024]{2,0,1:T(2,128)(2,1)S(1)} %copy.14), channel_id=1, replica_groups=mesh['seq'=32,'tp'=4] {'seq'}, dimensions={1}, use_global_device_ids=true | all-gather | bytes 270336 | tf_op jit(solution)/shard_map/all_gather | solution.py:345
  135.0 14.1 %attend.1 = (bf16[512,1024]{1,0:T(8,128)(2,1)S(1)}, bf16[1024,512]{1,0:T(8,128)(2,1)S(1)}, f32[8,1,512]{2,1,0:T(1,128)S(1)}) custom-call(s32[1]{0:T(128)} %bitcast.2.pos_ref, bf16[512,1024]{1,0:T(8,128)(2,1)S(1)} %copy-done.11, bf16[512,1024]{1,0:T(8,128)(2,1)S(1)} %copy-done.6, bf16[512,1024]{1,0:T(8,128)(2,1)S(1)} %copy-done.8, ...), custom_call_target="tpu_custom_call" | custom-call | tf_op jit(solution)/shard_map/attend/pallas_call | solution.py:178
  149.9 2.6 copy-done.3
  152.5 5.7 %weight_parts.3 = (bf16[8,2,256,128]{3,2,1,0:T(8,128)(2,1)}, bf16[8,2,256,128]{3,2,1,0:T(8,128)(2,1)}, bf16[8,2,256,128]{3,2,1,0:T(8,128)(2,1)}, bf16[8,2,256,128]{3,2,1,0:T(8,128)(2,1)}) custom-call(s32[4,8]{1,0:T(4,128)S(1)} %get-tuple-element.52.cols_ref, bf16[1024,512]{1,0:T(8,128)(2,1)S(1)} %get-tuple-element.42.attt_ref, bf16[512,4096]{1,0:T(8,128)(2,1)S(1)} %copy-done.3), custom_call_target="tpu_custom_call" | custom-call | tf_op jit(solution)/shard_map/weight_parts/pallas_call | solution.py:283
  158.5 5.5 convolution_convert_fusion.do_ref
  164.2 2.2 copy-done.4
  167.6 4.3 weight_parts.2
  173.0 15.5 %attend_grad.1 = (bf16[512,1024]{1,0:T(8,128)(2,1)}, f32[512,1024]{1,0:T(8,128)S(1)}, f32[512,1024]{1,0:T(8,128)S(1)}, bf16[2,160,1024]{2,1,0:T(8,128)(2,1)}, bf...) custom-call(s32[1]{0:T(128)} %bitcast.2.pos_ref, bf16[512,1024]{1,0:T(8,128)(2,1)S(1)} %copy-done.12, ...), custom_call_target="tpu_custom_call" | custom-call | tf_op jit(solution)/shard_map/attend_grad/pallas_call | solution.py:202
  191.9 4.1 collective-permute-start.4
  196.0 3.4 copy-done.1
  199.4 3.9 layer_parts.3
  203.3 3.4 copy-done.2
  206.7 3.9 layer_parts.2
  214.7 8.2 %collective-permute-start.7 = (bf16[4,2,256,128]{3,2,1,0:T(8,128)(2,1)S(1)}, bf16[4,2,256,128]{3,2,1,0:T(8,128)(2,1)S(1)}, u32[]{:S(2)}, u32[]{:S(2)}) collective-permute-start(bf16[4,2,256,128]{3,2,1,0:T(8,128)(2,1)S(1)} %add_convert_fusion.11), channel_id=1, source_target_pairs={{0,96},{4,100},{8,104},{12,108},{16,112},{20,116},{24,120},{28,124... | collective-permute-start | bytes 1572872 | tf_op jit(solution)/shard_map/ppermute | solution.py:325
  226.1 9.4 %collective-permute-done.7 = bf16[4,2,256,128]{3,2,1,0:T(8,128)(2,1)S(1)} collective-permute-done((bf16[4,2,256,128]{3,2,1,0:T(8,128)(2,1)S(1)}, bf16[4,2,256,128]{3,2,1,0:T(8,128)(2,1)S(1)}, u32[]{:S(2)}, u32[]{:S(2)}) %collective-permute-start.7) | collective-permute-done | bytes 524320 | tf_op jit(solution)/shard_map/ppermute | solution.py:325
  237.9 1.7 collective-permute-done.11
  240.9 9.7 %collective-permute-done.15 = bf16[4,2,256,128]{3,2,1,0:T(8,128)(2,1)S(1)} collective-permute-done((bf16[4,2,256,128]{3,2,1,0:T(8,128)(2,1)S(1)}, bf16[4,2,256,128]{3,2,1,0:T(8,128)(2,1)S(1)}, u32[]{:S(2)}, u32[]{:S(2)}) %collective-permute-start.15) | collective-permute-done | bytes 524320 | tf_op jit(solution)/shard_map/ppermute | solution.py:325
  251.8 2.0 collective-permute-done.19
  255.1 3.7 collective-permute-done.8
  259.5 1.9 collective-permute-done.12
  261.4 2.2 collective-permute-start.20
  263.7 2.7 collective-permute-done.16
  266.5 2.4 collective-permute-done.20
  269.2 3.5 collective-permute-done.9
  274.1 1.6 fusion.1
  276.9 1.9 collective-permute-done.17
  281.2 267.3 %all-reduce.3.cloned.1.call-done = f32[2,64,1024]{2,1,0:T(8,128)} async-done(((f32[2,64,1024]{2,1,0:T(8,128)}), f32[2,64,1024]{2,1,0:T(8,128)}) %all-reduce.3.cloned.1.call-update) | async-done | bytes 524304
  551.0 1.6 copy-done.21
  552.5 4.0 combine.1
  557.4 2.8 fusion
  (162 shorter events, 38.1 us)
Async XLA Ops:
  7.2 12.9 %copy-start.39 = (s32[4]{0:T(128)S(1)}, s32[4]{0:T(128)}, u32[]{:S(2)}) copy-start(s32[4]{0:T(128)} %constant.92.clone) | copy-start | bytes 52
  7.2 12.9 %copy-start.40 = (s32[4]{0:T(128)S(1)}, s32[4]{0:T(128)}, u32[]{:S(2)}) copy-start(s32[4]{0:T(128)} %constant.93.clone) | copy-start | bytes 52
  7.2 541.3 %all-reduce.3.cloned.1.call-start = ((), (), s32[]{:S(2)}) async-start(), calls=%async_computation | async-start | bytes 1048576
  9.7 122.1 %copy-start.6 = (bf16[512,1024]{1,0:T(8,128)(2,1)S(1)}, bf16[512,1024]{1,0:T(8,128)(2,1)}, u32[]{:S(2)}) copy-start(bf16[512,1024]{1,0:T(8,128)(2,1)} %k_ref.5) | copy-start | bytes 3145732
  9.7 122.1 %copy-start.8 = (bf16[512,1024]{1,0:T(8,128)(2,1)S(1)}, bf16[512,1024]{1,0:T(8,128)(2,1)}, u32[]{:S(2)}) copy-start(bf16[512,1024]{1,0:T(8,128)(2,1)} %v_ref.5) | copy-start | bytes 3145732
  12.8 118.0 %collective-permute-start = (bf16[2,160,1024]{2,1,0:T(8,128)(2,1)}, bf16[2,160,1024]{2,1,0:T(8,128)(2,1)S(1)}, u32[]{:S(2)}, u32[]{:S(2)}) collective-permute-start(bf16[2,160,1024]{2,1,0:T(8,128)(2,1)} %get-tuple-element.28), channel_id=1, source_target_pairs={{0,4},{4,8},{8,12},{12,16},{16,20},{20,24},{24,28},{28,32},{32,36}... | collective-permute-start | bytes 1966088 | tf_op jit(solution)/shard_map/ppermute | solution.py:343
  18.7 112.9 %collective-permute-start.1 = (bf16[2,160,1024]{2,1,0:T(8,128)(2,1)}, bf16[2,160,1024]{2,1,0:T(8,128)(2,1)}, u32[]{:S(2)}, u32[]{:S(2)}) collective-permute-start(bf16[2,160,1024]{2,1,0:T(8,128)(2,1)} %get-tuple-element.29), channel_id=1, source_target_pairs={{4,0},{8,4},{12,8},{16,12},{20,16},{24,20},{28,24},{32,28},{36,32}... | collective-permute-start | bytes 1966088 | tf_op jit(solution)/shard_map/ppermute | solution.py:344
  135.0 23.4 %copy-start = (bf16[1024,4096]{1,0:T(8,128)(2,1)S(1)}, bf16[1024,4096]{1,0:T(8,128)(2,1)}, u32[]{:S(2)}) copy-start(bf16[1024,4096]{1,0:T(8,128)(2,1)} %w_ref.3) | copy-start | bytes 25165828
  158.2 52.5 %collective-permute-start.6 = (bf16[8,2,256,128]{3,2,1,0:T(8,128)(2,1)}, bf16[8,2,256,128]{3,2,1,0:T(8,128)(2,1)}, u32[]{:S(2)}, u32[]{:S(2)}) collective-permute-start(bf16[8,2,256,128]{3,2,1,0:T(8,128)(2,1)} %get-tuple-element.44), channel_id=1, source_target_pairs={{0,32},{4,36},{8,40},{12,44},{16,48},{20,52},{24,56},{28,60},{32,0... | collective-permute-start | bytes 3145736 | tf_op jit(solution)/shard_map/ppermute | solution.py:325
  158.2 55.2 %collective-permute-start.10 = (bf16[8,2,256,128]{3,2,1,0:T(8,128)(2,1)}, bf16[8,2,256,128]{3,2,1,0:T(8,128)(2,1)}, u32[]{:S(2)}, u32[]{:S(2)}) collective-permute-start(bf16[8,2,256,128]{3,2,1,0:T(8,128)(2,1)} %get-tuple-element.46), channel_id=1, source_target_pairs={{0,96},{4,100},{8,104},{12,108},{16,112},{20,116},{24,120},{28,124... | collective-permute-start | bytes 3145736 | tf_op jit(solution)/shard_map/ppermute | solution.py:325
  158.3 56.4 %collective-permute-start.14 = (bf16[8,2,256,128]{3,2,1,0:T(8,128)(2,1)}, bf16[8,2,256,128]{3,2,1,0:T(8,128)(2,1)}, u32[]{:S(2)}, u32[]{:S(2)}) collective-permute-start(bf16[8,2,256,128]{3,2,1,0:T(8,128)(2,1)} %get-tuple-element.48), channel_id=1, source_target_pairs={{0,8},{4,12},{8,0},{12,4},{16,24},{20,28},{24,16},{28,20},{32,40},... | collective-permute-start | bytes 3145736 | tf_op jit(solution)/shard_map/ppermute | solution.py:325
  158.4 65.8 %collective-permute-start.18 = (bf16[8,2,256,128]{3,2,1,0:T(8,128)(2,1)}, bf16[8,2,256,128]{3,2,1,0:T(8,128)(2,1)}, u32[]{:S(2)}, u32[]{:S(2)}) collective-permute-start(bf16[8,2,256,128]{3,2,1,0:T(8,128)(2,1)} %get-tuple-element.50), channel_id=1, source_target_pairs={{0,24},{4,28},{8,16},{12,20},{16,8},{20,12},{24,0},{28,4},{32,56},... | collective-permute-start | bytes 3145736 | tf_op jit(solution)/shard_map/ppermute | solution.py:325
  172.9 15.5 %copy-start.24 = (bf16[8,2,256,128]{3,2,1,0:T(8,128)(2,1)}, bf16[8,2,256,128]{3,2,1,0:T(8,128)(2,1)S(1)}, u32[]{:S(2)}) copy-start(bf16[8,2,256,128]{3,2,1,0:T(8,128)(2,1)S(1)} %get-tuple-element.47) | copy-start | bytes 3145732
  172.9 15.5 %copy-start.26 = (bf16[8,2,256,128]{3,2,1,0:T(8,128)(2,1)}, bf16[8,2,256,128]{3,2,1,0:T(8,128)(2,1)S(1)}, u32[]{:S(2)}) copy-start(bf16[8,2,256,128]{3,2,1,0:T(8,128)(2,1)S(1)} %get-tuple-element.45) | copy-start | bytes 3145732
  172.9 15.5 %copy-start.28 = (bf16[8,2,256,128]{3,2,1,0:T(8,128)(2,1)}, bf16[8,2,256,128]{3,2,1,0:T(8,128)(2,1)S(1)}, u32[]{:S(2)}) copy-start(bf16[8,2,256,128]{3,2,1,0:T(8,128)(2,1)S(1)} %get-tuple-element.43) | copy-start | bytes 3145732
  191.9 357.4 %collective-permute-start.4 = (bf16[2,160,1024]{2,1,0:T(8,128)(2,1)}, bf16[2,160,1024]{2,1,0:T(8,128)(2,1)}, u32[]{:S(2)}, u32[]{:S(2)}) collective-permute-start(bf16[2,160,1024]{2,1,0:T(8,128)(2,1)} %get-tuple-element.37), channel_id=1, source_target_pairs={{0,4},{4,8},{8,12},{12,16},{16,20},{20,24},{24,28},{28,32},{32,36}... | collective-permute-start | bytes 1966088 | tf_op jit(solution)/shard_map/ppermute | solution.py:376
  210.7 338.7 %collective-permute-start.5 = (bf16[2,160,1024]{2,1,0:T(8,128)(2,1)}, bf16[2,160,1024]{2,1,0:T(8,128)(2,1)S(1)}, u32[]{:S(2)}, u32[]{:S(2)}) collective-permute-start(bf16[2,160,1024]{2,1,0:T(8,128)(2,1)} %get-tuple-element.38), channel_id=1, source_target_pairs={{4,0},{8,4},{12,8},{16,12},{20,16},{24,20},{28,24},{32,28},{36,32}... | collective-permute-start | bytes 1966088 | tf_op jit(solution)/shard_map/ppermute | solution.py:377
  213.4 60.7 %collective-permute-start.2 = (bf16[2,512,1024]{2,1,0:T(8,128)(2,1)S(1)}, bf16[2,512,1024]{2,1,0:T(8,128)(2,1)S(1)}, u32[]{:S(2)}, u32[]{:S(2)}) collective-permute-start(bf16[2,512,1024]{2,1,0:T(8,128)(2,1)S(1)} %layer_parts.3), channel_id=1, source_target_pairs={{0,1},{1,0},{2,3},{3,2},{4,5},{5,4},{6,7},{7,6},{8,9},{9,8},{10,11... | collective-permute-start | bytes 6291464 | tf_op jit(solution)/shard_map/ppermute | solution.py:325
  214.7 20.8 %collective-permute-start.7 = (bf16[4,2,256,128]{3,2,1,0:T(8,128)(2,1)S(1)}, bf16[4,2,256,128]{3,2,1,0:T(8,128)(2,1)S(1)}, u32[]{:S(2)}, u32[]{:S(2)}) collective-permute-start(bf16[4,2,256,128]{3,2,1,0:T(8,128)(2,1)S(1)} %add_convert_fusion.11), channel_id=1, source_target_pairs={{0,96},{4,100},{8,104},{12,108},{16,112},{20,116},{24,120},{28,124... | collective-permute-start | bytes 1572872 | tf_op jit(solution)/shard_map/ppermute | solution.py:325
  224.1 15.4 %collective-permute-start.11 = (bf16[4,2,256,128]{3,2,1,0:T(8,128)(2,1)S(1)}, bf16[4,2,256,128]{3,2,1,0:T(8,128)(2,1)S(1)}, u32[]{:S(2)}, u32[]{:S(2)}) collective-permute-start(bf16[4,2,256,128]{3,2,1,0:T(8,128)(2,1)S(1)} %add_convert_fusion.8), channel_id=1, source_target_pairs={{0,32},{4,36},{8,40},{12,44},{16,48},{20,52},{24,56},{28,60},{32,0... | collective-permute-start | bytes 1572872 | tf_op jit(solution)/shard_map/ppermute | solution.py:325
  235.5 15.1 %collective-permute-start.15 = (bf16[4,2,256,128]{3,2,1,0:T(8,128)(2,1)S(1)}, bf16[4,2,256,128]{3,2,1,0:T(8,128)(2,1)S(1)}, u32[]{:S(2)}, u32[]{:S(2)}) collective-permute-start(bf16[4,2,256,128]{3,2,1,0:T(8,128)(2,1)S(1)} %add_convert_fusion.5), channel_id=1, source_target_pairs={{0,24},{4,28},{8,16},{12,20},{16,8},{20,12},{24,0},{28,4},{32,56},... | collective-permute-start | bytes 1572872 | tf_op jit(solution)/shard_map/ppermute | solution.py:325
  239.6 14.2 %collective-permute-start.19 = (bf16[4,2,256,128]{3,2,1,0:T(8,128)(2,1)S(1)}, bf16[4,2,256,128]{3,2,1,0:T(8,128)(2,1)S(1)}, u32[]{:S(2)}, u32[]{:S(2)}) collective-permute-start(bf16[4,2,256,128]{3,2,1,0:T(8,128)(2,1)S(1)} %add_convert_fusion.2), channel_id=1, source_target_pairs={{0,8},{4,12},{8,0},{12,4},{16,24},{20,28},{24,16},{28,20},{32,40},... | collective-permute-start | bytes 1572872 | tf_op jit(solution)/shard_map/ppermute | solution.py:325
  250.6 8.3 %collective-permute-start.8 = (bf16[2,2,256,128]{3,2,1,0:T(8,128)(2,1)S(1)}, bf16[2,2,256,128]{3,2,1,0:T(8,128)(2,1)S(1)}, u32[]{:S(2)}, u32[]{:S(2)}) collective-permute-start(bf16[2,2,256,128]{3,2,1,0:T(8,128)(2,1)S(1)} %slice.159), channel_id=1, source_target_pairs={{0,8},{4,12},{8,0},{12,4},{16,24},{20,28},{24,16},{28,20},{32,40},... | collective-permute-start | bytes 786440 | tf_op jit(solution)/shard_map/ppermute | solution.py:325
  253.8 7.6 %collective-permute-start.12 = (bf16[2,2,256,128]{3,2,1,0:T(8,128)(2,1)S(1)}, bf16[2,2,256,128]{3,2,1,0:T(8,128)(2,1)S(1)}, u32[]{:S(2)}, u32[]{:S(2)}) collective-permute-start(bf16[2,2,256,128]{3,2,1,0:T(8,128)(2,1)S(1)} %slice.165), channel_id=1, source_target_pairs={{0,24},{4,28},{8,16},{12,20},{16,8},{20,12},{24,0},{28,4},{32,56},... | collective-permute-start | bytes 786440 | tf_op jit(solution)/shard_map/ppermute | solution.py:325
  258.9 7.6 %collective-permute-start.16 = (bf16[2,2,256,128]{3,2,1,0:T(8,128)(2,1)S(1)}, bf16[2,2,256,128]{3,2,1,0:T(8,128)(2,1)S(1)}, u32[]{:S(2)}, u32[]{:S(2)}) collective-permute-start(bf16[2,2,256,128]{3,2,1,0:T(8,128)(2,1)S(1)} %slice.171), channel_id=1, source_target_pairs={{0,32},{4,36},{8,40},{12,44},{16,48},{20,52},{24,56},{28,60},{32,0... | collective-permute-start | bytes 786440 | tf_op jit(solution)/shard_map/ppermute | solution.py:325
  261.4 7.6 %collective-permute-start.20 = (bf16[2,2,256,128]{3,2,1,0:T(8,128)(2,1)S(1)}, bf16[2,2,256,128]{3,2,1,0:T(8,128)(2,1)S(1)}, u32[]{:S(2)}, u32[]{:S(2)}) collective-permute-start(bf16[2,2,256,128]{3,2,1,0:T(8,128)(2,1)S(1)} %slice.177), channel_id=1, source_target_pairs={{0,96},{4,100},{8,104},{12,108},{16,112},{20,116},{24,120},{28,124... | collective-permute-start | bytes 786440 | tf_op jit(solution)/shard_map/ppermute | solution.py:325
  266.4 6.2 %collective-permute-start.9 = (bf16[1,2,256,128]{3,2,1,0:T(8,128)(2,1)S(1)}, bf16[1,2,256,128]{3,2,1,0:T(8,128)(2,1)S(1)}, u32[]{:S(2)}, u32[]{:S(2)}) collective-permute-start(bf16[1,2,256,128]{3,2,1,0:T(8,128)(2,1)S(1)} %slice.161), channel_id=1, source_target_pairs={{0,24},{4,28},{8,16},{12,20},{16,8},{20,12},{24,0},{28,4},{32,56},... | collective-permute-start | bytes 393224 | tf_op jit(solution)/shard_map/ppermute | solution.py:325
  269.0 5.0 collective-permute-start.13
  272.6 6.2 %collective-permute-start.17 = (bf16[1,2,256,128]{3,2,1,0:T(8,128)(2,1)S(1)}, bf16[1,2,256,128]{3,2,1,0:T(8,128)(2,1)S(1)}, u32[]{:S(2)}, u32[]{:S(2)}) collective-permute-start(bf16[1,2,256,128]{3,2,1,0:T(8,128)(2,1)S(1)} %slice.173), channel_id=1, source_target_pairs={{0,96},{4,100},{8,104},{12,108},{16,112},{20,116},{24,120},{28,124... | collective-permute-start | bytes 393224 | tf_op jit(solution)/shard_map/ppermute | solution.py:325
  273.9 5.1 collective-permute-start.21
  275.8 281.7 %collective-permute-start.3 = (bf16[512,1024]{1,0:T(8,128)(2,1)}, bf16[512,1024]{1,0:T(8,128)(2,1)}, u32[]{:S(2)}, u32[]{:S(2)}) collective-permute-start(bf16[512,1024]{1,0:T(8,128)(2,1)} %fusion.1), channel_id=1, source_target_pairs={{0,2},{1,3},{2,0},{3,1},{4,6},{5,7},{6,4},{7,5},{8,10},{9,11},{10,... | collective-permute-start | bytes 3145736 | tf_op jit(solution)/shard_map/ppermute | solution.py:325
  279.9 276.6 %collective-permute-start.22 = (bf16[1024,128]{1,0:T(8,128)(2,1)S(1)}, bf16[1024,128]{1,0:T(8,128)(2,1)S(1)}, u32[]{:S(2)}, u32[]{:S(2)}) collective-permute-start(bf16[1024,128]{1,0:T(8,128)(2,1)S(1)} %dynamic-slice_bitcast_fusion), channel_id=1, source_target_pairs={{0,4},{4,0},{8,12},{12,8},{16,20},{20,16},{24,28},{28,24},{32,36},... | collective-permute-start | bytes 786440 | tf_op jit(solution)/shard_map/ppermute | solution.py:325
  (34 other events, 121.1 us)
Sparse Core Ops, SparseCore 0:
  196.1 352.3 all-reduce.2

commit v2 on v1

--- a/solution.py
+++ b/solution.py
@@ -17,6 +17,8 @@
 NEG = -1e30
 LOG2E = math.log2(math.e)
 MB = 1024 * 1024
+HALVES = 2
+BIG = 58
 
 
 def dot(a, b, ca, cb):
@@ -42,19 +44,20 @@
         right_ref[i, FB:] = near
 
 
-def pool(k, v):
-    rows, feats = k.shape
+def pool(k, v, half):
+    rows, feats = k.shape[0], k.shape[1] // HALVES
     nr, fr = rows // P1, rows // P2
     cols = 256
+    per = feats // cols
     blk = lambda r: pl.BlockSpec((2, r, cols), lambda j: (0, 0, j))
     out = lambda r: jax.ShapeDtypeStruct((2, r, feats), BF)
     return pl.pallas_call(
         pool_kernel,
-        grid=(feats // cols,),
-        in_specs=[pl.BlockSpec((rows, cols), lambda j: (0, j))] * 2,
+        grid=(per,),
+        in_specs=[pl.BlockSpec((rows, cols), lambda j: (0, half * per + j))] * 2,
         out_specs=[blk(nr), blk(fr), blk(FB + nr), blk(FB + nr)],
         out_shape=[out(nr), out(fr), out(FB + nr), out(FB + nr)],
-        compiler_params=params(24),
+        compiler_params=params(BIG),
         name="pool",
     )(k, v)
 
@@ -148,7 +151,7 @@
         cg = dot(csrc[...], rhs, 1, 0) * mul
         sl_ref[i, FB:] = cg[:nr].astype(BF)
         sr_ref[i, FB:] = cg[2 * nr : 3 * nr].astype(BF)
-        gfar_ref[i] = cg[3 * nr :]
+        gfar_ref[i] = cg[3 * nr :].astype(BF)
         mine = cg[nr : 2 * nr] * (1.0 / P1)
         for c in range(blocks + 2):
             lo, hi = max(0, c - 2), min(blocks, c + 1)
@@ -164,47 +167,70 @@
                 g_ref[r * FB : (r + 1) * FB, :] = part + spread
 
 
-def attention_specs(tokens, halo, nr, fr, blocks):
-    tok = pl.BlockSpec((tokens, DH), lambda h, *_: (0, h))
-    lev = lambda r: pl.BlockSpec((2, r, DH), lambda h, *_: (0, 0, h))
-    bias = pl.BlockSpec((blocks, 3 * nr + fr, FB), lambda h, *_: (0, 0, 0))
-    return tok, [tok, tok, tok, lev(halo), lev(halo), lev(nr), lev(fr), bias], lev
-
-
-def forward(seq_count, pos, q, k, v, left, right, near, far, bias):
-    tokens, feats = q.shape
-    heads = feats // DH
-    tok, specs, _ = attention_specs(tokens, left.shape[1], near.shape[1], far.shape[1], tokens // FB)
+def forward(seq_count, pos, q, k, v, left, right, near, far, bias, half):
+    tokens, feats = q.shape[0], q.shape[1] // HALVES
+    heads, blocks = feats // DH, tokens // FB
+    tok = pl.BlockSpec((tokens, DH), lambda h, *_: (0, half * heads + h))
+    lev = lambda a: pl.BlockSpec((2, a.shape[1], DH), lambda h, *_: (0, 0, h))
+    far_spec = pl.BlockSpec((2, far.shape[1], DH), lambda h, *_: (0, 0, half * heads + h))
+    bias_spec = pl.BlockSpec(bias.shape, lambda h, *_: (0, 0, 0))
     return pl.pallas_call(
         functools.partial(fwd_kernel, seq_count),
         grid_spec=pltpu.PrefetchScalarGridSpec(
             num_scalar_prefetch=1,
             grid=(heads,),
-            in_specs=specs,
-            out_specs=[tok, pl.BlockSpec((DH, tokens), lambda h, *_: (h, 0)), pl.BlockSpec((1, 1, tokens), lambda h, *_: (h, 0, 0))],
+            in_specs=[tok, tok, tok, lev(left), lev(right), lev(near), far_spec, bias_spec],
+            out_specs=[
+                pl.BlockSpec((tokens, DH), lambda h, *_: (0, h)),
+                pl.BlockSpec((DH, tokens), lambda h, *_: (h, 0)),
+                pl.BlockSpec((1, 1, tokens), lambda h, *_: (h, 0, 0)),
+            ],
         ),
         out_shape=[
             jax.ShapeDtypeStruct((tokens, feats), BF),
             jax.ShapeDtypeStruct((feats, tokens), BF),
             jax.ShapeDtypeStruct((heads, 1, tokens), F32),
         ],
-        compiler_params=params(32),
+        compiler_params=params(BIG),
         name="attend",
     )(pos, q, k, v, left, right, near, far, bias)
+
+
+def bwd_halves_kernel(seq_count, pos_ref, q_ref, k_ref, v_ref, *refs):
+    per = pl.num_programs(0) // HALVES
+    first = pl.program_id(0) < per
+    pairs, rest = refs[: 5 * HALVES], refs[5 * HALVES :]
+    picked = [jnp.where(first, pairs[2 * i][...], pairs[2 * i + 1][...]) for i in range(5)]
+    left, right, near, att, lse = picked
+    far_ref, bias_ref, do_ref, *outs = rest
+    bwd_kernel(seq_count, pos_ref, q_ref, k_ref, v_ref, left, right, near, far_ref, bias_ref, do_ref, att, lse, *outs)
 
 
 def backward(seq_count, pos, q, k, v, left, right, near, far, bias, do, att, lse):
     tokens, feats = q.shape
     heads = feats // DH
-    halo, nr, fr = left.shape[1], near.shape[1], far.shape[1]
-    tok, specs, lev = attention_specs(tokens, halo, nr, fr, tokens // FB)
+    per = heads // HALVES
+    halo, nr, fr = left[0].shape[1], near[0].shape[1], far.shape[1]
     coarse = 3 * nr + fr
-    return pl.pallas_call(
-        functools.partial(bwd_kernel, seq_count),
+    tok = pl.BlockSpec((tokens, DH), lambda h, *_: (0, h))
+    lev = lambda r: pl.BlockSpec((2, r, DH), lambda h, *_: (0, 0, h))
+    at = (lambda h: jnp.minimum(h, per - 1), lambda h: jnp.maximum(h - per, 0))
+    pairs, pair_specs = [], []
+    for x in (left, right, near, att, lse):
+        for half, pick in enumerate(at):
+            pairs.append(x[half])
+            if x is att:
+                pair_specs.append(pl.BlockSpec((tokens, DH), lambda h, *_, p=pick: (0, p(h))))
+            elif x is lse:
+                pair_specs.append(pl.BlockSpec((1, 1, tokens), lambda h, *_, p=pick: (p(h), 0, 0)))
+            else:
+                pair_specs.append(pl.BlockSpec((2, x[half].shape[1], DH), lambda h, *_, p=pick: (0, 0, p(h))))
+    return pl.pallas_call(
+        functools.partial(bwd_halves_kernel, seq_count),
         grid_spec=pltpu.PrefetchScalarGridSpec(
             num_scalar_prefetch=1,
             grid=(heads,),
-            in_specs=[*specs, tok, tok, pl.BlockSpec((1, 1, tokens), lambda h, *_: (h, 0, 0))],
+            in_specs=[tok, tok, tok, *pair_specs, lev(fr), pl.BlockSpec(bias.shape, lambda h, *_: (0, 0, 0)), tok],
             out_specs=[tok, tok, tok, lev(halo), lev(halo), lev(fr)],
             scratch_shapes=[
                 pltpu.VMEM((tokens + 2 * FB, tokens), BF),
@@ -219,11 +245,11 @@
             jax.ShapeDtypeStruct((tokens, feats), F32),
             jax.ShapeDtypeStruct((2, halo, feats), BF),
             jax.ShapeDtypeStruct((2, halo, feats), BF),
-            jax.ShapeDtypeStruct((2, fr, feats), F32),
+            jax.ShapeDtypeStruct((2, fr, feats), BF),
         ],
-        compiler_params=params(40),
+        compiler_params=params(BIG),
         name="attend_grad",
-    )(pos, q, k, v, left, right, near, far, bias, do, att, lse)
+    )(pos, q, k, v, *pairs, far, bias, do)
 
 
 def combine_kernel(gk_ref, gv_ref, left_ref, right_ref, far_ref, ok_ref, ov_ref):
@@ -255,51 +281,138 @@
         in_specs=[tok, tok, lev(halo), lev(halo), lev(far.shape[1])],
         out_specs=[tok, tok],
         out_shape=[jax.ShapeDtypeStruct((rows, feats), BF)] * 2,
-        compiler_params=params(32),
+        compiler_params=params(BIG),
         name="combine",
     )(gk, gv, from_left, from_right, far)
 
 
 UNITS = 4
 ROUTE = ((0, 1, 3), (0, 3, 1), (1, 1, 3), (1, 3, 1))
-
-
-def weight_kernel(cols_ref, attt_ref, og_ref, *out_refs):
-    j = pl.program_id(0)
-    width = out_refs[0].shape[-1]
-    rows = attt_ref.shape[0] // UNITS
-    for u, o_ref in enumerate(out_refs):
-        at = pl.multiple_of(cols_ref[u, j] * (2 * width), 2 * width)
-        res = dot(attt_ref[u * rows : (u + 1) * rows, :], og_ref[:, pl.ds(at, 2 * width)], 1, 0).astype(BF)
-        o_ref[0, 0] = res[:, :width]
-        o_ref[0, 1] = res[:, width:]
-
-
-def weight_parts(cols, attt, og, width):
-    feats, tokens = attt.shape
-    steps = cols.shape[1]
-    rows = feats // UNITS
-    whole = lambda a: pl.BlockSpec(a.shape, lambda j, *_: (0, 0))
-    return pl.pallas_call(
-        weight_kernel,
+SECOND = ((1, 3), (3, 1))
+SHIFT = (3, 1)
+
+
+def block_order(pos):
+    coord = ((pos >> 3) & 3, (pos >> 1) & 3)
+    rows = []
+    for u, (axis, k1, k2) in enumerate(ROUTE):
+        m1, m2 = SECOND[u // 2]
+        first = coord[axis] ^ jnp.array([0, k2, k1, k1 ^ k2], jnp.int32)
+        second = coord[1 - axis] ^ jnp.array([0, m2, m1, m1 ^ m2], jnp.int32)
+        at = first[:, None] * 4 + second[None, :] if axis == 0 else second[None, :] * 4 + first[:, None]
+        rows.append(at.reshape(-1))
+    return jnp.stack(rows).astype(jnp.int32)
+
+
+def weight_kernel(n_units, n_recv, pair_out, cols_ref, *refs):
+    atts, ogs = refs[:n_units], refs[n_units : 2 * n_units]
+    recvs = refs[2 * n_units : 2 * n_units + n_recv]
+    outs = refs[2 * n_units + n_recv :]
+    for u in range(n_units):
+        res = dot(atts[u][...], ogs[u][...], 1, 0)
+        rows, width = res.shape[0], res.shape[1] // 2
+        for z in range(2):
+            part = res[:, z * width : (z + 1) * width]
+            for r in recvs[u::n_units]:
+                part += r[0, z].astype(F32)
+            if pair_out:
+                outs[u // 2][0, z, (u % 2) * rows : (u % 2 + 1) * rows] = part.astype(BF)
+            else:
+                outs[u][0, z] = part.astype(BF)
+
+
+def weight_step(cols, attt, og, width, units, start, count, recvs, pair_out):
+    tokens = attt[0].shape[1]
+    rows = attt[0].shape[0] * HALVES // UNITS
+    n = len(units)
+    per_half = UNITS // HALVES
+    in_specs, args = [], []
+    for u in units:
+        in_specs.append(pl.BlockSpec((rows, tokens), lambda j, *_, u=u: (u % per_half, 0)))
+        args.append(attt[u // per_half])
+    for u in units:
+        in_specs.append(pl.BlockSpec((tokens, 2 * width), lambda j, c, u=u: (0, c[u, start + j])))
+        args.append(og)
+    for step in recvs:
+        for u in units:
+            r, paired = step[u]
+            if paired:
+                in_specs.append(pl.BlockSpec((1, 2, rows, width), lambda j, *_, u=u: (start + j, 0, u % 2, 0)))
+            else:
+                in_specs.append(pl.BlockSpec((1, 2, rows, width), lambda j, *_: (start + j, 0, 0, 0)))
+            args.append(r)
+    n_out = n // 2 if pair_out else n
+    out_rows = 2 * rows if pair_out else rows
+    return pl.pallas_call(
+        functools.partial(weight_kernel, n, len(recvs) * n, pair_out),
         grid_spec=pltpu.PrefetchScalarGridSpec(
             num_scalar_prefetch=1,
-            grid=(steps,),
-            in_specs=[whole(attt), whole(og)],
-            out_specs=[pl.BlockSpec((1, 2, rows, width), lambda j, *_: (j, 0, 0, 0))] * UNITS,
+            grid=(count,),
+            in_specs=in_specs,
+            out_specs=[pl.BlockSpec((1, 2, out_rows, width), lambda j, *_: (j, 0, 0, 0))] * n_out,
         ),
-        out_shape=[jax.ShapeDtypeStruct((steps, 2, rows, width), BF)] * UNITS,
-        compiler_params=params(40),
-        name="weight_parts",
-    )(cols, attt, og)
-
-
-def layer_kernel(cols_ref, att_ref, w_ref, o_ref):
-    o_ref[0] = dot(att_ref[...], w_ref[...], 1, 0).astype(BF)
-
-
-def layer_parts(cols, att, w, width):
-    tokens, feats = att.shape
+        out_shape=[jax.ShapeDtypeStruct((count, 2, out_rows, width), BF)] * n_out,
+        compiler_params=params(BIG),
+        name="weight_step",
+    )(cols, *args)
+
+
+def weight_last_kernel(scale, n_recv, last, cols_ref, *refs):
+    o_ref = refs[-1]
+    atts, ogs = refs[:UNITS], refs[UNITS : 2 * UNITS]
+    recvs = refs[2 * UNITS : 2 * UNITS + n_recv]
+    rows = atts[0].shape[0]
+    for u in range(UNITS):
+        part = dot(atts[u][...], ogs[u][...], 1, 0)
+        for r in recvs[u::UNITS]:
+            part += r[0, 0].astype(F32)
+        if last:
+            part += refs[2 * UNITS + n_recv][u * rows : (u + 1) * rows].astype(F32)
+        o_ref[u * rows : (u + 1) * rows] = (part * scale).astype(o_ref.dtype)
+
+
+def weight_last(cols, attt, og, width, z, recvs, got, scale, dtype):
+    tokens = attt[0].shape[1]
+    rows = attt[0].shape[0] * HALVES // UNITS
+    per_half = UNITS // HALVES
+    table = jnp.concatenate([cols[:, 0] * 2 + z, z[None]])
+    in_specs, args = [], []
+    for u in range(UNITS):
+        in_specs.append(pl.BlockSpec((rows, tokens), lambda j, *_, u=u: (u % per_half, 0)))
+        args.append(attt[u // per_half])
+    for u in range(UNITS):
+        in_specs.append(pl.BlockSpec((tokens, width), lambda j, c, u=u: (0, c[u])))
+        args.append(og)
+    for step in recvs:
+        for u in range(UNITS):
+            r, paired = step[u]
+            at = u % 2 if paired else 0
+            in_specs.append(pl.BlockSpec((1, 1, rows, width), lambda j, c, at=at: (0, c[UNITS], at, 0)))
+            args.append(r)
+    full = pl.BlockSpec((UNITS * rows, width), lambda j, *_: (0, 0))
+    if got is not None:
+        in_specs.append(full)
+        args.append(got)
+    return pl.pallas_call(
+        functools.partial(weight_last_kernel, scale, len(recvs) * UNITS, got is not None),
+        grid_spec=pltpu.PrefetchScalarGridSpec(num_scalar_prefetch=1, grid=(1,), in_specs=in_specs, out_specs=full),
+        out_shape=jax.ShapeDtypeStruct((UNITS * rows, width), dtype),
+        compiler_params=params(BIG),
+        name="weight_last",
+    )(table, *args)
+
+
+def layer_kernel(cols_ref, a0_ref, a1_ref, w_ref, *refs):
+    o_ref = refs[-1]
+    half = a0_ref.shape[1]
+    res = dot(a0_ref[...], w_ref[:half], 1, 0) + dot(a1_ref[...], w_ref[half:], 1, 0)
+    for r in refs[:-1]:
+        res += r[0].astype(F32)
+    o_ref[0] = res.astype(BF)
+
+
+def layer_step(cols, att, w, width, recvs):
+    tokens, half = att[0].shape
     steps = cols.shape[0]
     sub = 2
     n = width // sub
@@ -309,15 +422,17 @@
             num_scalar_prefetch=1,
             grid=(steps, sub),
             in_specs=[
-                pl.BlockSpec((tokens, feats), lambda j, s, *_: (0, 0)),
-                pl.BlockSpec((feats, n), lambda j, s, c: (0, c[j] * sub + s)),
+                pl.BlockSpec((tokens, half), lambda j, s, *_: (0, 0)),
+                pl.BlockSpec((tokens, half), lambda j, s, *_: (0, 0)),
+                pl.BlockSpec((w.shape[0], n), lambda j, s, c: (0, c[j] * sub + s)),
+                *[pl.BlockSpec((1, tokens, n), lambda j, s, *_, at=at: (at, 0, s)) for _, at in recvs],
             ],
             out_specs=pl.BlockSpec((1, tokens, n), lambda j, s, *_: (j, 0, s)),
         ),
         out_shape=jax.ShapeDtypeStruct((steps, tokens, width), BF),
-        compiler_params=params(40),
-        name="layer_parts",
-    )(cols, att, w)
+        compiler_params=params(BIG),
+        name="layer_step",
+    )(cols, att[0], att[1], w, *[r for r, _ in recvs])
 
 
 def swap(x, axis, bits):
@@ -325,8 +440,8 @@
     return lax.ppermute(x, axis, [(i, i ^ bits) for i in range(n)])
 
 
-def add(a, b):
-    return (a.astype(F32) + b.astype(F32)).astype(BF)
+def after(x, *deps):
+    return lax.optimization_barrier((x, *deps))[0]
 
 
 def shards(queries, token_keys, token_values, out_weight, out_grad):
@@ -339,66 +454,64 @@
     right_perm = [(i, i + 1) for i in range(seq_count - 1)]
     left_perm = [(i + 1, i) for i in range(seq_count - 1)]
 
-    near, far_own, to_left, to_right = pool(token_keys, token_values)
-    from_left = lax.ppermute(to_right, "seq", right_perm)
-    from_right = lax.ppermute(to_left, "seq", left_perm)
-    far = lax.all_gather(far_own, "seq", axis=1, tiled=True)
+    near, far_own, from_left, from_right = [], [], [], []
+    for half in range(HALVES):
+        n, f, to_left, to_right = pool(token_keys, token_values, half)
+        near.append(n)
+        far_own.append(f)
+        from_left.append(lax.ppermute(to_right, "seq", right_perm))
+        from_right.append(lax.ppermute(to_left, "seq", left_perm))
+    far_all = jnp.concatenate(far_own, axis=2)
+    far_all = jnp.broadcast_to(far_all, (seq_count, *far_all.shape))
+    far_all = lax.all_to_all(far_all, "seq", 0, 0, tiled=True)
+    far = jnp.moveaxis(far_all, 0, 1).reshape(2, -1, feats)
     attn_grad = dot(out_grad, out_weight, 1, 1).astype(BF)
-    bias = level_bias(pos, tokens // FB, near.shape[1], far.shape[1], tokens, seq_count)
-    args = (seq_count, pos1, queries, token_keys, token_values, from_left, from_right, near, far, bias)
-    att, attt, lse = forward(*args)
+    bias = level_bias(pos, tokens // FB, near[0].shape[1], far.shape[1], tokens, seq_count)
+
+    att, attt, lse = zip(
+        *[
+            forward(seq_count, pos1, queries, token_keys, token_values, from_left[h], from_right[h], near[h], far, bias, h)
+            for h in range(HALVES)
+        ]
+    )
 
     part = width // seq_count
-    shift = (3, 1)
-    coord = ((pos >> 3) & 3, (pos >> 1) & 3)
-    rows = []
-    for axis, k1, k2 in ROUTE:
-        rel = jnp.array([0, k2, k1, k1 ^ k2], jnp.int32)
-        first = coord[axis] ^ rel
-        second = coord[1 - axis] ^ rel
-        xs, ys = (first[:, None], second[None, :]) if axis == 0 else (second[None, :], first[:, None])
-        rows.append((xs * 4 + ys).reshape(-1))
-    cols = jnp.stack(rows).astype(jnp.int32)
-    send = weight_parts(cols[:, 8:], attt, out_grad, part)
-    got = [swap(s, "seq", k1 << shift[axis]) for s, (axis, k1, k2) in zip(send, ROUTE)]
-    keep = weight_parts(cols[:, :8], attt, out_grad, part)
+    cols = block_order(pos)
+    recv1 = [None] * UNITS
+    for h in range(HALVES):
+        units = list(range(h * UNITS // HALVES, (h + 1) * UNITS // HALVES))
+        out = weight_step(cols, attt, out_grad, part, units, 8, 8, [], False)
+        for u, x in zip(units, out):
+            recv1[u] = (swap(x, "seq", ROUTE[u][1] << SHIFT[ROUTE[u][0]]), False)
 
     c, zl = tp & 1, tp >> 1
-    mine = jnp.stack([zl, zl ^ 1]) * 2
     lwidth = width // tp_count
-    lsend = layer_parts(mine + (c ^ 1), att, out_weight, lwidth)
-    lgot = swap(lsend, "tp", 1)
-    lkeep = layer_parts(mine + c, att, out_weight, lwidth)
-    lgot2 = swap(add(lkeep[1], lgot[1]), "tp", 2)
-    layer_out = (lkeep[0].astype(F32) + lgot[0].astype(F32) + lgot2.astype(F32)).astype(BF)
-
-    dq, gk, gv, sl, sr, gfar = backward(*args, attn_grad, att, lse)
+    lcols = jnp.stack([zl, zl ^ 1]) * 2
+    lgot1 = swap(layer_step(lcols + (c ^ 1), att, out_weight, lwidth, []), "tp", 1)
+
+    dq, gk, gv, sl, sr, gfar = backward(
+        seq_count, pos1, queries, token_keys, token_values, from_left, from_right, near, far, bias, attn_grad, att, lse
+    )
     back_left = lax.ppermute(sr, "seq", right_perm)
     back_right = lax.ppermute(sl, "seq", left_perm)
-    far_sum = lax.psum_scatter(gfar, "seq", scatter_dimension=1, tiled=True)
-
-    nxt = []
-    for k, r, (axis, k1, k2) in zip(keep, got, ROUTE):
-        s2 = add(k[4:], r[4:])
-        nxt.append((add(k[:4], r[:4]), swap(s2, "seq", k2 << shift[axis])))
-    halves = []
-    for p in (0, 2):
-        axis = ROUTE[p][0]
-        a = [add(k, r) for k, r in nxt[p : p + 2]]
-        outs = []
-        for unit, x in zip(ROUTE[p : p + 2], a):
-            _, k1, k2 = unit
-            o = shift[1 - axis]
-            x = add(x[:2], swap(x[2:], "seq", k1 << o))
-            x = add(x[:1], swap(x[1:], "seq", k2 << o))
-            outs.append(x[0])
-        halves.append(jnp.concatenate(outs, axis=1))
-    wsum = jnp.concatenate(halves, axis=1)
+
+    lgot2 = swap(layer_step(lcols[1:] + c, att, out_weight, lwidth, [(lgot1, 1)]), "tp", 2)
+
+    every = list(range(UNITS))
+    out = weight_step(cols, attt, out_grad, part, every, 4, 4, [recv1], False)
+    recv2 = [(swap(x, "seq", ROUTE[u][2] << SHIFT[ROUTE[u][0]]), False) for u, x in enumerate(out)]
+    far_parts = jnp.moveaxis(gfar.reshape(2, seq_count, -1, feats), 1, 0)
+    far_sum = lax.all_to_all(far_parts, "seq", 0, 0, tiled=True).astype(F32).sum(axis=0)
+    layer_out = layer_step(lcols[:1] + c, att, out_weight, lwidth, [(lgot1, 0), (lgot2, 0)])[0]
+
+    got = [recv1, recv2]
+    for step, (start, count) in enumerate(((2, 2), (1, 1))):
+        out = weight_step(cols, attt, out_grad, part, every, start, count, got, True)
+        moved = [swap(x, "seq", SECOND[p][step] << SHIFT[1 - ROUTE[2 * p][0]]) for p, x in enumerate(out)]
+        got.append([(moved[u // 2], True) for u in every])
     zh = pos & 1
-    wkeep = lax.dynamic_index_in_dim(wsum, zh, 0, keepdims=False)
-    wsend = lax.dynamic_index_in_dim(wsum, zh ^ 1, 0, keepdims=False)
-    wgot = swap(wsend, "seq", 1)
-    weight_grad = (wkeep.astype(F32) + wgot.astype(F32)) * (1.0 / math.sqrt(tokens * seq_count))
+    zgot = swap(weight_last(cols, attt, out_grad, part, zh ^ 1, got, None, 1.0, BF), "seq", 1)
+    weight_grad = weight_last(cols, attt, out_grad, part, zh, got, zgot, 1.0 / math.sqrt(tokens * seq_count), F32)
 
     key_grad, value_grad = combine(gk, gv, back_left, back_right, far_sum)
     return layer_out, dq, key_grad, value_grad, weight_grad

time: 568 us -> 232 us (0.41)
  waiting for transfers between devices: 306 us -> 52.5 us
  blocking collectives: 110 us -> 0 us
  Pallas kernels: 53.9 us -> 93.2 us
  starting transfers between devices: 28.6 us -> 58.4 us
  local copies, waits for them, and re-layouts: 31.3 us -> 11.5 us
  between operations: 15.3 us -> 2.24 us
  other arithmetic: 16 us -> 4.24 us
    unnamed x2 -> x0, waiting for transfers between devices: 267 us -> none
    all_gather x1 -> x0, blocking collectives: 110 us -> none  [shards(): far = lax.all_gather(far_own, 'seq', axis=1, tiled=True)]
    pallas_call x6 -> x13, Pallas kernels: 35.8 us -> 72.4 us  [the longest x5 30.8 us: weight_step(): pl.pallas_call(functools.partial(weight_kernel, n, len(recvs) * n, pair_o...]
    unnamed x86 -> x48, local copies, waits for them, and re-layouts: 30.5 us -> 6.75 us
    all_to_all x0 -> x2, starting transfers between devices: none -> 17.7 us  [the longest x1 10.7 us: shards(): far_all = lax.all_to_all(far_all, 'seq', 0, 0, tiled=True)]
    convert_element_type x14 -> x0, other arithmetic: 14.6 us -> none  [the longest x13 11.8 us: add(): return (a.astype(F32) + b.astype(F32)).astype(BF)]
    ppermute x2 -> x4, waiting for transfers between devices: 0.01 us -> 12.3 us  [the longest x2 12.3 us: shards(): from_left.append(lax.ppermute(to_right, 'seq', right_perm))]
    ppermute x2 -> x4, starting transfers between devices: 7.18 us -> 13.9 us  [the longest x2 11.3 us: shards(): from_left.append(lax.ppermute(to_right, 'seq', right_perm))]
  transfers between devices with their start and end apart: 24 -> 23, of which waited for: 12 -> 13; matrix products, arithmetic and copies ran while one was open for 4% -> 7% of each run, Pallas kernels for 6% -> 30%
where the time goes in v2:
time: 232 us; the launch traced here: 230 us
  Pallas kernels  93.2 us (40%)
  starting transfers between devices  58.4 us (25%)
  waiting for transfers between devices  52.5 us (23%)
  local copies, waits for them, and re-layouts  11.5 us (5%)
  matrix products  8.05 us (3%)
  other arithmetic  4.24 us (2%)
    ppermute x15, waiting for transfers between devices, swap(): return lax.ppermute(x, axis, [(i, i ^ bits) for i in range(n)])  39.8 us
    pallas_call x5, Pallas kernels, weight_step(): pl.pallas_call(functools.partial(weight_kernel, n, len(recvs) * n, pair_o...  30.8 us
    ppermute x15, starting transfers between devices, swap(): return lax.ppermute(x, axis, [(i, i ^ bits) for i in range(n)])  19.8 us
    pallas_call x2, Pallas kernels, forward(): pl.pallas_call(functools.partial(fwd_kernel, seq_count), grid_spec=pltpu....  16.3 us
    pallas_call x3, Pallas kernels, layer_step(): pl.pallas_call(layer_kernel, grid_spec=pltpu.PrefetchScalarGridSpec(num_s...  15.2 us
    pallas_call x1, Pallas kernels, backward(): pl.pallas_call(functools.partial(bwd_halves_kernel, seq_count), grid_spec...  14.6 us
    ppermute x2, waiting for transfers between devices, shards(): from_left.append(lax.ppermute(to_right, 'seq', right_perm))  12.3 us
    ppermute x2, starting transfers between devices, shards(): from_left.append(lax.ppermute(to_right, 'seq', right_perm))  11.3 us
  transfers between devices with their start and end apart: 23, of which 13 were waited for; matrix products, arithmetic and copies ran while one was open for 7% of the time, Pallas kernels for 30%

profile of v2, /device:TPU:0, one launch (start us, length us, event | category | flops | bytes accessed | tf_op | source)
XLA Modules:
  0.0 230.2 jit_solution(13822786734595573117)
XLA Ops:
  0.6 2.4 %pool.2 = (bf16[2,32,512]{2,1,0:T(8,128)(2,1)}, bf16[2,2,512]{2,1,0:T(2,128)(2,1)}, bf16[2,160,512]{2,1,0:T(8,128)(2,1)}, bf16[2,160,512]{2,1,0:T(8,128)(2,1)}) custom-call(bf16[512,1024]{1,0:T(8,128)(2,1)} %k_ref.9, bf16[512,1024]{1,0:T(8,128)(2,1)} %v_ref.9), custom_call_target="tpu_custom_call" | custom-call | tf_op jit(solution)/shard_map/pool/pallas_call | solution.py:54
  3.0 2.4 %pool.3 = (bf16[2,32,512]{2,1,0:T(8,128)(2,1)}, bf16[2,2,512]{2,1,0:T(2,128)(2,1)}, bf16[2,160,512]{2,1,0:T(8,128)(2,1)}, bf16[2,160,512]{2,1,0:T(8,128)(2,1)}) custom-call(bf16[512,1024]{1,0:T(8,128)(2,1)} %k_ref.9, bf16[512,1024]{1,0:T(8,128)(2,1)} %v_ref.9), custom_call_target="tpu_custom_call" | custom-call | tf_op jit(solution)/shard_map/pool/pallas_call | solution.py:54
  6.9 10.7 %all-to-all-start = ((bf16[32,2,2,1024]{3,2,1,0:T(2,128)(2,1)}), bf16[32,2,2,1024]{3,2,1,0:T(2,128)(2,1)S(1)}, u32[]{:S(2)}, u32[]{:S(2)}) async-start(bf16[32,2,2,1024]{3,2,1,0:T(2,128)(2,1)} %broadcast_in_dim.29), calls=%async_computation | async-start | bytes 524288 | tf_op jit(solution)/shard_map/all_to_all | solution.py:466
  17.6 5.2 %collective-permute-start.2 = (bf16[2,160,512]{2,1,0:T(8,128)(2,1)}, bf16[2,160,512]{2,1,0:T(8,128)(2,1)S(1)}, u32[]{:S(2)}, u32[]{:S(2)}) collective-permute-start(bf16[2,160,512]{2,1,0:T(8,128)(2,1)} %get-tuple-element.45), channel_id=1, source_target_pairs={{0,4},{4,8},{8,12},{12,16},{16,20},{20,24},{24,28},{28,32},{32,36}... | collective-permute-start | bytes 983048 | tf_op jit(solution)/shard_map/ppermute | solution.py:462
  24.1 6.1 %collective-permute-start = (bf16[2,160,512]{2,1,0:T(8,128)(2,1)}, bf16[2,160,512]{2,1,0:T(8,128)(2,1)S(1)}, u32[]{:S(2)}, u32[]{:S(2)}) collective-permute-start(bf16[2,160,512]{2,1,0:T(8,128)(2,1)} %get-tuple-element.39), channel_id=1, source_target_pairs={{0,4},{4,8},{8,12},{12,16},{16,20},{20,24},{24,28},{28,32},{32,36}... | collective-permute-start | bytes 983048 | tf_op jit(solution)/shard_map/ppermute | solution.py:462
  33.3 12.3 %collective-permute-done.2.left_ref.refs_1_ = bf16[2,160,512]{2,1,0:T(8,128)(2,1)S(1)} collective-permute-done((bf16[2,160,512]{2,1,0:T(8,128)(2,1)}, bf16[2,160,512]{2,1,0:T(8,128)(2,1)S(1)}, u32[]{:S(2)}, u32[]{:S(2)}) %collective-permute-start.2) | collective-permute-done | bytes 327712 | tf_op jit(solution)/shard_map/ppermute | solution.py:462
  46.6 8.2 %attend.3 = (bf16[512,512]{1,0:T(8,128)(2,1)}, bf16[512,512]{1,0:T(8,128)(2,1)}, f32[4,1,512]{2,1,0:T(1,128)}) custom-call(s32[1]{0:T(128)} %bitcast.3.pos_ref, bf16[512,1024]{1,0:T(8,128)(2,1)} %q_ref.5, bf16[512,1024]{1,0:T(8,128)(2,1)} %k_ref.9, bf16[512,1024]{1,0:T(8,128)(2,1)} %v_ref.9, bf16[2,160,512]{2,1,0:T(8,128)(2,1)} %copy-done.13, ...), custom_call_target="tpu_custom_call" | custom-call | tf_op jit(solution)/shard_map/attend/pallas_call | solution.py:177
  55.6 8.2 %attend.2 = (bf16[512,512]{1,0:T(8,128)(2,1)}, bf16[512,512]{1,0:T(8,128)(2,1)}, f32[4,1,512]{2,1,0:T(1,128)}) custom-call(s32[1]{0:T(128)} %bitcast.3.pos_ref, bf16[512,1024]{1,0:T(8,128)(2,1)} %q_ref.5, bf16[512,1024]{1,0:T(8,128)(2,1)} %k_ref.9, bf16[512,1024]{1,0:T(8,128)(2,1)} %v_ref.9, bf16[2,160,512]{2,1,0:T(8,128)(2,1)} %copy-done.15, ...), custom_call_target="tpu_custom_call" | custom-call | tf_op jit(solution)/shard_map/attend/pallas_call | solution.py:177
  63.8 6.9 %layer_step.3 = bf16[2,512,1024]{2,1,0:T(8,128)(2,1)} custom-call(s32[2]{0:T(128)} %get-tuple-element.75.cols_ref, bf16[512,512]{1,0:T(8,128)(2,1)} %get-tuple-element.44.a0_ref.refs_6_, bf16[512,512]{1,0:T(8,128)(2,1)} %get-tuple-element.48.a1_ref.refs_7_, bf16[1024,4096]{1,0:T(8,128)(2,1)} %w_ref.5), custom_call_target="tpu_custom_call" | custom-call | tf_op jit(solution)/shard_map/layer_step/pallas_call | solution.py:419
  71.7 8.0 %weight_step.6 = (bf16[8,2,256,128]{3,2,1,0:T(8,128)(2,1)}, bf16[8,2,256,128]{3,2,1,0:T(8,128)(2,1)}) custom-call(s32[4,16]{1,0:T(4,128)} %pad_add_fusion.cols_ref, bf16[512,512]{1,0:T(8,128)(2,1)} %get-tuple-element.60.refs_0_.refs_1_.refs_2_.refs_3_, bf16[512,512]{1,0:T(8,128)(2,1)} %get-tuple-element.60.refs_0_.refs_1_.refs_2_.refs_3_, ...), custom_call_target="tpu_custom_call" | custom-call | tf_op jit(solution)/shard_map/weight_step/pallas_call | solution.py:346
  79.7 2.8 %collective-permute-start.10 = (bf16[8,2,256,128]{3,2,1,0:T(8,128)(2,1)}, bf16[8,2,256,128]{3,2,1,0:T(8,128)(2,1)S(1)}, u32[]{:S(2)}, u32[]{:S(2)}) collective-permute-start(bf16[8,2,256,128]{3,2,1,0:T(8,128)(2,1)} %get-tuple-element.63), channel_id=1, source_target_pairs={{0,8},{4,12},{8,0},{12,4},{16,24},{20,28},{24,16},{28,20},{32,40},... | collective-permute-start | bytes 3145736 | tf_op jit(solution)/shard_map/ppermute | solution.py:440
  84.2 8.0 %weight_step.5 = (bf16[8,2,256,128]{3,2,1,0:T(8,128)(2,1)}, bf16[8,2,256,128]{3,2,1,0:T(8,128)(2,1)}) custom-call(s32[4,16]{1,0:T(4,128)} %pad_add_fusion.cols_ref, bf16[512,512]{1,0:T(8,128)(2,1)} %get-tuple-element.59.refs_0_.refs_1_, bf16[512,512]{1,0:T(8,128)(2,1)} %get-tuple-element.59.refs_0_.refs_1_, bf16[512,4096]{1,0:T(8,128)(2,1)} %refs_7_.9, ...), custom_call_target="tpu_custom_call" | custom-call | tf_op jit(solution)/shard_map/weight_step/pallas_call | solution.py:346
  94.7 11.9 %collective-permute-done.10.refs_10_ = bf16[8,2,256,128]{3,2,1,0:T(8,128)(2,1)S(1)} collective-permute-done((bf16[8,2,256,128]{3,2,1,0:T(8,128)(2,1)}, bf16[8,2,256,128]{3,2,1,0:T(8,128)(2,1)S(1)}, u32[]{:S(2)}, u32[]{:S(2)}) %collective-permute-start.10) | collective-permute-done | bytes 1048608 | tf_op jit(solution)/shard_map/ppermute | solution.py:440
  106.5 2.7 %collective-permute-done.11.refs_11_ = bf16[8,2,256,128]{3,2,1,0:T(8,128)(2,1)S(1)} collective-permute-done((bf16[8,2,256,128]{3,2,1,0:T(8,128)(2,1)}, bf16[8,2,256,128]{3,2,1,0:T(8,128)(2,1)S(1)}, u32[]{:S(2)}, u32[]{:S(2)}) %collective-permute-start.11) | collective-permute-done | bytes 1048608 | tf_op jit(solution)/shard_map/ppermute | solution.py:440
  109.2 8.1 %collective-permute-done.8.refs_8_ = bf16[8,2,256,128]{3,2,1,0:T(8,128)(2,1)S(1)} collective-permute-done((bf16[8,2,256,128]{3,2,1,0:T(8,128)(2,1)}, bf16[8,2,256,128]{3,2,1,0:T(8,128)(2,1)S(1)}, u32[]{:S(2)}, u32[]{:S(2)}) %collective-permute-start.8) | collective-permute-done | bytes 1048608 | tf_op jit(solution)/shard_map/ppermute | solution.py:440
  117.3 1.8 collective-permute-done.9.refs_9_
  120.1 6.5 %weight_step.7 = (bf16[4,2,256,128]{3,2,1,0:T(8,128)(2,1)}, bf16[4,2,256,128]{3,2,1,0:T(8,128)(2,1)}, bf16[4,2,256,128]{3,2,1,0:T(8,128)(2,1)}, bf16[4,2,256,128]{3,2,1,0:T(8,128)(2,1)}) custom-call(s32[4,16]{1,0:T(4,128)} %pad_add_fusion.cols_ref, bf16[512,512]{1,0:T(8,128)(2,1)} %get-tuple-element.59.refs_0_.refs_1_, ...), custom_call_target="tpu_custom_call" | custom-call | tf_op jit(solution)/shard_map/weight_step/pallas_call | solution.py:346
  128.3 2.2 collective-permute-start.14
  132.1 8.5 %collective-permute-done.12.refs_12_ = bf16[4,2,256,128]{3,2,1,0:T(8,128)(2,1)S(1)} collective-permute-done((bf16[4,2,256,128]{3,2,1,0:T(8,128)(2,1)}, bf16[4,2,256,128]{3,2,1,0:T(8,128)(2,1)S(1)}, u32[]{:S(2)}, u32[]{:S(2)}) %collective-permute-start.12) | collective-permute-done | bytes 524320 | tf_op jit(solution)/shard_map/ppermute | solution.py:440
  143.8 4.4 %weight_step.8 = (bf16[2,2,512,128]{3,2,1,0:T(8,128)(2,1)}, bf16[2,2,512,128]{3,2,1,0:T(8,128)(2,1)}) custom-call(s32[4,16]{1,0:T(4,128)} %pad_add_fusion.cols_ref, bf16[512,512]{1,0:T(8,128)(2,1)} %get-tuple-element.59.refs_0_.refs_1_, bf16[512,512]{1,0:T(8,128)(2,1)} %get-tuple-element.59.refs_0_.refs_1_, ...), custom_call_target="tpu_custom_call" | custom-call | tf_op jit(solution)/shard_map/weight_step/pallas_call | solution.py:346
  150.1 3.9 %layer_step.4 = bf16[1,512,1024]{2,1,0:T(8,128)(2,1)} custom-call(s32[1]{0:T(128)S(6)} %add.152.cols_ref, bf16[512,512]{1,0:T(8,128)(2,1)} %get-tuple-element.44.a0_ref.refs_6_, bf16[512,512]{1,0:T(8,128)(2,1)} %get-tuple-element.48.a1_ref.refs_7_, bf16[1024,4096]{1,0:T(8,128)(2,1)} %w_ref.5, bf16[2,512,1024]{2,1,0:T(8,128)(2,1)} %collective-permute-done.4.refs_0_), custom_call_target="tpu_custom_call" | custom-call | tf_op jit(solution)/shard_map/layer_step/pallas_call | solution.py:419
  155.0 8.0 %convolution_convert_fusion.refs_12_ = bf16[512,1024]{1,0:T(8,128)(2,1)} fusion(bf16[512,4096]{1,0:T(8,128)(2,1)S(1)} %copy-done, bf16[1024,4096]{1,0:T(8,128)(2,1)} %w_ref.5), kind=kOutput, calls=%fused_computation | convolution fusion | flops 4295491584 | bytes 13631488 | tf_op jit(solution)/shard_map/dot_general | solution.py:25
  163.1 14.6 %attend_grad.1 = (bf16[512,1024]{1,0:T(8,128)(2,1)}, f32[512,1024]{1,0:T(8,128)}, f32[512,1024]{1,0:T(8,128)}, bf16[2,160,1024]{2,1,0:T(8,128)(2,1)}, bf16[2,160...) custom-call(s32[1]{0:T(128)} %bitcast.3.pos_ref, bf16[512,1024]{1,0:T(8,128)(2,1)} %q_ref.5, bf16[512,1024]{1,0:T(8,128)(2,1)} %k_ref.9, ...), custom_call_target="tpu_custom_call" | custom-call | tf_op jit(solution)/shard_map/attend_grad/pallas_call | solution.py:228
  177.7 5.6 %collective-permute-start.6 = (bf16[2,160,1024]{2,1,0:T(8,128)(2,1)}, bf16[2,160,1024]{2,1,0:T(8,128)(2,1)S(1)}, u32[]{:S(2)}, u32[]{:S(2)}) collective-permute-start(bf16[2,160,1024]{2,1,0:T(8,128)(2,1)} %get-tuple-element.54), channel_id=1, source_target_pairs={{0,4},{4,8},{8,12},{12,16},{16,20},{20,24},{24,28},{28,32},{32,36}... | collective-permute-start | bytes 1966088 | tf_op jit(solution)/shard_map/ppermute | solution.py:495
  186.3 3.9 %weight_step.9 = (bf16[1,2,512,128]{3,2,1,0:T(8,128)(2,1)}, bf16[1,2,512,128]{3,2,1,0:T(8,128)(2,1)}) custom-call(s32[4,16]{1,0:T(4,128)} %pad_add_fusion.cols_ref, bf16[512,512]{1,0:T(8,128)(2,1)} %get-tuple-element.59.refs_0_.refs_1_, bf16[512,512]{1,0:T(8,128)(2,1)} %get-tuple-element.59.refs_0_.refs_1_, ...), custom_call_target="tpu_custom_call" | custom-call | tf_op jit(solution)/shard_map/weight_step/pallas_call | solution.py:346
  190.2 3.5 %collective-permute-start.18 = (bf16[1,2,512,128]{3,2,1,0:T(8,128)(2,1)}, bf16[1,2,512,128]{3,2,1,0:T(8,128)(2,1)S(1)}, u32[]{:S(2)}, u32[]{:S(2)}) collective-permute-start(bf16[1,2,512,128]{3,2,1,0:T(8,128)(2,1)} %get-tuple-element.71), channel_id=1, source_target_pairs={{0,24},{4,28},{8,16},{12,20},{16,8},{20,12},{24,0},{28,4},{32,56},... | collective-permute-start | bytes 786440 | tf_op jit(solution)/shard_map/ppermute | solution.py:440
  196.3 7.0 %all-to-all-start.1 = ((bf16[32,2,2,1024]{3,2,1,0:T(2,128)(2,1)}), bf16[32,2,2,1024]{3,2,1,0:T(2,128)(2,1)S(1)}, u32[]{:S(2)}, u32[]{:S(2)}) async-start(bf16[32,2,2,1024]{3,2,1,0:T(2,128)(2,1)} %bitcast.12), calls=%async_computation.1 | async-start | bytes 524288 | tf_op jit(solution)/shard_map/all_to_all | solution.py:504
  204.2 2.7 %collective-permute-done.18.refs_20_.refs_21_ = bf16[1,2,512,128]{3,2,1,0:T(8,128)(2,1)S(1)} collective-permute-done((bf16[1,2,512,128]{3,2,1,0:T(8,128)(2,1)}, bf16[1,2,512,128]{3,2,1,0:T(8,128)(2,1)S(1)}, u32[]{:S(2)}, u32[]{:S(2)}) %collective-permute-start.18) | collective-permute-done | bytes 262176 | tf_op jit(solution)/shard_map/ppermute | solution.py:440
  208.5 3.4 %weight_last.2 = bf16[1024,128]{1,0:T(8,128)(2,1)} custom-call(s32[5]{0:T(128)} %pad_add_fusion.2.cols_ref, bf16[512,512]{1,0:T(8,128)(2,1)} %get-tuple-element.59.refs_0_.refs_1_, bf16[512,512]{1,0:T(8,128)(2,1)} %get-tuple-element.59.refs_0_.refs_1_, bf16[512,512]{1,0:T(8,128)(2,1)} %get-tuple-element.60.refs_0_.refs_1_.refs_2_.refs_3_, ...), custom_call_target="tpu_custom_call" | custom-call | tf_op jit(solution)/shard_map/weight_last/pallas_call | solution.py:396
  216.0 4.5 %combine.1 = (bf16[512,1024]{1,0:T(8,128)(2,1)}, bf16[512,1024]{1,0:T(8,128)(2,1)}) custom-call(f32[512,1024]{1,0:T(8,128)} %get-tuple-element.52.gk_ref, f32[512,1024]{1,0:T(8,128)} %get-tuple-element.53.gv_ref, bf16[2,160,1024]{2,1,0:T(8,128)(2,1)} %copy-done.17, bf16[2,160,1024]{2,1,0:T(8,128)(2,1)} %copy-done.18, f32[2,2,1024]{2,1,0:T(2,128)} %convert_reduce_fusion.far_ref), custom_call_target="tpu_custom_call" | custom-call | tf_op jit(solution)/shard_map/combine/pallas_call | solution.py:278
  222.1 3.7 %weight_last.3 = f32[1024,128]{1,0:T(8,128)} custom-call(s32[5]{0:T(128)} %pad_add_fusion.1.cols_ref, bf16[512,512]{1,0:T(8,128)(2,1)} %get-tuple-element.59.refs_0_.refs_1_, bf16[512,512]{1,0:T(8,128)(2,1)} %get-tuple-element.59.refs_0_.refs_1_, bf16[512,512]{1,0:T(8,128)(2,1)} %get-tuple-element.60.refs_0_.refs_1_.refs_2_.refs_3_, ...), custom_call_target="tpu_custom_call" | custom-call | tf_op jit(solution)/shard_map/weight_last/pallas_call | solution.py:396
  225.8 4.4 %layer_step.5 = bf16[1,512,1024]{2,1,0:T(8,128)(2,1)} custom-call(s32[1]{0:T(128)S(6)} %add.149.cols_ref, bf16[512,512]{1,0:T(8,128)(2,1)} %get-tuple-element.44.a0_ref.refs_6_, bf16[512,512]{1,0:T(8,128)(2,1)} %get-tuple-element.48.a1_ref.refs_7_, bf16[1024,4096]{1,0:T(8,128)(2,1)} %w_ref.5, bf16[2,512,1024]{2,1,0:T(8,128)(2,1)} %collective-permute-done.4.refs_0_, ...), custom_call_target="tpu_custom_call" | custom-call | tf_op jit(solution)/shard_map/layer_step/pallas_call | solution.py:419
  (105 shorter events, 35.7 us)
Async XLA Ops:
  6.9 25.4 %all-to-all-start = ((bf16[32,2,2,1024]{3,2,1,0:T(2,128)(2,1)}), bf16[32,2,2,1024]{3,2,1,0:T(2,128)(2,1)S(1)}, u32[]{:S(2)}, u32[]{:S(2)}) async-start(bf16[32,2,2,1024]{3,2,1,0:T(2,128)(2,1)} %broadcast_in_dim.29), calls=%async_computation | async-start | bytes 524288 | tf_op jit(solution)/shard_map/all_to_all | solution.py:466
  17.6 28.0 %collective-permute-start.2 = (bf16[2,160,512]{2,1,0:T(8,128)(2,1)}, bf16[2,160,512]{2,1,0:T(8,128)(2,1)S(1)}, u32[]{:S(2)}, u32[]{:S(2)}) collective-permute-start(bf16[2,160,512]{2,1,0:T(8,128)(2,1)} %get-tuple-element.45), channel_id=1, source_target_pairs={{0,4},{4,8},{8,12},{12,16},{16,20},{20,24},{24,28},{28,32},{32,36}... | collective-permute-start | bytes 983048 | tf_op jit(solution)/shard_map/ppermute | solution.py:462
  22.8 22.8 %collective-permute-start.3 = (bf16[2,160,512]{2,1,0:T(8,128)(2,1)}, bf16[2,160,512]{2,1,0:T(8,128)(2,1)S(1)}, u32[]{:S(2)}, u32[]{:S(2)}) collective-permute-start(bf16[2,160,512]{2,1,0:T(8,128)(2,1)} %get-tuple-element.46), channel_id=1, source_target_pairs={{4,0},{8,4},{12,8},{16,12},{20,16},{24,20},{28,24},{32,28},{36,32}... | collective-permute-start | bytes 983048 | tf_op jit(solution)/shard_map/ppermute | solution.py:463
  24.1 30.6 %collective-permute-start = (bf16[2,160,512]{2,1,0:T(8,128)(2,1)}, bf16[2,160,512]{2,1,0:T(8,128)(2,1)S(1)}, u32[]{:S(2)}, u32[]{:S(2)}) collective-permute-start(bf16[2,160,512]{2,1,0:T(8,128)(2,1)} %get-tuple-element.39), channel_id=1, source_target_pairs={{0,4},{4,8},{8,12},{12,16},{16,20},{20,24},{24,28},{28,32},{32,36}... | collective-permute-start | bytes 983048 | tf_op jit(solution)/shard_map/ppermute | solution.py:462
  30.2 24.6 %collective-permute-start.1 = (bf16[2,160,512]{2,1,0:T(8,128)(2,1)}, bf16[2,160,512]{2,1,0:T(8,128)(2,1)S(1)}, u32[]{:S(2)}, u32[]{:S(2)}) collective-permute-start(bf16[2,160,512]{2,1,0:T(8,128)(2,1)} %get-tuple-element.40), channel_id=1, source_target_pairs={{4,0},{8,4},{12,8},{16,12},{20,16},{24,20},{28,24},{32,28},{36,32}... | collective-permute-start | bytes 983048 | tf_op jit(solution)/shard_map/ppermute | solution.py:463
  63.8 6.9 %copy-start.22 = (s32[4]{0:T(128)S(1)}, s32[4]{0:T(128)}, u32[]{:S(2)}) copy-start(s32[4]{0:T(128)} %constant.87.clone) | copy-start | bytes 52
  63.8 6.9 %copy-start.23 = (s32[4]{0:T(128)S(1)}, s32[4]{0:T(128)}, u32[]{:S(2)}) copy-start(s32[4]{0:T(128)} %constant.88.clone) | copy-start | bytes 52
  70.7 79.4 %collective-permute-start.4 = (bf16[2,512,1024]{2,1,0:T(8,128)(2,1)}, bf16[2,512,1024]{2,1,0:T(8,128)(2,1)}, u32[]{:S(2)}, u32[]{:S(2)}) collective-permute-start(bf16[2,512,1024]{2,1,0:T(8,128)(2,1)} %layer_step.3), channel_id=1, source_target_pairs={{0,1},{1,0},{2,3},{3,2},{4,5},{5,4},{6,7},{7,6},{8,9},{9,8},{10,11... | collective-permute-start | bytes 6291464 | tf_op jit(solution)/shard_map/ppermute | solution.py:440
  79.7 26.8 %collective-permute-start.10 = (bf16[8,2,256,128]{3,2,1,0:T(8,128)(2,1)}, bf16[8,2,256,128]{3,2,1,0:T(8,128)(2,1)S(1)}, u32[]{:S(2)}, u32[]{:S(2)}) collective-permute-start(bf16[8,2,256,128]{3,2,1,0:T(8,128)(2,1)} %get-tuple-element.63), channel_id=1, source_target_pairs={{0,8},{4,12},{8,0},{12,4},{16,24},{20,28},{24,16},{28,20},{32,40},... | collective-permute-start | bytes 3145736 | tf_op jit(solution)/shard_map/ppermute | solution.py:440
  82.5 26.7 %collective-permute-start.11 = (bf16[8,2,256,128]{3,2,1,0:T(8,128)(2,1)}, bf16[8,2,256,128]{3,2,1,0:T(8,128)(2,1)S(1)}, u32[]{:S(2)}, u32[]{:S(2)}) collective-permute-start(bf16[8,2,256,128]{3,2,1,0:T(8,128)(2,1)} %get-tuple-element.64), channel_id=1, source_target_pairs={{0,24},{4,28},{8,16},{12,20},{16,8},{20,12},{24,0},{28,4},{32,56},... | collective-permute-start | bytes 3145736 | tf_op jit(solution)/shard_map/ppermute | solution.py:440
  92.2 25.1 %collective-permute-start.8 = (bf16[8,2,256,128]{3,2,1,0:T(8,128)(2,1)}, bf16[8,2,256,128]{3,2,1,0:T(8,128)(2,1)S(1)}, u32[]{:S(2)}, u32[]{:S(2)}) collective-permute-start(bf16[8,2,256,128]{3,2,1,0:T(8,128)(2,1)} %get-tuple-element.61), channel_id=1, source_target_pairs={{0,32},{4,36},{8,40},{12,44},{16,48},{20,52},{24,56},{28,60},{32,0... | collective-permute-start | bytes 3145736 | tf_op jit(solution)/shard_map/ppermute | solution.py:440
  93.1 26.1 %collective-permute-start.9 = (bf16[8,2,256,128]{3,2,1,0:T(8,128)(2,1)}, bf16[8,2,256,128]{3,2,1,0:T(8,128)(2,1)S(1)}, u32[]{:S(2)}, u32[]{:S(2)}) collective-permute-start(bf16[8,2,256,128]{3,2,1,0:T(8,128)(2,1)} %get-tuple-element.62), channel_id=1, source_target_pairs={{0,96},{4,100},{8,104},{12,108},{16,112},{20,116},{24,120},{28,124... | collective-permute-start | bytes 3145736 | tf_op jit(solution)/shard_map/ppermute | solution.py:440
  106.5 12.6 %copy-start.1 = (bf16[8,2,256,128]{3,2,1,0:T(8,128)(2,1)}, bf16[8,2,256,128]{3,2,1,0:T(8,128)(2,1)S(1)}, u32[]{:S(2)}) copy-start(bf16[8,2,256,128]{3,2,1,0:T(8,128)(2,1)S(1)} %collective-permute-done.10.refs_10_) | copy-start | bytes 3145732
  109.2 9.9 %copy-start.2 = (bf16[8,2,256,128]{3,2,1,0:T(8,128)(2,1)}, bf16[8,2,256,128]{3,2,1,0:T(8,128)(2,1)S(1)}, u32[]{:S(2)}) copy-start(bf16[8,2,256,128]{3,2,1,0:T(8,128)(2,1)S(1)} %collective-permute-done.11.refs_11_) | copy-start | bytes 3145732
  126.6 14.0 %collective-permute-start.12 = (bf16[4,2,256,128]{3,2,1,0:T(8,128)(2,1)}, bf16[4,2,256,128]{3,2,1,0:T(8,128)(2,1)S(1)}, u32[]{:S(2)}, u32[]{:S(2)}) collective-permute-start(bf16[4,2,256,128]{3,2,1,0:T(8,128)(2,1)} %get-tuple-element.65), channel_id=1, source_target_pairs={{0,96},{4,100},{8,104},{12,108},{16,112},{20,116},{24,120},{28,124... | collective-permute-start | bytes 1572872 | tf_op jit(solution)/shard_map/ppermute | solution.py:440
  128.3 12.4 %collective-permute-start.13 = (bf16[4,2,256,128]{3,2,1,0:T(8,128)(2,1)}, bf16[4,2,256,128]{3,2,1,0:T(8,128)(2,1)S(1)}, u32[]{:S(2)}, u32[]{:S(2)}) collective-permute-start(bf16[4,2,256,128]{3,2,1,0:T(8,128)(2,1)} %get-tuple-element.66), channel_id=1, source_target_pairs={{0,32},{4,36},{8,40},{12,44},{16,48},{20,52},{24,56},{28,60},{32,0... | collective-permute-start | bytes 1572872 | tf_op jit(solution)/shard_map/ppermute | solution.py:440
  128.3 13.7 %collective-permute-start.14 = (bf16[4,2,256,128]{3,2,1,0:T(8,128)(2,1)}, bf16[4,2,256,128]{3,2,1,0:T(8,128)(2,1)S(1)}, u32[]{:S(2)}, u32[]{:S(2)}) collective-permute-start(bf16[4,2,256,128]{3,2,1,0:T(8,128)(2,1)} %get-tuple-element.67), channel_id=1, source_target_pairs={{0,24},{4,28},{8,16},{12,20},{16,8},{20,12},{24,0},{28,4},{32,56},... | collective-permute-start | bytes 1572872 | tf_op jit(solution)/shard_map/ppermute | solution.py:440
  130.5 12.5 %collective-permute-start.15 = (bf16[4,2,256,128]{3,2,1,0:T(8,128)(2,1)}, bf16[4,2,256,128]{3,2,1,0:T(8,128)(2,1)S(1)}, u32[]{:S(2)}, u32[]{:S(2)}) collective-permute-start(bf16[4,2,256,128]{3,2,1,0:T(8,128)(2,1)} %get-tuple-element.68), channel_id=1, source_target_pairs={{0,8},{4,12},{8,0},{12,4},{16,24},{20,28},{24,16},{28,20},{32,40},... | collective-permute-start | bytes 1572872 | tf_op jit(solution)/shard_map/ppermute | solution.py:440
  140.6 2.4 %copy-start.7 = (bf16[4,2,256,128]{3,2,1,0:T(8,128)(2,1)}, bf16[4,2,256,128]{3,2,1,0:T(8,128)(2,1)S(1)}, u32[]{:S(2)}) copy-start(bf16[4,2,256,128]{3,2,1,0:T(8,128)(2,1)S(1)} %collective-permute-done.12.refs_12_) | copy-start | bytes 1572868
  140.7 2.3 copy-start.8
  148.2 36.5 %collective-permute-start.16 = (bf16[2,2,512,128]{3,2,1,0:T(8,128)(2,1)}, bf16[2,2,512,128]{3,2,1,0:T(8,128)(2,1)S(1)}, u32[]{:S(2)}, u32[]{:S(2)}) collective-permute-start(bf16[2,2,512,128]{3,2,1,0:T(8,128)(2,1)} %get-tuple-element.69), channel_id=1, source_target_pairs={{0,8},{4,12},{8,0},{12,4},{16,24},{20,28},{24,16},{28,20},{32,40},... | collective-permute-start | bytes 1572872 | tf_op jit(solution)/shard_map/ppermute | solution.py:440
  148.6 6.4 %copy-start = (bf16[512,4096]{1,0:T(8,128)(2,1)S(1)}, bf16[512,4096]{1,0:T(8,128)(2,1)}, u32[]{:S(2)}) copy-start(bf16[512,4096]{1,0:T(8,128)(2,1)} %refs_7_.9) | copy-start | bytes 12582916
  148.6 36.1 %collective-permute-start.17 = (bf16[2,2,512,128]{3,2,1,0:T(8,128)(2,1)}, bf16[2,2,512,128]{3,2,1,0:T(8,128)(2,1)S(1)}, u32[]{:S(2)}, u32[]{:S(2)}) collective-permute-start(bf16[2,2,512,128]{3,2,1,0:T(8,128)(2,1)} %get-tuple-element.70), channel_id=1, source_target_pairs={{0,96},{4,100},{8,104},{12,108},{16,112},{20,116},{24,120},{28,124... | collective-permute-start | bytes 1572872 | tf_op jit(solution)/shard_map/ppermute | solution.py:440
  154.0 71.8 %collective-permute-start.5 = (bf16[1,512,1024]{2,1,0:T(8,128)(2,1)}, bf16[1,512,1024]{2,1,0:T(8,128)(2,1)}, u32[]{:S(2)}, u32[]{:S(2)}) collective-permute-start(bf16[1,512,1024]{2,1,0:T(8,128)(2,1)} %layer_step.4), channel_id=1, source_target_pairs={{0,2},{1,3},{2,0},{3,1},{4,6},{5,7},{6,4},{7,5},{8,10},{9,11},{10,... | collective-permute-start | bytes 3145736 | tf_op jit(solution)/shard_map/ppermute | solution.py:440
  177.7 37.2 %collective-permute-start.6 = (bf16[2,160,1024]{2,1,0:T(8,128)(2,1)}, bf16[2,160,1024]{2,1,0:T(8,128)(2,1)S(1)}, u32[]{:S(2)}, u32[]{:S(2)}) collective-permute-start(bf16[2,160,1024]{2,1,0:T(8,128)(2,1)} %get-tuple-element.54), channel_id=1, source_target_pairs={{0,4},{4,8},{8,12},{12,16},{16,20},{20,24},{24,28},{28,32},{32,36}... | collective-permute-start | bytes 1966088 | tf_op jit(solution)/shard_map/ppermute | solution.py:495
  183.3 12.1 %copy-start.20 = (bf16[2,64,1024]{2,1,0:T(8,128)(2,1)S(1)}, bf16[2,64,1024]{2,1,0:T(8,128)(2,1)}, u32[]{:S(2)}) copy-start(bf16[2,64,1024]{2,1,0:T(8,128)(2,1)} %get-tuple-element.56) | copy-start | bytes 786436
  183.3 20.1 %copy-start.21 = (s32[4,16]{1,0:T(4,128)S(1)}, s32[4,16]{1,0:T(4,128)}, u32[]{:S(2)}) copy-start(s32[4,16]{1,0:T(4,128)} %pad_add_fusion.cols_ref) | copy-start | bytes 772
  183.3 31.6 %collective-permute-start.7 = (bf16[2,160,1024]{2,1,0:T(8,128)(2,1)}, bf16[2,160,1024]{2,1,0:T(8,128)(2,1)S(1)}, u32[]{:S(2)}, u32[]{:S(2)}) collective-permute-start(bf16[2,160,1024]{2,1,0:T(8,128)(2,1)} %get-tuple-element.55), channel_id=1, source_target_pairs={{4,0},{8,4},{12,8},{16,12},{20,16},{24,20},{28,24},{32,28},{36,32}... | collective-permute-start | bytes 1966088 | tf_op jit(solution)/shard_map/ppermute | solution.py:496
  190.2 16.6 %collective-permute-start.18 = (bf16[1,2,512,128]{3,2,1,0:T(8,128)(2,1)}, bf16[1,2,512,128]{3,2,1,0:T(8,128)(2,1)S(1)}, u32[]{:S(2)}, u32[]{:S(2)}) collective-permute-start(bf16[1,2,512,128]{3,2,1,0:T(8,128)(2,1)} %get-tuple-element.71), channel_id=1, source_target_pairs={{0,24},{4,28},{8,16},{12,20},{16,8},{20,12},{24,0},{28,4},{32,56},... | collective-permute-start | bytes 786440 | tf_op jit(solution)/shard_map/ppermute | solution.py:440
  193.7 14.1 %collective-permute-start.19 = (bf16[1,2,512,128]{3,2,1,0:T(8,128)(2,1)}, bf16[1,2,512,128]{3,2,1,0:T(8,128)(2,1)S(1)}, u32[]{:S(2)}, u32[]{:S(2)}) collective-permute-start(bf16[1,2,512,128]{3,2,1,0:T(8,128)(2,1)} %get-tuple-element.72), channel_id=1, source_target_pairs={{0,32},{4,36},{8,40},{12,44},{16,48},{20,52},{24,56},{28,60},{32,0... | collective-permute-start | bytes 786440 | tf_op jit(solution)/shard_map/ppermute | solution.py:440
  196.3 17.7 %all-to-all-start.1 = ((bf16[32,2,2,1024]{3,2,1,0:T(2,128)(2,1)}), bf16[32,2,2,1024]{3,2,1,0:T(2,128)(2,1)S(1)}, u32[]{:S(2)}, u32[]{:S(2)}) async-start(bf16[32,2,2,1024]{3,2,1,0:T(2,128)(2,1)} %bitcast.12), calls=%async_computation.1 | async-start | bytes 524288 | tf_op jit(solution)/shard_map/all_to_all | solution.py:504
  211.9 9.5 %collective-permute-start.20 = (bf16[1024,128]{1,0:T(8,128)(2,1)}, bf16[1024,128]{1,0:T(8,128)(2,1)S(1)}, u32[]{:S(2)}, u32[]{:S(2)}) collective-permute-start(bf16[1024,128]{1,0:T(8,128)(2,1)} %weight_last.2), channel_id=1, source_target_pairs={{0,4},{4,0},{8,12},{12,8},{16,20},{20,16},{24,28},{28,24},{32,36},... | collective-permute-start | bytes 786440 | tf_op jit(solution)/shard_map/ppermute | solution.py:440
  (15 other events, 14.1 us)

commit v3 on v2

--- a/solution.py
+++ b/solution.py
@@ -18,11 +18,16 @@
 LOG2E = math.log2(math.e)
 MB = 1024 * 1024
 HALVES = 2
-BIG = 58
+BIG = 20
+SMALL = pl.CostEstimate(flops=1000, bytes_accessed=1000, transcendentals=0)
 
 
 def dot(a, b, ca, cb):
     return lax.dot_general(a, b, (((ca,), (cb,)), ((), ())), preferred_element_type=F32)
+
+
+def pinned(*args):
+    return [pltpu.with_memory_space_constraint(a, pltpu.HBM) for a in args]
 
 
 def params(limit):
@@ -50,7 +55,7 @@
     cols = 256
     per = feats // cols
     blk = lambda r: pl.BlockSpec((2, r, cols), lambda j: (0, 0, j))
-    out = lambda r: jax.ShapeDtypeStruct((2, r, feats), BF)
+    out = lambda r: pltpu.HBM((2, r, feats), BF)
     return pl.pallas_call(
         pool_kernel,
         grid=(per,),
@@ -58,8 +63,9 @@
         out_specs=[blk(nr), blk(fr), blk(FB + nr), blk(FB + nr)],
         out_shape=[out(nr), out(fr), out(FB + nr), out(FB + nr)],
         compiler_params=params(BIG),
+        cost_estimate=SMALL,
         name="pool",
-    )(k, v)
+    )(*pinned(k, v))
 
 
 def level_bias(position, blocks, pooled_rows, coarse_count, tokens_here, seq_count):
@@ -103,9 +109,9 @@
     vals, cvals = gathered(1, left_ref, v_ref, right_ref, near_ref, far_ref)
     vals_t, cvals_t = vals.T, cvals.T
     csc = dot(ckeys, q, 1, 1)
-    for b in range(blocks):
-        fine, coarse = scores(b, blocks, pos_ref, seq_count, q, keys, csc, bias_ref)
-        peak = jnp.maximum(fine.max(axis=0, keepdims=True), coarse.max(axis=0, keepdims=True))
+    raw = [scores(b, blocks, pos_ref, seq_count, q, keys, csc, bias_ref) for b in range(blocks)]
+    peaks = [jnp.maximum(fine.max(axis=0, keepdims=True), coarse.max(axis=0, keepdims=True)) for fine, coarse in raw]
+    for b, ((fine, coarse), peak) in enumerate(zip(raw, peaks)):
         pf = jnp.exp2(fine - peak)
         pc = jnp.exp2(coarse - peak)
         total = pf.sum(axis=0, keepdims=True) + pc.sum(axis=0, keepdims=True)
@@ -192,8 +198,9 @@
             jax.ShapeDtypeStruct((heads, 1, tokens), F32),
         ],
         compiler_params=params(BIG),
+        cost_estimate=SMALL,
         name="attend",
-    )(pos, q, k, v, left, right, near, far, bias)
+    )(pos, *pinned(q, k, v, left, right, near, far, bias))
 
 
 def bwd_halves_kernel(seq_count, pos_ref, q_ref, k_ref, v_ref, *refs):
@@ -240,16 +247,17 @@
             ],
         ),
         out_shape=[
-            jax.ShapeDtypeStruct((tokens, feats), BF),
-            jax.ShapeDtypeStruct((tokens, feats), F32),
-            jax.ShapeDtypeStruct((tokens, feats), F32),
+            pltpu.HBM((tokens, feats), BF),
+            pltpu.HBM((tokens, feats), F32),
+            pltpu.HBM((tokens, feats), F32),
             jax.ShapeDtypeStruct((2, halo, feats), BF),
             jax.ShapeDtypeStruct((2, halo, feats), BF),
             jax.ShapeDtypeStruct((2, fr, feats), BF),
         ],
         compiler_params=params(BIG),
+        cost_estimate=SMALL,
         name="attend_grad",
-    )(pos, q, k, v, *pairs, far, bias, do)
+    )(pos, *pinned(q, k, v, *pairs, far, bias), do)
 
 
 def combine_kernel(gk_ref, gv_ref, left_ref, right_ref, far_ref, ok_ref, ov_ref):
@@ -282,8 +290,9 @@
         out_specs=[tok, tok],
         out_shape=[jax.ShapeDtypeStruct((rows, feats), BF)] * 2,
         compiler_params=params(BIG),
+        cost_estimate=SMALL,
         name="combine",
-    )(gk, gv, from_left, from_right, far)
+    )(*pinned(gk, gv, from_left, from_right, far))
 
 
 UNITS = 4
@@ -304,24 +313,25 @@
     return jnp.stack(rows).astype(jnp.int32)
 
 
-def weight_kernel(n_units, n_recv, pair_out, cols_ref, *refs):
-    atts, ogs = refs[:n_units], refs[n_units : 2 * n_units]
-    recvs = refs[2 * n_units : 2 * n_units + n_recv]
-    outs = refs[2 * n_units + n_recv :]
+def weight_kernel(n_units, per, n_recv, pair_out, cols_ref, *refs):
+    atts, ogs = refs[:n_units], refs[n_units : n_units + n_units * per]
+    recvs = refs[n_units + n_units * per : n_units + n_units * per + n_recv]
+    outs = refs[n_units + n_units * per + n_recv :]
     for u in range(n_units):
-        res = dot(atts[u][...], ogs[u][...], 1, 0)
-        rows, width = res.shape[0], res.shape[1] // 2
-        for z in range(2):
-            part = res[:, z * width : (z + 1) * width]
-            for r in recvs[u::n_units]:
-                part += r[0, z].astype(F32)
-            if pair_out:
-                outs[u // 2][0, z, (u % 2) * rows : (u % 2 + 1) * rows] = part.astype(BF)
-            else:
-                outs[u][0, z] = part.astype(BF)
-
-
-def weight_step(cols, attt, og, width, units, start, count, recvs, pair_out):
+        for b in range(per):
+            res = dot(atts[u][...], ogs[u * per + b][...], 1, 0)
+            rows, width = res.shape[0], res.shape[1] // 2
+            for z in range(2):
+                part = res[:, z * width : (z + 1) * width]
+                for r in recvs[u::n_units]:
+                    part += r[b, z].astype(F32)
+                if pair_out:
+                    outs[u // 2][b, z, (u % 2) * rows : (u % 2 + 1) * rows] = part.astype(BF)
+                else:
+                    outs[u][b, z] = part.astype(BF)
+
+
+def weight_step(cols, attt, og, width, units, start, count, per, recvs, pair_out):
     tokens = attt[0].shape[1]
     rows = attt[0].shape[0] * HALVES // UNITS
     n = len(units)
@@ -329,110 +339,174 @@
     in_specs, args = [], []
     for u in units:
         in_specs.append(pl.BlockSpec((rows, tokens), lambda j, *_, u=u: (u % per_half, 0)))
-        args.append(attt[u // per_half])
+        args += pinned(attt[u // per_half]) if recvs else [attt[u // per_half]]
     for u in units:
-        in_specs.append(pl.BlockSpec((tokens, 2 * width), lambda j, c, u=u: (0, c[u, start + j])))
-        args.append(og)
-    for step in recvs:
+        for b in range(per):
+            in_specs.append(pl.BlockSpec((tokens, 2 * width), lambda j, c, u=u, b=b: (0, c[u, start + j * per + b])))
+            args += pinned(og)
+    for i, step in enumerate(recvs):
         for u in units:
             r, paired = step[u]
-            if paired:
-                in_specs.append(pl.BlockSpec((1, 2, rows, width), lambda j, *_, u=u: (start + j, 0, u % 2, 0)))
-            else:
-                in_specs.append(pl.BlockSpec((1, 2, rows, width), lambda j, *_: (start + j, 0, 0, 0)))
+            if i < len(recvs) - 1:
+                (r,) = pinned(r)
+            at = u % 2 if paired else 0
+            in_specs.append(pl.BlockSpec((per, 2, rows, width), lambda j, *_, at=at: (start // per + j, 0, at, 0)))
             args.append(r)
     n_out = n // 2 if pair_out else n
     out_rows = 2 * rows if pair_out else rows
     return pl.pallas_call(
-        functools.partial(weight_kernel, n, len(recvs) * n, pair_out),
+        functools.partial(weight_kernel, n, per, len(recvs) * n, pair_out),
         grid_spec=pltpu.PrefetchScalarGridSpec(
             num_scalar_prefetch=1,
-            grid=(count,),
+            grid=(count // per,),
             in_specs=in_specs,
-            out_specs=[pl.BlockSpec((1, 2, out_rows, width), lambda j, *_: (j, 0, 0, 0))] * n_out,
+            out_specs=[pl.BlockSpec((per, 2, out_rows, width), lambda j, *_: (j, 0, 0, 0))] * n_out,
         ),
         out_shape=[jax.ShapeDtypeStruct((count, 2, out_rows, width), BF)] * n_out,
         compiler_params=params(BIG),
+        cost_estimate=SMALL,
         name="weight_step",
     )(cols, *args)
 
 
-def weight_last_kernel(scale, n_recv, last, cols_ref, *refs):
-    o_ref = refs[-1]
+def weight_last_kernel(n_recv, table_ref, *refs):
+    send_ref, keep_ref = refs[-2:]
     atts, ogs = refs[:UNITS], refs[UNITS : 2 * UNITS]
     recvs = refs[2 * UNITS : 2 * UNITS + n_recv]
+    own_first = table_ref[UNITS] == 0
     rows = atts[0].shape[0]
     for u in range(UNITS):
-        part = dot(atts[u][...], ogs[u][...], 1, 0)
-        for r in recvs[u::UNITS]:
-            part += r[0, 0].astype(F32)
-        if last:
-            part += refs[2 * UNITS + n_recv][u * rows : (u + 1) * rows].astype(F32)
-        o_ref[u * rows : (u + 1) * rows] = (part * scale).astype(o_ref.dtype)
-
-
-def weight_last(cols, attt, og, width, z, recvs, got, scale, dtype):
+        res = dot(atts[u][...], ogs[u][...], 1, 0)
+        width = res.shape[1] // 2
+        parts = []
+        for z in range(2):
+            part = res[:, z * width : (z + 1) * width]
+            for r in recvs[u::UNITS]:
+                part += r[0, z].astype(F32)
+            parts.append(part)
+        at = slice(u * rows, (u + 1) * rows)
+        keep_ref[at] = jnp.where(own_first, parts[0], parts[1])
+        send_ref[at] = jnp.where(own_first, parts[1], parts[0]).astype(BF)
+
+
+def weight_last(cols, attt, og, width, z, recvs):
     tokens = attt[0].shape[1]
     rows = attt[0].shape[0] * HALVES // UNITS
     per_half = UNITS // HALVES
-    table = jnp.concatenate([cols[:, 0] * 2 + z, z[None]])
+    table = jnp.concatenate([cols[:, 0], z[None]])
     in_specs, args = [], []
     for u in range(UNITS):
         in_specs.append(pl.BlockSpec((rows, tokens), lambda j, *_, u=u: (u % per_half, 0)))
-        args.append(attt[u // per_half])
+        args += pinned(attt[u // per_half])
     for u in range(UNITS):
-        in_specs.append(pl.BlockSpec((tokens, width), lambda j, c, u=u: (0, c[u])))
-        args.append(og)
-    for step in recvs:
+        in_specs.append(pl.BlockSpec((tokens, 2 * width), lambda j, c, u=u: (0, c[u])))
+        args += pinned(og)
+    for i, step in enumerate(recvs):
         for u in range(UNITS):
             r, paired = step[u]
+            if i < len(recvs) - 1:
+                (r,) = pinned(r)
             at = u % 2 if paired else 0
-            in_specs.append(pl.BlockSpec((1, 1, rows, width), lambda j, c, at=at: (0, c[UNITS], at, 0)))
+            in_specs.append(pl.BlockSpec((1, 2, rows, width), lambda j, c, at=at: (0, 0, at, 0)))
             args.append(r)
     full = pl.BlockSpec((UNITS * rows, width), lambda j, *_: (0, 0))
-    if got is not None:
-        in_specs.append(full)
-        args.append(got)
-    return pl.pallas_call(
-        functools.partial(weight_last_kernel, scale, len(recvs) * UNITS, got is not None),
-        grid_spec=pltpu.PrefetchScalarGridSpec(num_scalar_prefetch=1, grid=(1,), in_specs=in_specs, out_specs=full),
-        out_shape=jax.ShapeDtypeStruct((UNITS * rows, width), dtype),
-        compiler_params=params(BIG),
+    return pl.pallas_call(
+        functools.partial(weight_last_kernel, len(recvs) * UNITS),
+        grid_spec=pltpu.PrefetchScalarGridSpec(num_scalar_prefetch=1, grid=(1,), in_specs=in_specs, out_specs=[full, full]),
+        out_shape=[jax.ShapeDtypeStruct((UNITS * rows, width), t) for t in (BF, F32)],
+        compiler_params=params(BIG),
+        cost_estimate=SMALL,
         name="weight_last",
     )(table, *args)
 
 
-def layer_kernel(cols_ref, a0_ref, a1_ref, w_ref, *refs):
-    o_ref = refs[-1]
+def project_kernel(og_ref, w_ref, o_ref):
+    n = o_ref.shape[1]
+    at = pl.multiple_of(pl.program_id(0) * n, n)
+    o_ref[...] = dot(og_ref[...], w_ref[pl.ds(at, n), :], 1, 1).astype(BF)
+
+
+def project(og, w):
+    tokens, feats = og.shape[0], w.shape[0]
+    n = 256
+    return pl.pallas_call(
+        project_kernel,
+        grid=(feats // n,),
+        in_specs=[pl.BlockSpec(memory_space=pltpu.VMEM)] * 2,
+        out_specs=pl.BlockSpec((tokens, n), lambda j: (0, j)),
+        out_shape=jax.ShapeDtypeStruct((tokens, feats), BF),
+        compiler_params=params(BIG),
+        cost_estimate=SMALL,
+        name="project",
+    )(og, w)
+
+
+def project_kernel(cols_ref, a0_ref, a1_ref, og_ref, w_ref, send_ref, keep_ref, grad_ref, acc_ref):
+    step = pl.program_id(0)
     half = a0_ref.shape[1]
-    res = dot(a0_ref[...], w_ref[:half], 1, 0) + dot(a1_ref[...], w_ref[half:], 1, 0)
-    for r in refs[:-1]:
-        res += r[0].astype(F32)
-    o_ref[0] = res.astype(BF)
-
-
-def layer_step(cols, att, w, width, recvs):
+    part = dot(og_ref[...], w_ref[...], 1, 1)
+
+    @pl.when(step == 0)
+    def _():
+        acc_ref[...] = part
+
+    @pl.when(step > 0)
+    def _():
+        acc_ref[...] += part
+
+    res = (dot(a0_ref[...], w_ref[:half], 1, 0) + dot(a1_ref[...], w_ref[half:], 1, 0)).astype(BF)
+
+    @pl.when(step < pl.num_programs(0) // 2)
+    def _():
+        send_ref[0] = res
+
+    @pl.when(step >= pl.num_programs(0) // 2)
+    def _():
+        keep_ref[0] = res
+
+    @pl.when(step == pl.num_programs(0) - 1)
+    def _():
+        grad_ref[...] = acc_ref[...].astype(BF)
+
+
+def project(cols, att, og, w, width):
     tokens, half = att[0].shape
-    steps = cols.shape[0]
-    sub = 2
+    feats = w.shape[0]
+    sub = 1
     n = width // sub
-    return pl.pallas_call(
-        layer_kernel,
+    parts = cols.shape[0]
+    steps = parts * sub
+    mid = steps // 2
+    whole = lambda r, c: pl.BlockSpec((r, c), lambda s, *_: (0, 0))
+    first = lambda s: jnp.minimum(s, mid - 1)
+    later = lambda s: jnp.maximum(s - mid, 0)
+    return pl.pallas_call(
+        project_kernel,
         grid_spec=pltpu.PrefetchScalarGridSpec(
             num_scalar_prefetch=1,
-            grid=(steps, sub),
+            grid=(steps,),
             in_specs=[
-                pl.BlockSpec((tokens, half), lambda j, s, *_: (0, 0)),
-                pl.BlockSpec((tokens, half), lambda j, s, *_: (0, 0)),
-                pl.BlockSpec((w.shape[0], n), lambda j, s, c: (0, c[j] * sub + s)),
-                *[pl.BlockSpec((1, tokens, n), lambda j, s, *_, at=at: (at, 0, s)) for _, at in recvs],
+                whole(tokens, half),
+                whole(tokens, half),
+                pl.BlockSpec((tokens, n), lambda s, c: (0, c[s // sub] * sub + s % sub)),
+                pl.BlockSpec((feats, n), lambda s, c: (0, c[s // sub] * sub + s % sub)),
             ],
-            out_specs=pl.BlockSpec((1, tokens, n), lambda j, s, *_: (j, 0, s)),
+            out_specs=[
+                pl.BlockSpec((1, tokens, n), lambda s, *_: (first(s) // sub, 0, first(s) % sub)),
+                pl.BlockSpec((1, tokens, n), lambda s, *_: (later(s) // sub, 0, later(s) % sub)),
+                whole(tokens, feats),
+            ],
+            scratch_shapes=[pltpu.VMEM((tokens, feats), F32)],
         ),
-        out_shape=jax.ShapeDtypeStruct((steps, tokens, width), BF),
-        compiler_params=params(BIG),
-        name="layer_step",
-    )(cols, att[0], att[1], w, *[r for r, _ in recvs])
+        out_shape=[
+            jax.ShapeDtypeStruct((parts // 2, tokens, width), BF),
+            pltpu.HBM((parts // 2, tokens, width), BF),
+            jax.ShapeDtypeStruct((tokens, feats), BF),
+        ],
+        compiler_params=params(BIG),
+        cost_estimate=SMALL,
+        name="project",
+    )(cols, *att, *pinned(og, w))
 
 
 def swap(x, axis, bits):
@@ -442,6 +516,20 @@
 
 def after(x, *deps):
     return lax.optimization_barrier((x, *deps))[0]
+
+
+def own_rows(x, pos, seq_count):
+    bit = seq_count // 2
+    while bit:
+        low = (pos & bit) == 0
+        half = x.shape[1] // 2
+        a, b = x[:, :half], x[:, half:]
+        got = swap(jnp.where(low, b, a), "seq", bit)
+        x = jnp.where(low, a, b).astype(F32) + got.astype(F32)
+        bit //= 2
+        if bit:
+            x = x.astype(BF)
+    return x
 
 
 def shards(queries, token_keys, token_values, out_weight, out_grad):
@@ -454,66 +542,81 @@
     right_perm = [(i, i + 1) for i in range(seq_count - 1)]
     left_perm = [(i + 1, i) for i in range(seq_count - 1)]
 
-    near, far_own, from_left, from_right = [], [], [], []
-    for half in range(HALVES):
-        n, f, to_left, to_right = pool(token_keys, token_values, half)
-        near.append(n)
-        far_own.append(f)
+    pools = [pool(token_keys, token_values, half) for half in range(HALVES)]
+    near = [p[0] for p in pools]
+    far_own = jnp.concatenate([p[1] for p in pools], axis=2)
+    from_left, from_right = [], []
+    for half, (_, _, to_left, to_right) in enumerate(pools):
+        if half > 0:
+            to_left, to_right = lax.optimization_barrier((to_left, to_right, from_left[0], from_right[0]))[:2]
         from_left.append(lax.ppermute(to_right, "seq", right_perm))
         from_right.append(lax.ppermute(to_left, "seq", left_perm))
-    far_all = jnp.concatenate(far_own, axis=2)
-    far_all = jnp.broadcast_to(far_all, (seq_count, *far_all.shape))
+    far_all = jnp.broadcast_to(far_own, (seq_count, *far_own.shape))
     far_all = lax.all_to_all(far_all, "seq", 0, 0, tiled=True)
     far = jnp.moveaxis(far_all, 0, 1).reshape(2, -1, feats)
-    attn_grad = dot(out_grad, out_weight, 1, 1).astype(BF)
     bias = level_bias(pos, tokens // FB, near[0].shape[1], far.shape[1], tokens, seq_count)
-
-    att, attt, lse = zip(
-        *[
-            forward(seq_count, pos1, queries, token_keys, token_values, from_left[h], from_right[h], near[h], far, bias, h)
-            for h in range(HALVES)
-        ]
-    )
 
     part = width // seq_count
     cols = block_order(pos)
-    recv1 = [None] * UNITS
-    for h in range(HALVES):
-        units = list(range(h * UNITS // HALVES, (h + 1) * UNITS // HALVES))
-        out = weight_step(cols, attt, out_grad, part, units, 8, 8, [], False)
+    recv1, recv2 = [None] * UNITS, [None] * UNITS
+    att, attt, lse = [], [], []
+    half_units = [list(range(h * UNITS // HALVES, (h + 1) * UNITS // HALVES)) for h in range(HALVES)]
+    out = None
+    for h, units in enumerate(half_units):
+        q = queries if out is None else after(queries, *out)
+        a, at, ls = forward(seq_count, pos1, q, token_keys, token_values, from_left[h], from_right[h], near[h], far, bias, h)
+        att.append(a)
+        attt.append(at)
+        lse.append(ls)
+        table = after(cols, from_left[1], from_right[1]) if h == 0 else cols
+        out = weight_step(table, attt, out_grad, part, units, 8, 8, 4, [], False)
         for u, x in zip(units, out):
             recv1[u] = (swap(x, "seq", ROUTE[u][1] << SHIFT[ROUTE[u][0]]), False)
+
+    def second(pair, dep):
+        out = weight_step(after(cols, *dep), attt, out_grad, part, half_units[pair], 4, 4, 2, [recv1], False)
+        for u, x in zip(half_units[pair], out):
+            recv2[u] = (swap(x, "seq", ROUTE[u][2] << SHIFT[ROUTE[u][0]]), False)
+        return out
+
+    recv3, recv4 = [None] * UNITS, [None] * UNITS
+
+    def along_other(pair, step, dep):
+        got = [recv1, recv2, recv3][: 2 + step]
+        start = 2 - step
+        out = weight_step(after(cols, *dep), attt, out_grad, part, half_units[pair], start, start, start, got, True)
+        moved = swap(out[0], "seq", SECOND[pair][step] << SHIFT[1 - ROUTE[2 * pair][0]])
+        for u in half_units[pair]:
+            (recv3, recv4)[step][u] = (moved, True)
+        return out
 
     c, zl = tp & 1, tp >> 1
     lwidth = width // tp_count
     lcols = jnp.stack([zl, zl ^ 1]) * 2
-    lgot1 = swap(layer_step(lcols + (c ^ 1), att, out_weight, lwidth, []), "tp", 1)
-
+    lorder = jnp.concatenate([lcols + (c ^ 1), lcols + c])
+    lsend1, lkeep, attn_grad = project(lorder, (after(att[0], *out), att[1]), out_grad, out_weight, lwidth)
+    lgot1 = swap(lsend1, "tp", 1)
+
+    out = second(0, [attn_grad])
     dq, gk, gv, sl, sr, gfar = backward(
-        seq_count, pos1, queries, token_keys, token_values, from_left, from_right, near, far, bias, attn_grad, att, lse
+        seq_count, pos1, after(queries, *out), token_keys, token_values, from_left, from_right, near, far, bias, attn_grad, att, lse
     )
     back_left = lax.ppermute(sr, "seq", right_perm)
     back_right = lax.ppermute(sl, "seq", left_perm)
-
-    lgot2 = swap(layer_step(lcols[1:] + c, att, out_weight, lwidth, [(lgot1, 1)]), "tp", 2)
-
-    every = list(range(UNITS))
-    out = weight_step(cols, attt, out_grad, part, every, 4, 4, [recv1], False)
-    recv2 = [(swap(x, "seq", ROUTE[u][2] << SHIFT[ROUTE[u][0]]), False) for u, x in enumerate(out)]
-    far_parts = jnp.moveaxis(gfar.reshape(2, seq_count, -1, feats), 1, 0)
-    far_sum = lax.all_to_all(far_parts, "seq", 0, 0, tiled=True).astype(F32).sum(axis=0)
-    layer_out = layer_step(lcols[:1] + c, att, out_weight, lwidth, [(lgot1, 0), (lgot2, 0)])[0]
-
-    got = [recv1, recv2]
-    for step, (start, count) in enumerate(((2, 2), (1, 1))):
-        out = weight_step(cols, attt, out_grad, part, every, start, count, got, True)
-        moved = [swap(x, "seq", SECOND[p][step] << SHIFT[1 - ROUTE[2 * p][0]]) for p, x in enumerate(out)]
-        got.append([(moved[u // 2], True) for u in every])
-    zh = pos & 1
-    zgot = swap(weight_last(cols, attt, out_grad, part, zh ^ 1, got, None, 1.0, BF), "seq", 1)
-    weight_grad = weight_last(cols, attt, out_grad, part, zh, got, zgot, 1.0 / math.sqrt(tokens * seq_count), F32)
-
+    out = along_other(0, 0, [gfar])
+    out = second(1, out)
+    lsend2 = (lkeep[1].astype(F32) + lgot1[1].astype(F32)).astype(BF)
+    lgot2 = swap(lsend2, "tp", 2)
+    out = along_other(0, 1, out)
+    far_sum = own_rows(after(gfar, *out), pos, seq_count)
+    out = along_other(1, 0, out)
+    out = along_other(1, 1, [*out, back_left, back_right])
+    got = [recv1, recv2, recv3, recv4]
+    zsend, zkeep = weight_last(cols, attt, out_grad, part, pos & 1, got)
+    zgot = swap(zsend, "seq", 1)
+    layer_out = (lkeep[0].astype(F32) + lgot1[0].astype(F32) + lgot2.astype(F32)).astype(BF)
     key_grad, value_grad = combine(gk, gv, back_left, back_right, far_sum)
+    weight_grad = (zkeep + zgot.astype(F32)) * (1.0 / math.sqrt(tokens * seq_count))
     return layer_out, dq, key_grad, value_grad, weight_grad
 
 

time: 232 us -> 210 us (0.905)
  Pallas kernels: 93.2 us -> 77.7 us
  local copies, waits for them, and re-layouts: 11.5 us -> 3.33 us
  matrix products: 8.05 us -> 0 us
  starting transfers between devices: 58.4 us -> 64.6 us
  other arithmetic: 4.24 us -> 7.81 us
    ppermute x15 -> x20, starting transfers between devices: 19.8 us -> 34.3 us  [swap(): return lax.ppermute(x, axis, [(i, i ^ bits) for i in range(n)])]
    ppermute x2, waiting for transfers between devices: 12.3 us -> 2.28 us  [shards(): from_left.append(lax.ppermute(to_right, 'seq', right_perm))]
    pallas_call x10, Pallas kernels: 53.1 us -> 43.8 us  [the longest x8 25.2 us: weight_step(): pl.pallas_call(functools.partial(weight_kernel, n, per, len(recvs) * n, p...]
    dot_general x1 -> x0, matrix products: 8.05 us -> none  [dot(): lax.dot_general(a, b, (((ca,), (cb,)), ((), ())), preferred_element_type=...]
    ppermute x15 -> x20, waiting for transfers between devices: 39.8 us -> 47.5 us  [swap(): return lax.ppermute(x, axis, [(i, i ^ bits) for i in range(n)])]
    all_to_all x1 -> x0, starting transfers between devices: 7.03 us -> none  [shards(): lax.all_to_all(far_parts, 'seq', 0, 0, tiled=True).astype(F32).sum(axis=0)]
    unnamed x48 -> x44, local copies, waits for them, and re-layouts: 6.75 us -> 0.1 us
    pallas_call x2, Pallas kernels: 16.3 us -> 9.78 us  [forward(): pl.pallas_call(functools.partial(fwd_kernel, seq_count), grid_spec=pltpu....]
  transfers between devices with their start and end apart: 23 -> 27, of which waited for: 13 -> 9; matrix products, arithmetic and copies ran while one was open for 7% -> 5% of each run, Pallas kernels for 30% -> 34%
where the time goes in v3:
time: 210 us; the launch traced here: 208 us
  Pallas kernels  77.7 us (37%)
  starting transfers between devices  64.6 us (31%)
  waiting for transfers between devices  53.4 us (25%)
  other arithmetic  7.81 us (4%)
  local copies, waits for them, and re-layouts  3.33 us (2%)
    ppermute x20, waiting for transfers between devices, swap(): return lax.ppermute(x, axis, [(i, i ^ bits) for i in range(n)])  47.5 us
    ppermute x20, starting transfers between devices, swap(): return lax.ppermute(x, axis, [(i, i ^ bits) for i in range(n)])  34.3 us
    pallas_call x8, Pallas kernels, weight_step(): pl.pallas_call(functools.partial(weight_kernel, n, per, len(recvs) * n, p...  25.2 us
    pallas_call x1, Pallas kernels, project(): pl.pallas_call(project_kernel, grid_spec=pltpu.PrefetchScalarGridSpec(num...  15.4 us
    pallas_call x1, Pallas kernels, backward(): pl.pallas_call(functools.partial(bwd_halves_kernel, seq_count), grid_spec...  14.9 us
    ppermute x2, starting transfers between devices, shards(): from_left.append(lax.ppermute(to_right, 'seq', right_perm))  11.2 us
    all_to_all x1, starting transfers between devices, shards(): far_all = lax.all_to_all(far_all, 'seq', 0, 0, tiled=True)  10.9 us
    pallas_call x2, Pallas kernels, forward(): pl.pallas_call(functools.partial(fwd_kernel, seq_count), grid_spec=pltpu....  9.78 us
  transfers between devices with their start and end apart: 27, of which 9 were waited for; matrix products, arithmetic and copies ran while one was open for 5% of the time, Pallas kernels for 34%

profile of v3, /device:TPU:0, one launch (start us, length us, event | category | flops | bytes accessed | tf_op | source)
XLA Modules:
  0.0 208.0 jit_solution(4870956860230549147)
XLA Ops:
  0.7 2.4 %pool.2 = (bf16[2,32,512]{2,1,0:T(8,128)(2,1)}, bf16[2,2,512]{2,1,0:T(2,128)(2,1)}, bf16[2,160,512]{2,1,0:T(8,128)(2,1)}, bf16[2,160,512]{2,1,0:T(8,128)(2,1)}) custom-call(bf16[512,1024]{1,0:T(8,128)(2,1)} %k_ref.9, bf16[512,1024]{1,0:T(8,128)(2,1)} %v_ref.9), custom_call_target="tpu_custom_call" | custom-call | flops 1000 | bytes 1000 | tf_op jit(solution)/shard_map/pool/pallas_call | solution.py:59
  3.0 6.0 %collective-permute-start = (bf16[2,160,512]{2,1,0:T(8,128)(2,1)}, bf16[2,160,512]{2,1,0:T(8,128)(2,1)S(1)}, u32[]{:S(2)}, u32[]{:S(2)}) collective-permute-start(bf16[2,160,512]{2,1,0:T(8,128)(2,1)} %get-tuple-element.53), channel_id=1, source_target_pairs={{0,4},{4,8},{8,12},{12,16},{16,20},{20,24},{24,28},{28,32},{32,36}... | collective-permute-start | bytes 983048 | tf_op jit(solution)/shard_map/ppermute | solution.py:552
  10.3 2.4 %pool.3 = (bf16[2,32,512]{2,1,0:T(8,128)(2,1)}, bf16[2,2,512]{2,1,0:T(2,128)(2,1)}, bf16[2,160,512]{2,1,0:T(8,128)(2,1)}, bf16[2,160,512]{2,1,0:T(8,128)(2,1)}) custom-call(bf16[512,1024]{1,0:T(8,128)(2,1)} %k_ref.9, bf16[512,1024]{1,0:T(8,128)(2,1)} %v_ref.9), custom_call_target="tpu_custom_call" | custom-call | flops 1000 | bytes 1000 | tf_op jit(solution)/shard_map/pool/pallas_call | solution.py:59
  14.2 10.9 %all-to-all-start = ((bf16[32,2,2,1024]{3,2,1,0:T(2,128)(2,1)}), bf16[32,2,2,1024]{3,2,1,0:T(2,128)(2,1)S(1)}, u32[]{:S(2)}, u32[]{:S(2)}) async-start(bf16[32,2,2,1024]{3,2,1,0:T(2,128)(2,1)} %broadcast_in_dim.27), calls=%async_computation | async-start | bytes 524288 | tf_op jit(solution)/shard_map/all_to_all | solution.py:555
  25.7 5.2 %collective-permute-start.2 = (bf16[2,160,512]{2,1,0:T(8,128)(2,1)}, bf16[2,160,512]{2,1,0:T(8,128)(2,1)S(1)}, u32[]{:S(2)}, u32[]{:S(2)}) collective-permute-start(bf16[2,160,512]{2,1,0:T(8,128)(2,1)} %get-tuple-element.61), channel_id=1, source_target_pairs={{0,4},{4,8},{8,12},{12,16},{16,20},{20,24},{24,28},{28,32},{32,36}... | collective-permute-start | bytes 983048 | tf_op jit(solution)/shard_map/ppermute | solution.py:552
  32.3 3.6 %all-to-all-done = bf16[32,2,2,1024]{3,2,1,0:T(2,128)(2,1)S(1)} async-done(((bf16[32,2,2,1024]{3,2,1,0:T(2,128)(2,1)}), bf16[32,2,2,1024]{3,2,1,0:T(2,128)(2,1)S(1)}, u32[]{:S(2)}, u32[]{:S(2)}) %all-to-all-start) | async-done | bytes 262176 | tf_op jit(solution)/shard_map/all_to_all | solution.py:555
  37.8 4.9 %attend.2 = (bf16[512,512]{1,0:T(8,128)(2,1)S(1)}, bf16[512,512]{1,0:T(8,128)(2,1)S(1)}, f32[4,1,512]{2,1,0:T(1,128)S(1)}) custom-call(s32[1]{0:T(128)} %bitcast.2.pos_ref, bf16[512,1024]{1,0:T(8,128)(2,1)} %q_ref.3, bf16[512,1024]{1,0:T(8,128)(2,1)} %k_ref.9, bf16[512,1024]{1,0:T(8,128)(2,1)} %v_ref.9, bf16[2,160,512]{2,1,0:T(8,128)(2,1)} %copy-done.15, ...), custom_call_target="tpu_custom_call" | custom-call | flops 1000 | bytes 1000 | tf_op jit(solution)/shard_map/attend/pallas_call | solution.py:183
  42.7 2.3 %collective-permute-done.2.left_ref.refs_1_ = bf16[2,160,512]{2,1,0:T(8,128)(2,1)S(1)} collective-permute-done((bf16[2,160,512]{2,1,0:T(8,128)(2,1)}, bf16[2,160,512]{2,1,0:T(8,128)(2,1)S(1)}, u32[]{:S(2)}, u32[]{:S(2)}) %collective-permute-start.2) | collective-permute-done | bytes 327712 | tf_op jit(solution)/shard_map/ppermute | solution.py:552
  44.9 4.5 %weight_step.8 = (bf16[8,2,256,128]{3,2,1,0:T(8,128)(2,1)}, bf16[8,2,256,128]{3,2,1,0:T(8,128)(2,1)}) custom-call(s32[4,16]{1,0:T(4,128)S(1)} %pad_add_fusion.cols_ref, bf16[512,512]{1,0:T(8,128)(2,1)S(1)} %get-tuple-element.64.refs_0_.refs_1_, bf16[512,512]{1,0:T(8,128)(2,1)S(1)} %get-tuple-element.64.refs_0_.refs_1_, bf16[512,4096]{1,0:T(8,128)(2,1)} %refs_7_.5, ...), custom_call_target="tpu_custom_call" | custom-call | flops 1000 | bytes 1000 | tf_op jit(solution)/shard_map/weight_step/pallas_call | solution.py:357
  49.5 6.2 %collective-permute-start.6 = (bf16[8,2,256,128]{3,2,1,0:T(8,128)(2,1)}, bf16[8,2,256,128]{3,2,1,0:T(8,128)(2,1)S(1)}, u32[]{:S(2)}, u32[]{:S(2)}) collective-permute-start(bf16[8,2,256,128]{3,2,1,0:T(8,128)(2,1)} %get-tuple-element.65), channel_id=1, source_target_pairs={{0,32},{4,36},{8,40},{12,44},{16,48},{20,52},{24,56},{28,60},{32,0... | collective-permute-start | bytes 3145736 | tf_op jit(solution)/shard_map/ppermute | solution.py:514
  57.9 4.9 %attend.3 = (bf16[512,512]{1,0:T(8,128)(2,1)S(1)}, bf16[512,512]{1,0:T(8,128)(2,1)S(1)}, f32[4,1,512]{2,1,0:T(1,128)S(1)}) custom-call(s32[1]{0:T(128)} %bitcast.2.pos_ref, bf16[512,1024]{1,0:T(8,128)(2,1)} %q_ref.3, bf16[512,1024]{1,0:T(8,128)(2,1)} %k_ref.9, bf16[512,1024]{1,0:T(8,128)(2,1)} %v_ref.9, bf16[2,160,512]{2,1,0:T(8,128)(2,1)} %copy-done.17, ...), custom_call_target="tpu_custom_call" | custom-call | flops 1000 | bytes 1000 | tf_op jit(solution)/shard_map/attend/pallas_call | solution.py:183
  62.9 4.6 %weight_step.9 = (bf16[8,2,256,128]{3,2,1,0:T(8,128)(2,1)}, bf16[8,2,256,128]{3,2,1,0:T(8,128)(2,1)}) custom-call(s32[4,16]{1,0:T(4,128)S(1)} %pad_add_fusion.cols_ref, bf16[512,512]{1,0:T(8,128)(2,1)S(1)} %get-tuple-element.69.refs_0_.refs_1_.refs_2_.refs_3_, bf16[512,512]{1,0:T(8,128)(2,1)S(1)} %get-tuple-element.69.refs_0_.refs_1_.refs_2_.refs_3_, ...), custom_call_target="tpu_custom_call" | custom-call | flops 1000 | bytes 1000 | tf_op jit(solution)/shard_map/weight_step/pallas_call | solution.py:357
  67.7 15.4 %project.1 = (bf16[2,512,1024]{2,1,0:T(8,128)(2,1)}, bf16[2,512,1024]{2,1,0:T(8,128)(2,1)}, bf16[512,1024]{1,0:T(8,128)(2,1)S(1)}) custom-call(s32[4]{0:T(128)S(1)} %pad_add_fusion.1.cols_ref, bf16[512,512]{1,0:T(8,128)(2,1)S(1)} %get-tuple-element.72.a0_ref.refs_6_, bf16[512,512]{1,0:T(8,128)(2,1)S(1)} %get-tuple-element.73.a1_ref.refs_7_, ...), custom_call_target="tpu_custom_call" | custom-call | flops 1000 | bytes 1000 | tf_op jit(solution)/shard_map/project/pallas_call | solution.py:483
  83.1 3.2 %weight_step.10 = (bf16[4,2,256,128]{3,2,1,0:T(8,128)(2,1)S(1)}, bf16[4,2,256,128]{3,2,1,0:T(8,128)(2,1)S(1)}) custom-call(s32[4,16]{1,0:T(4,128)S(1)} %pad_add_fusion.cols_ref, bf16[512,512]{1,0:T(8,128)(2,1)} %copy-done, bf16[512,512]{1,0:T(8,128)(2,1)} %copy-done, bf16[512,4096]{1,0:T(8,128)(2,1)} %refs_7_.5, bf16[512,4096]{1,0:T(8,128)(2,1)} %refs_7_.5, ...), custom_call_target="tpu_custom_call" | custom-call | flops 1000 | bytes 1000 | tf_op jit(solution)/shard_map/weight_step/pallas_call | solution.py:357
  87.7 14.9 %attend_grad.1 = (bf16[512,1024]{1,0:T(8,128)(2,1)}, f32[512,1024]{1,0:T(8,128)}, f32[512,1024]{1,0:T(8,128)}, bf16[2,160,1024]{2,1,0:T(8,128)(2,1)S(1)}, bf16[2...) custom-call(s32[1]{0:T(128)} %bitcast.2.pos_ref, bf16[512,1024]{1,0:T(8,128)(2,1)} %q_ref.3, ...), custom_call_target="tpu_custom_call" | custom-call | flops 1000 | bytes 1000 | tf_op jit(solution)/shard_map/attend_grad/pallas_call | solution.py:235
  102.6 2.6 %weight_step.11 = bf16[2,2,512,128]{3,2,1,0:T(8,128)(2,1)S(1)} custom-call(s32[4,16]{1,0:T(4,128)S(1)} %pad_add_fusion.cols_ref, bf16[512,512]{1,0:T(8,128)(2,1)} %copy-done, bf16[512,512]{1,0:T(8,128)(2,1)} %copy-done, bf16[512,4096]{1,0:T(8,128)(2,1)} %refs_7_.5, bf16[512,4096]{1,0:T(8,128)(2,1)} %refs_7_.5, bf16[512,4096]{1,0:T(8,128)(2,1)} %refs_7_.5, ...), custom_call_target="tpu_custom_call" | custom-call | flops 1000 | bytes 1000 | tf_op jit(solution)/shard_map/weight_step/pallas_call | solution.py:357
  107.3 3.4 %weight_step.12 = (bf16[4,2,256,128]{3,2,1,0:T(8,128)(2,1)S(1)}, bf16[4,2,256,128]{3,2,1,0:T(8,128)(2,1)S(1)}) custom-call(s32[4,16]{1,0:T(4,128)S(1)} %pad_add_fusion.cols_ref, bf16[512,512]{1,0:T(8,128)(2,1)} %copy-done.1, bf16[512,512]{1,0:T(8,128)(2,1)} %copy-done.1, bf16[512,4096]{1,0:T(8,128)(2,1)} %refs_7_.5, bf16[512,4096]{1,0:T(8,128)(2,1)} %refs_7_.5, ...), custom_call_target="tpu_custom_call" | custom-call | flops 1000 | bytes 1000 | tf_op jit(solution)/shard_map/weight_step/pallas_call | solution.py:357
  110.7 9.2 %collective-permute-done.14.refs_8_.refs_9_.refs_16_.refs_17_ = bf16[2,2,512,128]{3,2,1,0:T(8,128)(2,1)S(1)} collective-permute-done((bf16[2,2,512,128]{3,2,1,0:T(8,128)(2,1)S(1)}, bf16[2,2,512,128]{3,2,1,0:T(8,128)(2,1)S(1)}, u32[]{:S(2)}, u32[]{:S(2)}) %collective-permute-start.14) | collective-permute-done | bytes 524320 | tf_op jit(solution)/shard_map/ppermute | solution.py:514
  119.9 2.3 %weight_step.13 = bf16[1,2,512,128]{3,2,1,0:T(8,128)(2,1)S(1)} custom-call(s32[4,16]{1,0:T(4,128)S(1)} %pad_add_fusion.cols_ref, bf16[512,512]{1,0:T(8,128)(2,1)} %copy-done, bf16[512,512]{1,0:T(8,128)(2,1)} %copy-done, bf16[512,4096]{1,0:T(8,128)(2,1)} %refs_7_.5, bf16[512,4096]{1,0:T(8,128)(2,1)} %refs_7_.5, bf16[8,2,256,128]{3,2,1,0:T(8,128)(2,1)} %copy-done.2, ...), custom_call_target="tpu_custom_call" | custom-call | flops 1000 | bytes 1000 | tf_op jit(solution)/shard_map/weight_step/pallas_call | solution.py:357
  122.2 3.6 %collective-permute-start.15 = (bf16[2,32,1024]{2,1,0:T(8,128)(2,1)S(1)}, bf16[2,32,1024]{2,1,0:T(8,128)(2,1)S(1)}, u32[]{:S(2)}, u32[]{:S(2)}) collective-permute-start(bf16[2,32,1024]{2,1,0:T(8,128)(2,1)S(1)} %broadcast_select_fusion), channel_id=1, source_target_pairs={{0,64},{4,68},{8,72},{12,76},{16,80},{20,84},{24,88},{28,92},{32,9... | collective-permute-start | bytes 393224 | tf_op jit(solution)/shard_map/ppermute | solution.py:514
  125.8 3.5 %collective-permute-done.15 = bf16[2,32,1024]{2,1,0:T(8,128)(2,1)S(1)} collective-permute-done((bf16[2,32,1024]{2,1,0:T(8,128)(2,1)S(1)}, bf16[2,32,1024]{2,1,0:T(8,128)(2,1)S(1)}, u32[]{:S(2)}, u32[]{:S(2)}) %collective-permute-start.15) | collective-permute-done | bytes 131104 | tf_op jit(solution)/shard_map/ppermute | solution.py:514
  131.1 4.3 %collective-permute-start.8 = (bf16[2,160,1024]{2,1,0:T(8,128)(2,1)}, bf16[2,160,1024]{2,1,0:T(8,128)(2,1)}, u32[]{:S(2)}, u32[]{:S(2)}) collective-permute-start(bf16[2,160,1024]{2,1,0:T(8,128)(2,1)} %get-tuple-element.86), channel_id=1, source_target_pairs={{0,4},{4,8},{8,12},{12,16},{16,20},{20,24},{24,28},{28,32},{32,36}... | collective-permute-start | bytes 1966088 | tf_op jit(solution)/shard_map/ppermute | solution.py:604
  136.8 5.7 %collective-permute-start.20 = (bf16[4,2,256,128]{3,2,1,0:T(8,128)(2,1)S(1)}, bf16[4,2,256,128]{3,2,1,0:T(8,128)(2,1)S(1)}, u32[]{:S(2)}, u32[]{:S(2)}) collective-permute-start(bf16[4,2,256,128]{3,2,1,0:T(8,128)(2,1)S(1)} %get-tuple-element.91), channel_id=1, source_target_pairs={{0,24},{4,28},{8,16},{12,20},{16,8},{20,12},{24,0},{28,4},{32,56},... | collective-permute-start | bytes 1572872 | tf_op jit(solution)/shard_map/ppermute | solution.py:514
  146.1 20.0 %collective-permute-done.20.refs_8_.refs_6_.refs_14_ = bf16[4,2,256,128]{3,2,1,0:T(8,128)(2,1)S(1)} collective-permute-done((bf16[4,2,256,128]{3,2,1,0:T(8,128)(2,1)S(1)}, bf16[4,2,256,128]{3,2,1,0:T(8,128)(2,1)S(1)}, u32[]{:S(2)}, u32[]{:S(2)}) %collective-permute-start.20) | collective-permute-done | bytes 524320 | tf_op jit(solution)/shard_map/ppermute | solution.py:514
  167.1 2.5 %weight_step.14 = bf16[2,2,512,128]{3,2,1,0:T(8,128)(2,1)S(1)} custom-call(s32[4,16]{1,0:T(4,128)S(1)} %pad_add_fusion.cols_ref, bf16[512,512]{1,0:T(8,128)(2,1)} %copy-done.1, bf16[512,512]{1,0:T(8,128)(2,1)} %copy-done.1, bf16[512,4096]{1,0:T(8,128)(2,1)} %refs_7_.5, bf16[512,4096]{1,0:T(8,128)(2,1)} %refs_7_.5, bf16[512,4096]{1,0:T(8,128)(2,1)} %refs_7_.5, ...), custom_call_target="tpu_custom_call" | custom-call | flops 1000 | bytes 1000 | tf_op jit(solution)/shard_map/weight_step/pallas_call | solution.py:357
  170.3 3.1 %collective-permute-start.18 = (bf16[2,4,1024]{2,1,0:T(4,128)(2,1)S(1)}, bf16[2,4,1024]{2,1,0:T(4,128)(2,1)S(1)}, u32[]{:S(2)}, u32[]{:S(2)}) collective-permute-start(bf16[2,4,1024]{2,1,0:T(4,128)(2,1)S(1)} %broadcast_select_fusion.3), channel_id=1, source_target_pairs={{0,8},{4,12},{8,0},{12,4},{16,24},{20,28},{24,16},{28,20},{32,40},... | collective-permute-start | bytes 49160 | tf_op jit(solution)/shard_map/ppermute | solution.py:514
  175.7 8.7 %collective-permute-done.22.refs_8_.refs_9_.refs_18_.refs_19_ = bf16[2,2,512,128]{3,2,1,0:T(8,128)(2,1)S(1)} collective-permute-done((bf16[2,2,512,128]{3,2,1,0:T(8,128)(2,1)S(1)}, bf16[2,2,512,128]{3,2,1,0:T(8,128)(2,1)S(1)}, u32[]{:S(2)}, u32[]{:S(2)}) %collective-permute-start.22) | collective-permute-done | bytes 524320 | tf_op jit(solution)/shard_map/ppermute | solution.py:514
  186.8 2.9 %collective-permute-done.19 = bf16[2,2,1024]{2,1,0:T(2,128)(2,1)S(1)} collective-permute-done((bf16[2,2,1024]{2,1,0:T(2,128)(2,1)S(1)}, bf16[2,2,1024]{2,1,0:T(2,128)(2,1)S(1)}, u32[]{:S(2)}, u32[]{:S(2)}) %collective-permute-start.19) | collective-permute-done | bytes 8224 | tf_op jit(solution)/shard_map/ppermute | solution.py:514
  190.3 4.5 %combine.1 = (bf16[512,1024]{1,0:T(8,128)(2,1)}, bf16[512,1024]{1,0:T(8,128)(2,1)}) custom-call(f32[512,1024]{1,0:T(8,128)} %get-tuple-element.84.gk_ref, f32[512,1024]{1,0:T(8,128)} %get-tuple-element.85.gv_ref, bf16[2,160,1024]{2,1,0:T(8,128)(2,1)} %collective-permute-done.8.left_ref, bf16[2,160,1024]{2,1,0:T(8,128)(2,1)} %collective-permute-done.9.right_ref, ...), custom_call_target="tpu_custom_call" | custom-call | flops 1000 | bytes 1000 | tf_op jit(solution)/shard_map/combine/pallas_call | solution.py:286
  194.8 3.2 %weight_last.1 = (bf16[1024,128]{1,0:T(8,128)(2,1)S(1)}, f32[1024,128]{1,0:T(8,128)S(1)}) custom-call(s32[5]{0:T(128)S(1)} %pad_add_fusion.2.table_ref, bf16[512,512]{1,0:T(8,128)(2,1)} %copy-done, bf16[512,512]{1,0:T(8,128)(2,1)} %copy-done, bf16[512,512]{1,0:T(8,128)(2,1)} %copy-done.1, bf16[512,512]{1,0:T(8,128)(2,1)} %copy-done.1, ...), custom_call_target="tpu_custom_call" | custom-call | flops 1000 | bytes 1000 | tf_op jit(solution)/shard_map/weight_last/pallas_call | solution.py:413
  198.0 4.1 %collective-permute-start.25 = (bf16[1024,128]{1,0:T(8,128)(2,1)S(1)}, bf16[1024,128]{1,0:T(8,128)(2,1)S(1)}, u32[]{:S(2)}, u32[]{:S(2)}) collective-permute-start(bf16[1024,128]{1,0:T(8,128)(2,1)S(1)} %get-tuple-element.100), channel_id=1, source_target_pairs={{0,4},{4,0},{8,12},{12,8},{16,20},{20,16},{24,28},{28,24},{32,36},... | collective-permute-start | bytes 786440 | tf_op jit(solution)/shard_map/ppermute | solution.py:514
  202.0 3.1 %fusion = bf16[512,1024]{1,0:T(8,128)(2,1)} fusion(bf16[512,1024]{1,0:T(8,128)(2,1)} %collective-permute-done.5, bf16[2,512,1024]{2,1,0:T(8,128)(2,1)} %collective-permute-done.4, bf16[2,512,1024]{2,1,0:T(8,128)(2,1)S(1)} %copy-done.14), kind=kLoop, calls=%fused_computation.1 | loop fusion | flops 3145728 | bytes 4194304 | tf_op jit(solution)/shard_map/convert_element_type | solution.py:617
  (117 shorter events, 29.0 us)
Async XLA Ops:
  0.6 24.5 %copy-start.20 = (s32[4]{0:T(128)S(1)}, s32[4]{0:T(128)}, u32[]{:S(2)}) copy-start(s32[4]{0:T(128)} %constant.92.clone) | copy-start | bytes 52
  0.6 24.5 %copy-start.21 = (s32[4]{0:T(128)S(1)}, s32[4]{0:T(128)}, u32[]{:S(2)}) copy-start(s32[4]{0:T(128)} %constant.91.clone) | copy-start | bytes 52
  3.0 22.6 %collective-permute-start = (bf16[2,160,512]{2,1,0:T(8,128)(2,1)}, bf16[2,160,512]{2,1,0:T(8,128)(2,1)S(1)}, u32[]{:S(2)}, u32[]{:S(2)}) collective-permute-start(bf16[2,160,512]{2,1,0:T(8,128)(2,1)} %get-tuple-element.53), channel_id=1, source_target_pairs={{0,4},{4,8},{8,12},{12,16},{16,20},{20,24},{24,28},{28,32},{32,36}... | collective-permute-start | bytes 983048 | tf_op jit(solution)/shard_map/ppermute | solution.py:552
  9.0 16.6 %collective-permute-start.1 = (bf16[2,160,512]{2,1,0:T(8,128)(2,1)}, bf16[2,160,512]{2,1,0:T(8,128)(2,1)S(1)}, u32[]{:S(2)}, u32[]{:S(2)}) collective-permute-start(bf16[2,160,512]{2,1,0:T(8,128)(2,1)} %get-tuple-element.54), channel_id=1, source_target_pairs={{4,0},{8,4},{12,8},{16,12},{20,16},{24,20},{28,24},{32,28},{36,32}... | collective-permute-start | bytes 983048 | tf_op jit(solution)/shard_map/ppermute | solution.py:553
  14.2 21.7 %all-to-all-start = ((bf16[32,2,2,1024]{3,2,1,0:T(2,128)(2,1)}), bf16[32,2,2,1024]{3,2,1,0:T(2,128)(2,1)S(1)}, u32[]{:S(2)}, u32[]{:S(2)}) async-start(bf16[32,2,2,1024]{3,2,1,0:T(2,128)(2,1)} %broadcast_in_dim.27), calls=%async_computation | async-start | bytes 524288 | tf_op jit(solution)/shard_map/all_to_all | solution.py:555
  25.7 12.1 %copy-start.15 = (bf16[2,160,512]{2,1,0:T(8,128)(2,1)}, bf16[2,160,512]{2,1,0:T(8,128)(2,1)S(1)}, u32[]{:S(2)}) copy-start(bf16[2,160,512]{2,1,0:T(8,128)(2,1)S(1)} %collective-permute-done.left_ref.refs_0_) | copy-start | bytes 983044
  25.7 12.1 %copy-start.16 = (bf16[2,160,512]{2,1,0:T(8,128)(2,1)}, bf16[2,160,512]{2,1,0:T(8,128)(2,1)S(1)}, u32[]{:S(2)}) copy-start(bf16[2,160,512]{2,1,0:T(8,128)(2,1)S(1)} %collective-permute-done.1.right_ref.refs_2_) | copy-start | bytes 983044
  25.7 19.3 %collective-permute-start.2 = (bf16[2,160,512]{2,1,0:T(8,128)(2,1)}, bf16[2,160,512]{2,1,0:T(8,128)(2,1)S(1)}, u32[]{:S(2)}, u32[]{:S(2)}) collective-permute-start(bf16[2,160,512]{2,1,0:T(8,128)(2,1)} %get-tuple-element.61), channel_id=1, source_target_pairs={{0,4},{4,8},{8,12},{12,16},{16,20},{20,24},{24,28},{28,32},{32,36}... | collective-permute-start | bytes 983048 | tf_op jit(solution)/shard_map/ppermute | solution.py:552
  30.9 14.0 %collective-permute-start.3 = (bf16[2,160,512]{2,1,0:T(8,128)(2,1)}, bf16[2,160,512]{2,1,0:T(8,128)(2,1)S(1)}, u32[]{:S(2)}, u32[]{:S(2)}) collective-permute-start(bf16[2,160,512]{2,1,0:T(8,128)(2,1)} %get-tuple-element.62), channel_id=1, source_target_pairs={{4,0},{8,4},{12,8},{16,12},{20,16},{24,20},{28,24},{32,28},{36,32}... | collective-permute-start | bytes 983048 | tf_op jit(solution)/shard_map/ppermute | solution.py:553
  42.6 25.0 %copy-start.10 = (bf16[512,512]{1,0:T(8,128)(2,1)}, bf16[512,512]{1,0:T(8,128)(2,1)S(1)}, u32[]{:S(2)}) copy-start(bf16[512,512]{1,0:T(8,128)(2,1)S(1)} %get-tuple-element.72.a0_ref.refs_6_) | copy-start | bytes 1572868
  49.5 33.6 %collective-permute-start.6 = (bf16[8,2,256,128]{3,2,1,0:T(8,128)(2,1)}, bf16[8,2,256,128]{3,2,1,0:T(8,128)(2,1)S(1)}, u32[]{:S(2)}, u32[]{:S(2)}) collective-permute-start(bf16[8,2,256,128]{3,2,1,0:T(8,128)(2,1)} %get-tuple-element.65), channel_id=1, source_target_pairs={{0,32},{4,36},{8,40},{12,44},{16,48},{20,52},{24,56},{28,60},{32,0... | collective-permute-start | bytes 3145736 | tf_op jit(solution)/shard_map/ppermute | solution.py:514
  55.7 27.4 %collective-permute-start.7 = (bf16[8,2,256,128]{3,2,1,0:T(8,128)(2,1)}, bf16[8,2,256,128]{3,2,1,0:T(8,128)(2,1)S(1)}, u32[]{:S(2)}, u32[]{:S(2)}) collective-permute-start(bf16[8,2,256,128]{3,2,1,0:T(8,128)(2,1)} %get-tuple-element.66), channel_id=1, source_target_pairs={{0,96},{4,100},{8,104},{12,108},{16,112},{20,116},{24,120},{28,124... | collective-permute-start | bytes 3145736 | tf_op jit(solution)/shard_map/ppermute | solution.py:514
  67.5 39.8 %collective-permute-start.12 = (bf16[8,2,256,128]{3,2,1,0:T(8,128)(2,1)}, bf16[8,2,256,128]{3,2,1,0:T(8,128)(2,1)}, u32[]{:S(2)}, u32[]{:S(2)}) collective-permute-start(bf16[8,2,256,128]{3,2,1,0:T(8,128)(2,1)} %get-tuple-element.70), channel_id=1, source_target_pairs={{0,8},{4,12},{8,0},{12,4},{16,24},{20,28},{24,16},{28,20},{32,40},... | collective-permute-start | bytes 3145736 | tf_op jit(solution)/shard_map/ppermute | solution.py:514
  67.6 39.7 %collective-permute-start.13 = (bf16[8,2,256,128]{3,2,1,0:T(8,128)(2,1)}, bf16[8,2,256,128]{3,2,1,0:T(8,128)(2,1)}, u32[]{:S(2)}, u32[]{:S(2)}) collective-permute-start(bf16[8,2,256,128]{3,2,1,0:T(8,128)(2,1)} %get-tuple-element.71), channel_id=1, source_target_pairs={{0,24},{4,28},{8,16},{12,20},{16,8},{20,12},{24,0},{28,4},{32,56},... | collective-permute-start | bytes 3145736 | tf_op jit(solution)/shard_map/ppermute | solution.py:514
  86.3 16.3 %collective-permute-start.10 = (bf16[4,2,256,128]{3,2,1,0:T(8,128)(2,1)S(1)}, bf16[4,2,256,128]{3,2,1,0:T(8,128)(2,1)S(1)}, u32[]{:S(2)}, u32[]{:S(2)}) collective-permute-start(bf16[4,2,256,128]{3,2,1,0:T(8,128)(2,1)S(1)} %get-tuple-element.78), channel_id=1, source_target_pairs={{0,96},{4,100},{8,104},{12,108},{16,112},{20,116},{24,120},{28,124... | collective-permute-start | bytes 1572872 | tf_op jit(solution)/shard_map/ppermute | solution.py:514
  87.7 15.0 %collective-permute-start.11 = (bf16[4,2,256,128]{3,2,1,0:T(8,128)(2,1)S(1)}, bf16[4,2,256,128]{3,2,1,0:T(8,128)(2,1)S(1)}, u32[]{:S(2)}, u32[]{:S(2)}) collective-permute-start(bf16[4,2,256,128]{3,2,1,0:T(8,128)(2,1)S(1)} %get-tuple-element.79), channel_id=1, source_target_pairs={{0,32},{4,36},{8,40},{12,44},{16,48},{20,52},{24,56},{28,60},{32,0... | collective-permute-start | bytes 1572872 | tf_op jit(solution)/shard_map/ppermute | solution.py:514
  87.7 55.6 %collective-permute-start.4 = (bf16[2,512,1024]{2,1,0:T(8,128)(2,1)}, bf16[2,512,1024]{2,1,0:T(8,128)(2,1)}, u32[]{:S(2)}, u32[]{:S(2)}) collective-permute-start(bf16[2,512,1024]{2,1,0:T(8,128)(2,1)} %get-tuple-element.75), channel_id=1, source_target_pairs={{0,1},{1,0},{2,3},{3,2},{4,5},{5,4},{6,7},{7,6},{8,9},{9,8},{10,11... | collective-permute-start | bytes 6291464 | tf_op jit(solution)/shard_map/ppermute | solution.py:514
  105.2 14.7 %collective-permute-start.14 = (bf16[2,2,512,128]{3,2,1,0:T(8,128)(2,1)S(1)}, bf16[2,2,512,128]{3,2,1,0:T(8,128)(2,1)S(1)}, u32[]{:S(2)}, u32[]{:S(2)}) collective-permute-start(bf16[2,2,512,128]{3,2,1,0:T(8,128)(2,1)S(1)} %weight_step.11), channel_id=1, source_target_pairs={{0,8},{4,12},{8,0},{12,4},{16,24},{20,28},{24,16},{28,20},{32,40},... | collective-permute-start | bytes 1572872 | tf_op jit(solution)/shard_map/ppermute | solution.py:514
  122.2 7.1 %collective-permute-start.15 = (bf16[2,32,1024]{2,1,0:T(8,128)(2,1)S(1)}, bf16[2,32,1024]{2,1,0:T(8,128)(2,1)S(1)}, u32[]{:S(2)}, u32[]{:S(2)}) collective-permute-start(bf16[2,32,1024]{2,1,0:T(8,128)(2,1)S(1)} %broadcast_select_fusion), channel_id=1, source_target_pairs={{0,64},{4,68},{8,72},{12,76},{16,80},{20,84},{24,88},{28,92},{32,9... | collective-permute-start | bytes 393224 | tf_op jit(solution)/shard_map/ppermute | solution.py:514
  129.4 13.1 %collective-permute-start.16 = (bf16[2,16,1024]{2,1,0:T(8,128)(2,1)S(1)}, bf16[2,16,1024]{2,1,0:T(8,128)(2,1)S(1)}, u32[]{:S(2)}, u32[]{:S(2)}) collective-permute-start(bf16[2,16,1024]{2,1,0:T(8,128)(2,1)S(1)} %broadcast_select_fusion.1), channel_id=1, source_target_pairs={{0,32},{4,36},{8,40},{12,44},{16,48},{20,52},{24,56},{28,60},{32,0... | collective-permute-start | bytes 196616 | tf_op jit(solution)/shard_map/ppermute | solution.py:514
  131.1 42.5 %collective-permute-start.8 = (bf16[2,160,1024]{2,1,0:T(8,128)(2,1)}, bf16[2,160,1024]{2,1,0:T(8,128)(2,1)}, u32[]{:S(2)}, u32[]{:S(2)}) collective-permute-start(bf16[2,160,1024]{2,1,0:T(8,128)(2,1)} %get-tuple-element.86), channel_id=1, source_target_pairs={{0,4},{4,8},{8,12},{12,16},{16,20},{20,24},{24,28},{28,32},{32,36}... | collective-permute-start | bytes 1966088 | tf_op jit(solution)/shard_map/ppermute | solution.py:604
  135.5 38.5 %collective-permute-start.9 = (bf16[2,160,1024]{2,1,0:T(8,128)(2,1)S(1)}, bf16[2,160,1024]{2,1,0:T(8,128)(2,1)}, u32[]{:S(2)}, u32[]{:S(2)}) collective-permute-start(bf16[2,160,1024]{2,1,0:T(8,128)(2,1)S(1)} %get-tuple-element.87), channel_id=1, source_target_pairs={{4,0},{8,4},{12,8},{16,12},{20,16},{24,20},{28,24},{32,28},{36,32}... | collective-permute-start | bytes 1966088 | tf_op jit(solution)/shard_map/ppermute | solution.py:605
  136.8 29.3 %collective-permute-start.20 = (bf16[4,2,256,128]{3,2,1,0:T(8,128)(2,1)S(1)}, bf16[4,2,256,128]{3,2,1,0:T(8,128)(2,1)S(1)}, u32[]{:S(2)}, u32[]{:S(2)}) collective-permute-start(bf16[4,2,256,128]{3,2,1,0:T(8,128)(2,1)S(1)} %get-tuple-element.91), channel_id=1, source_target_pairs={{0,24},{4,28},{8,16},{12,20},{16,8},{20,12},{24,0},{28,4},{32,56},... | collective-permute-start | bytes 1572872 | tf_op jit(solution)/shard_map/ppermute | solution.py:514
  142.5 24.7 %collective-permute-start.21 = (bf16[4,2,256,128]{3,2,1,0:T(8,128)(2,1)S(1)}, bf16[4,2,256,128]{3,2,1,0:T(8,128)(2,1)S(1)}, u32[]{:S(2)}, u32[]{:S(2)}) collective-permute-start(bf16[4,2,256,128]{3,2,1,0:T(8,128)(2,1)S(1)} %get-tuple-element.92), channel_id=1, source_target_pairs={{0,8},{4,12},{8,0},{12,4},{16,24},{20,28},{24,16},{28,20},{32,40},... | collective-permute-start | bytes 1572872 | tf_op jit(solution)/shard_map/ppermute | solution.py:514
  143.2 27.1 %collective-permute-start.17 = (bf16[2,8,1024]{2,1,0:T(8,128)(2,1)S(1)}, bf16[2,8,1024]{2,1,0:T(8,128)(2,1)S(1)}, u32[]{:S(2)}, u32[]{:S(2)}) collective-permute-start(bf16[2,8,1024]{2,1,0:T(8,128)(2,1)S(1)} %broadcast_select_fusion.2), channel_id=1, source_target_pairs={{0,16},{4,20},{8,24},{12,28},{16,0},{20,4},{24,8},{28,12},{32,48},... | collective-permute-start | bytes 98312 | tf_op jit(solution)/shard_map/ppermute | solution.py:514
  166.1 36.0 %collective-permute-start.5 = (bf16[512,1024]{1,0:T(8,128)(2,1)S(1)}, bf16[512,1024]{1,0:T(8,128)(2,1)}, u32[]{:S(2)}, u32[]{:S(2)}) collective-permute-start(bf16[512,1024]{1,0:T(8,128)(2,1)S(1)} %fusion.1), channel_id=1, source_target_pairs={{0,2},{1,3},{2,0},{3,1},{4,6},{5,7},{6,4},{7,5},{8,10},{9,11},{10,... | collective-permute-start | bytes 3145736 | tf_op jit(solution)/shard_map/ppermute | solution.py:514
  169.7 14.7 %collective-permute-start.22 = (bf16[2,2,512,128]{3,2,1,0:T(8,128)(2,1)S(1)}, bf16[2,2,512,128]{3,2,1,0:T(8,128)(2,1)S(1)}, u32[]{:S(2)}, u32[]{:S(2)}) collective-permute-start(bf16[2,2,512,128]{3,2,1,0:T(8,128)(2,1)S(1)} %weight_step.14), channel_id=1, source_target_pairs={{0,96},{4,100},{8,104},{12,108},{16,112},{20,116},{24,120},{28,124... | collective-permute-start | bytes 1572872 | tf_op jit(solution)/shard_map/ppermute | solution.py:514
  170.3 4.9 %collective-permute-start.18 = (bf16[2,4,1024]{2,1,0:T(4,128)(2,1)S(1)}, bf16[2,4,1024]{2,1,0:T(4,128)(2,1)S(1)}, u32[]{:S(2)}, u32[]{:S(2)}) collective-permute-start(bf16[2,4,1024]{2,1,0:T(4,128)(2,1)S(1)} %broadcast_select_fusion.3), channel_id=1, source_target_pairs={{0,8},{4,12},{8,0},{12,4},{16,24},{20,28},{24,16},{28,20},{32,40},... | collective-permute-start | bytes 49160 | tf_op jit(solution)/shard_map/ppermute | solution.py:514
  173.6 21.2 %collective-permute-start.23 = (bf16[1,2,512,128]{3,2,1,0:T(8,128)(2,1)S(1)}, bf16[1,2,512,128]{3,2,1,0:T(8,128)(2,1)S(1)}, u32[]{:S(2)}, u32[]{:S(2)}) collective-permute-start(bf16[1,2,512,128]{3,2,1,0:T(8,128)(2,1)S(1)} %weight_step.13), channel_id=1, source_target_pairs={{0,24},{4,28},{8,16},{12,20},{16,8},{20,12},{24,0},{28,4},{32,56},... | collective-permute-start | bytes 786440 | tf_op jit(solution)/shard_map/ppermute | solution.py:514
  175.2 14.5 %collective-permute-start.19 = (bf16[2,2,1024]{2,1,0:T(2,128)(2,1)S(1)}, bf16[2,2,1024]{2,1,0:T(2,128)(2,1)S(1)}, u32[]{:S(2)}, u32[]{:S(2)}) collective-permute-start(bf16[2,2,1024]{2,1,0:T(2,128)(2,1)S(1)} %broadcast_select_fusion.4), channel_id=1, source_target_pairs={{0,4},{4,0},{8,12},{12,8},{16,20},{20,16},{24,28},{28,24},{32,36},... | collective-permute-start | bytes 24584 | tf_op jit(solution)/shard_map/ppermute | solution.py:514
  186.6 8.1 %collective-permute-start.24 = (bf16[1,2,512,128]{3,2,1,0:T(8,128)(2,1)S(1)}, bf16[1,2,512,128]{3,2,1,0:T(8,128)(2,1)S(1)}, u32[]{:S(2)}, u32[]{:S(2)}) collective-permute-start(bf16[1,2,512,128]{3,2,1,0:T(8,128)(2,1)S(1)} %weight_step.15), channel_id=1, source_target_pairs={{0,32},{4,36},{8,40},{12,44},{16,48},{20,52},{24,56},{28,60},{32,0... | collective-permute-start | bytes 786440 | tf_op jit(solution)/shard_map/ppermute | solution.py:514
  198.0 9.2 %collective-permute-start.25 = (bf16[1024,128]{1,0:T(8,128)(2,1)S(1)}, bf16[1024,128]{1,0:T(8,128)(2,1)S(1)}, u32[]{:S(2)}, u32[]{:S(2)}) collective-permute-start(bf16[1024,128]{1,0:T(8,128)(2,1)S(1)} %get-tuple-element.100), channel_id=1, source_target_pairs={{0,4},{4,0},{8,12},{12,8},{16,20},{20,16},{24,28},{28,24},{32,36},... | collective-permute-start | bytes 786440 | tf_op jit(solution)/shard_map/ppermute | solution.py:514
  (17 other events, 76.0 us)

commit v4 on v3

--- a/solution.py
+++ b/solution.py
@@ -17,7 +17,7 @@
 NEG = -1e30
 LOG2E = math.log2(math.e)
 MB = 1024 * 1024
-HALVES = 2
+HALVES = 1
 BIG = 20
 SMALL = pl.CostEstimate(flops=1000, bytes_accessed=1000, transcendentals=0)
 
@@ -203,41 +203,23 @@
     )(pos, *pinned(q, k, v, left, right, near, far, bias))
 
 
-def bwd_halves_kernel(seq_count, pos_ref, q_ref, k_ref, v_ref, *refs):
-    per = pl.num_programs(0) // HALVES
-    first = pl.program_id(0) < per
-    pairs, rest = refs[: 5 * HALVES], refs[5 * HALVES :]
-    picked = [jnp.where(first, pairs[2 * i][...], pairs[2 * i + 1][...]) for i in range(5)]
-    left, right, near, att, lse = picked
-    far_ref, bias_ref, do_ref, *outs = rest
-    bwd_kernel(seq_count, pos_ref, q_ref, k_ref, v_ref, left, right, near, far_ref, bias_ref, do_ref, att, lse, *outs)
-
-
 def backward(seq_count, pos, q, k, v, left, right, near, far, bias, do, att, lse):
     tokens, feats = q.shape
     heads = feats // DH
-    per = heads // HALVES
-    halo, nr, fr = left[0].shape[1], near[0].shape[1], far.shape[1]
+    halo, nr, fr = left.shape[1], near.shape[1], far.shape[1]
     coarse = 3 * nr + fr
     tok = pl.BlockSpec((tokens, DH), lambda h, *_: (0, h))
     lev = lambda r: pl.BlockSpec((2, r, DH), lambda h, *_: (0, 0, h))
-    at = (lambda h: jnp.minimum(h, per - 1), lambda h: jnp.maximum(h - per, 0))
-    pairs, pair_specs = [], []
-    for x in (left, right, near, att, lse):
-        for half, pick in enumerate(at):
-            pairs.append(x[half])
-            if x is att:
-                pair_specs.append(pl.BlockSpec((tokens, DH), lambda h, *_, p=pick: (0, p(h))))
-            elif x is lse:
-                pair_specs.append(pl.BlockSpec((1, 1, tokens), lambda h, *_, p=pick: (p(h), 0, 0)))
-            else:
-                pair_specs.append(pl.BlockSpec((2, x[half].shape[1], DH), lambda h, *_, p=pick: (0, 0, p(h))))
-    return pl.pallas_call(
-        functools.partial(bwd_halves_kernel, seq_count),
+    return pl.pallas_call(
+        functools.partial(bwd_kernel, seq_count),
         grid_spec=pltpu.PrefetchScalarGridSpec(
             num_scalar_prefetch=1,
             grid=(heads,),
-            in_specs=[tok, tok, tok, *pair_specs, lev(fr), pl.BlockSpec(bias.shape, lambda h, *_: (0, 0, 0)), tok],
+            in_specs=[
+                *[tok, tok, tok, lev(halo), lev(halo), lev(nr), lev(fr)],
+                pl.BlockSpec(bias.shape, lambda h, *_: (0, 0, 0)),
+                *[tok, tok, pl.BlockSpec((1, 1, tokens), lambda h, *_: (h, 0, 0))],
+            ],
             out_specs=[tok, tok, tok, lev(halo), lev(halo), lev(fr)],
             scratch_shapes=[
                 pltpu.VMEM((tokens + 2 * FB, tokens), BF),
@@ -257,7 +239,7 @@
         compiler_params=params(BIG),
         cost_estimate=SMALL,
         name="attend_grad",
-    )(pos, *pinned(q, k, v, *pairs, far, bias), do)
+    )(pos, *pinned(q, k, v, left, right, near, far, bias), do, att, lse)
 
 
 def combine_kernel(gk_ref, gv_ref, left_ref, right_ref, far_ref, ok_ref, ov_ref):
@@ -420,30 +402,8 @@
     )(table, *args)
 
 
-def project_kernel(og_ref, w_ref, o_ref):
-    n = o_ref.shape[1]
-    at = pl.multiple_of(pl.program_id(0) * n, n)
-    o_ref[...] = dot(og_ref[...], w_ref[pl.ds(at, n), :], 1, 1).astype(BF)
-
-
-def project(og, w):
-    tokens, feats = og.shape[0], w.shape[0]
-    n = 256
-    return pl.pallas_call(
-        project_kernel,
-        grid=(feats // n,),
-        in_specs=[pl.BlockSpec(memory_space=pltpu.VMEM)] * 2,
-        out_specs=pl.BlockSpec((tokens, n), lambda j: (0, j)),
-        out_shape=jax.ShapeDtypeStruct((tokens, feats), BF),
-        compiler_params=params(BIG),
-        cost_estimate=SMALL,
-        name="project",
-    )(og, w)
-
-
-def project_kernel(cols_ref, a0_ref, a1_ref, og_ref, w_ref, send_ref, keep_ref, grad_ref, acc_ref):
+def project_kernel(og_ref, w_ref, o_ref, acc_ref):
     step = pl.program_id(0)
-    half = a0_ref.shape[1]
     part = dot(og_ref[...], w_ref[...], 1, 1)
 
     @pl.when(step == 0)
@@ -454,59 +414,65 @@
     def _():
         acc_ref[...] += part
 
-    res = (dot(a0_ref[...], w_ref[:half], 1, 0) + dot(a1_ref[...], w_ref[half:], 1, 0)).astype(BF)
-
-    @pl.when(step < pl.num_programs(0) // 2)
-    def _():
-        send_ref[0] = res
-
-    @pl.when(step >= pl.num_programs(0) // 2)
-    def _():
-        keep_ref[0] = res
-
     @pl.when(step == pl.num_programs(0) - 1)
     def _():
-        grad_ref[...] = acc_ref[...].astype(BF)
-
-
-def project(cols, att, og, w, width):
-    tokens, half = att[0].shape
-    feats = w.shape[0]
-    sub = 1
-    n = width // sub
+        o_ref[...] = acc_ref[...].astype(BF)
+
+
+def project(og, w):
+    tokens, feats = og.shape[0], w.shape[0]
+    n = 1024
+    return pl.pallas_call(
+        project_kernel,
+        grid=(w.shape[1] // n,),
+        in_specs=[pl.BlockSpec((tokens, n), lambda s: (0, s)), pl.BlockSpec((feats, n), lambda s: (0, s))],
+        out_specs=pl.BlockSpec((tokens, feats), lambda s: (0, 0)),
+        out_shape=pltpu.HBM((tokens, feats), BF),
+        scratch_shapes=[pltpu.VMEM((tokens, feats), F32)],
+        compiler_params=params(BIG),
+        cost_estimate=SMALL,
+        name="project",
+    )(*pinned(og, w))
+
+
+def layer_kernel(cols_ref, att_ref, w_ref, *part_refs):
+    res = dot(att_ref[...], w_ref[...], 1, 0).astype(BF)
+    top_ref, bottom_ref, *rest = part_refs
+    rows = top_ref.shape[0]
+
+    @pl.when(pl.program_id(0) == 0)
+    def _():
+        top_ref[...] = res[:rows]
+        bottom_ref[...] = res[rows:]
+
+    for i, ref in enumerate(rest):
+
+        @pl.when(pl.program_id(0) == i + 1)
+        def _(ref=ref):
+            ref[...] = res
+
+
+def layer_parts(cols, att, w, width):
+    tokens, feats = att.shape
     parts = cols.shape[0]
-    steps = parts * sub
-    mid = steps // 2
     whole = lambda r, c: pl.BlockSpec((r, c), lambda s, *_: (0, 0))
-    first = lambda s: jnp.minimum(s, mid - 1)
-    later = lambda s: jnp.maximum(s - mid, 0)
-    return pl.pallas_call(
-        project_kernel,
+    return pl.pallas_call(
+        layer_kernel,
         grid_spec=pltpu.PrefetchScalarGridSpec(
             num_scalar_prefetch=1,
-            grid=(steps,),
-            in_specs=[
-                whole(tokens, half),
-                whole(tokens, half),
-                pl.BlockSpec((tokens, n), lambda s, c: (0, c[s // sub] * sub + s % sub)),
-                pl.BlockSpec((feats, n), lambda s, c: (0, c[s // sub] * sub + s % sub)),
-            ],
-            out_specs=[
-                pl.BlockSpec((1, tokens, n), lambda s, *_: (first(s) // sub, 0, first(s) % sub)),
-                pl.BlockSpec((1, tokens, n), lambda s, *_: (later(s) // sub, 0, later(s) % sub)),
-                whole(tokens, feats),
-            ],
-            scratch_shapes=[pltpu.VMEM((tokens, feats), F32)],
+            grid=(parts,),
+            in_specs=[whole(tokens, feats), pl.BlockSpec((feats, width), lambda s, c: (0, c[s]))],
+            out_specs=[whole(tokens // 2, width)] * 2 + [whole(tokens, width)] * (parts - 1),
         ),
         out_shape=[
-            jax.ShapeDtypeStruct((parts // 2, tokens, width), BF),
-            pltpu.HBM((parts // 2, tokens, width), BF),
-            jax.ShapeDtypeStruct((tokens, feats), BF),
+            *[jax.ShapeDtypeStruct((tokens // 2, width), BF)] * 2,
+            jax.ShapeDtypeStruct((tokens, width), BF),
+            *[pltpu.HBM((tokens, width), BF)] * (parts - 2),
         ],
         compiler_params=params(BIG),
         cost_estimate=SMALL,
-        name="project",
-    )(cols, *att, *pinned(og, w))
+        name="layer_parts",
+    )(cols, att, *pinned(w))
 
 
 def swap(x, axis, bits):
@@ -516,6 +482,10 @@
 
 def after(x, *deps):
     return lax.optimization_barrier((x, *deps))[0]
+
+
+def add(a, b):
+    return (a.astype(F32) + b.astype(F32)).astype(BF)
 
 
 def own_rows(x, pos, seq_count):
@@ -542,79 +512,66 @@
     right_perm = [(i, i + 1) for i in range(seq_count - 1)]
     left_perm = [(i + 1, i) for i in range(seq_count - 1)]
 
-    pools = [pool(token_keys, token_values, half) for half in range(HALVES)]
-    near = [p[0] for p in pools]
-    far_own = jnp.concatenate([p[1] for p in pools], axis=2)
-    from_left, from_right = [], []
-    for half, (_, _, to_left, to_right) in enumerate(pools):
-        if half > 0:
-            to_left, to_right = lax.optimization_barrier((to_left, to_right, from_left[0], from_right[0]))[:2]
-        from_left.append(lax.ppermute(to_right, "seq", right_perm))
-        from_right.append(lax.ppermute(to_left, "seq", left_perm))
-    far_all = jnp.broadcast_to(far_own, (seq_count, *far_own.shape))
+    near, far_own, to_left, to_right = pool(token_keys, token_values, 0)
+    from_left = lax.ppermute(to_right, "seq", right_perm)
+    from_right = lax.ppermute(to_left, "seq", left_perm)
+    attn_grad = project(after(out_grad, far_own), out_weight)
+    far_all = jnp.broadcast_to(after(far_own, attn_grad), (seq_count, *far_own.shape))
     far_all = lax.all_to_all(far_all, "seq", 0, 0, tiled=True)
     far = jnp.moveaxis(far_all, 0, 1).reshape(2, -1, feats)
-    bias = level_bias(pos, tokens // FB, near[0].shape[1], far.shape[1], tokens, seq_count)
+    bias = level_bias(pos, tokens // FB, near.shape[1], far.shape[1], tokens, seq_count)
+    att, attt, lse = forward(
+        seq_count, pos1, after(queries, attn_grad), token_keys, token_values, from_left, from_right, near, far, bias, 0
+    )
 
     part = width // seq_count
     cols = block_order(pos)
-    recv1, recv2 = [None] * UNITS, [None] * UNITS
-    att, attt, lse = [], [], []
-    half_units = [list(range(h * UNITS // HALVES, (h + 1) * UNITS // HALVES)) for h in range(HALVES)]
-    out = None
-    for h, units in enumerate(half_units):
-        q = queries if out is None else after(queries, *out)
-        a, at, ls = forward(seq_count, pos1, q, token_keys, token_values, from_left[h], from_right[h], near[h], far, bias, h)
-        att.append(a)
-        attt.append(at)
-        lse.append(ls)
-        table = after(cols, from_left[1], from_right[1]) if h == 0 else cols
-        out = weight_step(table, attt, out_grad, part, units, 8, 8, 4, [], False)
-        for u, x in zip(units, out):
-            recv1[u] = (swap(x, "seq", ROUTE[u][1] << SHIFT[ROUTE[u][0]]), False)
-
-    def second(pair, dep):
-        out = weight_step(after(cols, *dep), attt, out_grad, part, half_units[pair], 4, 4, 2, [recv1], False)
-        for u, x in zip(half_units[pair], out):
-            recv2[u] = (swap(x, "seq", ROUTE[u][2] << SHIFT[ROUTE[u][0]]), False)
+    every = list(range(UNITS))
+    recv1, recv2, recv3, recv4 = ([None] * UNITS for _ in range(4))
+    attt = [attt]
+
+    def first_axis(step, dep):
+        start, per = (8, 2) if step == 0 else (4, 2)
+        got = [recv1][:step]
+        out = weight_step(after(cols, *dep), attt, out_grad, part, every, start, start, per, got, False)
+        for u, x in enumerate(out):
+            (recv1, recv2)[step][u] = (swap(x, "seq", ROUTE[u][1 + step] << SHIFT[ROUTE[u][0]]), False)
         return out
 
-    recv3, recv4 = [None] * UNITS, [None] * UNITS
-
-    def along_other(pair, step, dep):
+    def second_axis(step, dep):
+        start = 2 - step
         got = [recv1, recv2, recv3][: 2 + step]
-        start = 2 - step
-        out = weight_step(after(cols, *dep), attt, out_grad, part, half_units[pair], start, start, start, got, True)
-        moved = swap(out[0], "seq", SECOND[pair][step] << SHIFT[1 - ROUTE[2 * pair][0]])
-        for u in half_units[pair]:
-            (recv3, recv4)[step][u] = (moved, True)
+        out = weight_step(after(cols, *dep), attt, out_grad, part, every, start, start, start, got, True)
+        for p, x in enumerate(out):
+            moved = swap(x, "seq", SECOND[p][step] << SHIFT[1 - ROUTE[2 * p][0]])
+            (recv3, recv4)[step][2 * p : 2 * p + 2] = [(moved, True)] * 2
         return out
 
-    c, zl = tp & 1, tp >> 1
-    lwidth = width // tp_count
-    lcols = jnp.stack([zl, zl ^ 1]) * 2
-    lorder = jnp.concatenate([lcols + (c ^ 1), lcols + c])
-    lsend1, lkeep, attn_grad = project(lorder, (after(att[0], *out), att[1]), out_grad, out_weight, lwidth)
-    lgot1 = swap(lsend1, "tp", 1)
-
-    out = second(0, [attn_grad])
+    out = first_axis(0, [])
     dq, gk, gv, sl, sr, gfar = backward(
         seq_count, pos1, after(queries, *out), token_keys, token_values, from_left, from_right, near, far, bias, attn_grad, att, lse
     )
     back_left = lax.ppermute(sr, "seq", right_perm)
     back_right = lax.ppermute(sl, "seq", left_perm)
-    out = along_other(0, 0, [gfar])
-    out = second(1, out)
-    lsend2 = (lkeep[1].astype(F32) + lgot1[1].astype(F32)).astype(BF)
+    out = first_axis(1, [gfar])
+
+    c, zl = tp & 1, tp >> 1
+    lwidth = width // tp_count
+    lcols = jnp.stack([zl ^ 1, zl]) * 2
+    lorder = jnp.concatenate([lcols + (c ^ 1), lcols + c])
+    top_send, bottom_send, own_send, far_keep, own_keep = layer_parts(lorder, after(att, *out), out_weight, lwidth)
+    far_got = jnp.concatenate([swap(top_send, "tp", 1), swap(bottom_send, "tp", 1)])
+    own_got = swap(own_send, "tp", 1)
+    out = second_axis(0, [top_send, back_left, back_right])
+    lsend2 = add(after(far_keep, *out), far_got)
     lgot2 = swap(lsend2, "tp", 2)
-    out = along_other(0, 1, out)
-    far_sum = own_rows(after(gfar, *out), pos, seq_count)
-    out = along_other(1, 0, out)
-    out = along_other(1, 1, [*out, back_left, back_right])
+    far_parts = jnp.moveaxis(after(gfar, *out).reshape(2, seq_count, -1, feats), 1, 0)
+    far_sum = lax.all_to_all(far_parts, "seq", 0, 0, tiled=True).astype(F32).sum(axis=0)
+    out = second_axis(1, [*out])
     got = [recv1, recv2, recv3, recv4]
     zsend, zkeep = weight_last(cols, attt, out_grad, part, pos & 1, got)
     zgot = swap(zsend, "seq", 1)
-    layer_out = (lkeep[0].astype(F32) + lgot1[0].astype(F32) + lgot2.astype(F32)).astype(BF)
+    layer_out = (own_keep.astype(F32) + own_got.astype(F32) + lgot2.astype(F32)).astype(BF)
     key_grad, value_grad = combine(gk, gv, back_left, back_right, far_sum)
     weight_grad = (zkeep + zgot.astype(F32)) * (1.0 / math.sqrt(tokens * seq_count))
     return layer_out, dq, key_grad, value_grad, weight_grad

time: 210 us -> 181 us (0.86)
  starting transfers between devices: 64.6 us -> 53.7 us
  waiting for transfers between devices: 53.4 us -> 42.7 us
  Pallas kernels: 77.7 us -> 71.6 us
  local copies, waits for them, and re-layouts: 3.33 us -> 5.83 us
  other arithmetic: 7.81 us -> 5.64 us
    ppermute x20 -> x17, waiting for transfers between devices: 47.5 us -> 15.9 us  [swap(): return lax.ppermute(x, axis, [(i, i ^ bits) for i in range(n)])]
    ppermute x20 -> x17, starting transfers between devices: 34.3 us -> 20.2 us  [swap(): return lax.ppermute(x, axis, [(i, i ^ bits) for i in range(n)])]
    ppermute x1, waiting for transfers between devices: 0.01 us -> 12.8 us  [shards(): back_left = lax.ppermute(sr, 'seq', right_perm)]
    all_to_all x0 -> x1, starting transfers between devices: none -> 9.34 us  [shards(): lax.all_to_all(far_parts, 'seq', 0, 0, tiled=True).astype(F32).sum(axis=0)]
    pallas_call x8 -> x4, Pallas kernels: 25.2 us -> 17.6 us  [weight_step(): pl.pallas_call(functools.partial(weight_kernel, n, per, len(recvs) * n, p...]
    ppermute x4 -> x2, starting transfers between devices: 13.8 us -> 7.18 us  [the longest x1 5.89 us: shards(): from_left = lax.ppermute(to_right, 'seq', right_perm)]
    all_to_all x1, waiting for transfers between devices: 3.57 us -> 10 us  [shards(): far_all = lax.all_to_all(far_all, 'seq', 0, 0, tiled=True)]
    all_to_all x0 -> x1, waiting for transfers between devices: none -> 3.99 us  [shards(): lax.all_to_all(far_parts, 'seq', 0, 0, tiled=True).astype(F32).sum(axis=0)]
  transfers between devices with their start and end apart: 27 -> 23, of which waited for: 9 -> 9; matrix products, arithmetic and copies ran while one was open for 5% -> 3% of each run, Pallas kernels for 34% -> 29%
where the time goes in v4:
time: 181 us
  Pallas kernels  71.6 us (40%)
  starting transfers between devices  53.7 us (30%)
  waiting for transfers between devices  42.7 us (24%)
  local copies, waits for them, and re-layouts  5.83 us (3%)
  other arithmetic  5.64 us (3%)
    ppermute x17, starting transfers between devices, swap(): return lax.ppermute(x, axis, [(i, i ^ bits) for i in range(n)])  20.2 us
    pallas_call x4, Pallas kernels, weight_step(): pl.pallas_call(functools.partial(weight_kernel, n, per, len(recvs) * n, p...  17.6 us
    ppermute x17, waiting for transfers between devices, swap(): return lax.ppermute(x, axis, [(i, i ^ bits) for i in range(n)])  15.9 us
    pallas_call x1, Pallas kernels, backward(): pl.pallas_call(functools.partial(bwd_kernel, seq_count), grid_spec=pltpu....  14.4 us
    ppermute x1, waiting for transfers between devices, shards(): back_left = lax.ppermute(sr, 'seq', right_perm)  12.8 us
    all_to_all x1, starting transfers between devices, shards(): far_all = lax.all_to_all(far_all, 'seq', 0, 0, tiled=True)  10.9 us
    all_to_all x1, waiting for transfers between devices, shards(): far_all = lax.all_to_all(far_all, 'seq', 0, 0, tiled=True)  10 us
    pallas_call x1, Pallas kernels, layer_parts(): pl.pallas_call(layer_kernel, grid_spec=pltpu.PrefetchScalarGridSpec(num_s...  9.61 us
  transfers between devices with their start and end apart: 23, of which 9 were waited for; matrix products, arithmetic and copies ran while one was open for 3% of the time, Pallas kernels for 29%

profile of v4, /device:TPU:0, one launch (start us, length us, event | category | flops | bytes accessed | tf_op | source)
XLA Modules:
  0.0 180.5 jit_solution(10412175011870795278)
XLA Ops:
  0.6 4.1 %pool.1 = (bf16[2,32,1024]{2,1,0:T(8,128)(2,1)}, bf16[2,2,1024]{2,1,0:T(2,128)(2,1)}, bf16[2,160,1024]{2,1,0:T(8,128)(2,1)}, bf16[2,160,1024]{2,1,0:T(8,128)(2,1)}) custom-call(bf16[512,1024]{1,0:T(8,128)(2,1)} %k_ref.5, bf16[512,1024]{1,0:T(8,128)(2,1)} %v_ref.5), custom_call_target="tpu_custom_call" | custom-call | flops 1000 | bytes 1000 | tf_op jit(solution)/shard_map/pool/pallas_call | solution.py:59
  4.8 5.9 %collective-permute-start = (bf16[2,160,1024]{2,1,0:T(8,128)(2,1)}, bf16[2,160,1024]{2,1,0:T(8,128)(2,1)S(1)}, u32[]{:S(2)}, u32[]{:S(2)}) collective-permute-start(bf16[2,160,1024]{2,1,0:T(8,128)(2,1)} %get-tuple-element.52), channel_id=1, source_target_pairs={{0,4},{4,8},{8,12},{12,16},{16,20},{20,24},{24,28},{28,32},{32,36}... | collective-permute-start | bytes 1966088 | tf_op jit(solution)/shard_map/ppermute | solution.py:516
  10.7 1.3 collective-permute-start.1
  12.0 9.4 %project.1.do_ref = bf16[512,1024]{1,0:T(8,128)(2,1)} custom-call(bf16[512,4096]{1,0:T(8,128)(2,1)} %refs_7_.9, bf16[1024,4096]{1,0:T(8,128)(2,1)} %w_ref.3), custom_call_target="tpu_custom_call" | custom-call | flops 1000 | bytes 1000 | tf_op jit(solution)/shard_map/project/pallas_call | solution.py:425
  22.3 10.9 %all-to-all-start = ((bf16[32,2,2,1024]{3,2,1,0:T(2,128)(2,1)}), bf16[32,2,2,1024]{3,2,1,0:T(2,128)(2,1)S(1)}, u32[]{:S(2)}, u32[]{:S(2)}) async-start(bf16[32,2,2,1024]{3,2,1,0:T(2,128)(2,1)} %broadcast_in_dim.27), calls=%async_computation | async-start | bytes 524288 | tf_op jit(solution)/shard_map/all_to_all | solution.py:520
  33.8 10.0 %all-to-all-done = bf16[32,2,2,1024]{3,2,1,0:T(2,128)(2,1)S(1)} async-done(((bf16[32,2,2,1024]{3,2,1,0:T(2,128)(2,1)}), bf16[32,2,2,1024]{3,2,1,0:T(2,128)(2,1)S(1)}, u32[]{:S(2)}, u32[]{:S(2)}) %all-to-all-start) | async-done | bytes 262176 | tf_op jit(solution)/shard_map/all_to_all | solution.py:520
  46.0 8.7 %attend.1 = (bf16[512,1024]{1,0:T(8,128)(2,1)S(1)}, bf16[1024,512]{1,0:T(8,128)(2,1)S(1)}, f32[8,1,512]{2,1,0:T(1,128)S(1)}) custom-call(s32[1]{0:T(128)} %bitcast.2.pos_ref, bf16[512,1024]{1,0:T(8,128)(2,1)} %q_ref.1, bf16[512,1024]{1,0:T(8,128)(2,1)} %k_ref.5, bf16[512,1024]{1,0:T(8,128)(2,1)} %v_ref.5, bf16[2,160,1024]{2,1,0:T(8,128)(2,1)} %copy-done.14, ...), custom_call_target="tpu_custom_call" | custom-call | flops 1000 | bytes 1000 | tf_op jit(solution)/shard_map/attend/pallas_call | solution.py:183
  54.7 6.8 %weight_step.4 = (bf16[8,2,256,128]{3,2,1,0:T(8,128)(2,1)S(1)}, bf16[8,2,256,128]{3,2,1,0:T(8,128)(2,1)S(1)}, bf16[8,2,256,128]{3,2,1,0:T(8,128)(2,1)S(1)}, bf16[8,2,256,128]{3,2,1,0:T(8,128)(2,1)S(1)}) custom-call(s32[4,16]{1,0:T(4,128)S(1)} %pad_add_fusion.cols_ref, bf16[1024,512]{1,0:T(8,128)(2,1)S(1)} %get-tuple-element.57.refs_0_.refs_1_.refs_2_.refs_3_, ...), custom_call_target="tpu_custom_call" | custom-call | flops 1000 | bytes 1000 | tf_op jit(solution)/shard_map/weight_step/pallas_call | solution.py:339
  61.5 2.6 %collective-permute-start.2 = (bf16[8,2,256,128]{3,2,1,0:T(8,128)(2,1)S(1)}, bf16[8,2,256,128]{3,2,1,0:T(8,128)(2,1)S(1)}, u32[]{:S(2)}, u32[]{:S(2)}) collective-permute-start(bf16[8,2,256,128]{3,2,1,0:T(8,128)(2,1)S(1)} %get-tuple-element.58), channel_id=1, source_target_pairs={{0,32},{4,36},{8,40},{12,44},{16,48},{20,52},{24,56},{28,60},{32,0... | collective-permute-start | bytes 3145736 | tf_op jit(solution)/shard_map/ppermute | solution.py:480
  64.1 2.1 %collective-permute-start.3 = (bf16[8,2,256,128]{3,2,1,0:T(8,128)(2,1)S(1)}, bf16[8,2,256,128]{3,2,1,0:T(8,128)(2,1)S(1)}, u32[]{:S(2)}, u32[]{:S(2)}) collective-permute-start(bf16[8,2,256,128]{3,2,1,0:T(8,128)(2,1)S(1)} %get-tuple-element.59), channel_id=1, source_target_pairs={{0,96},{4,100},{8,104},{12,108},{16,112},{20,116},{24,120},{28,124... | collective-permute-start | bytes 3145736 | tf_op jit(solution)/shard_map/ppermute | solution.py:480
  66.2 1.5 collective-permute-start.5
  67.7 14.4 %attend_grad.1 = (bf16[512,1024]{1,0:T(8,128)(2,1)}, f32[512,1024]{1,0:T(8,128)}, f32[512,1024]{1,0:T(8,128)}, bf16[2,160,1024]{2,1,0:T(8,128)(2,1)}, bf16[2,160...) custom-call(s32[1]{0:T(128)} %bitcast.2.pos_ref, bf16[512,1024]{1,0:T(8,128)(2,1)} %q_ref.1, ...), custom_call_target="tpu_custom_call" | custom-call | flops 1000 | bytes 1000 | tf_op jit(solution)/shard_map/attend_grad/pallas_call | solution.py:213
  82.1 4.9 %collective-permute-start.7 = (bf16[2,160,1024]{2,1,0:T(8,128)(2,1)}, bf16[2,160,1024]{2,1,0:T(8,128)(2,1)S(1)}, u32[]{:S(2)}, u32[]{:S(2)}) collective-permute-start(bf16[2,160,1024]{2,1,0:T(8,128)(2,1)} %get-tuple-element.75), channel_id=1, source_target_pairs={{0,4},{4,8},{8,12},{12,16},{16,20},{20,24},{24,28},{28,32},{32,36}... | collective-permute-start | bytes 1966088 | tf_op jit(solution)/shard_map/ppermute | solution.py:554
  87.4 1.3 collective-permute-start.8
  88.7 1.4 collective-permute-done.3.refs_13_.refs_9_
  91.9 4.5 %weight_step.5 = (bf16[4,2,256,128]{3,2,1,0:T(8,128)(2,1)S(1)}, bf16[4,2,256,128]{3,2,1,0:T(8,128)(2,1)S(1)}, bf16[4,2,256,128]{3,2,1,0:T(8,128)(2,1)S(1)}, bf16[4,2,256,128]{3,2,1,0:T(8,128)(2,1)S(1)}) custom-call(s32[4,16]{1,0:T(4,128)S(1)} %pad_add_fusion.cols_ref, bf16[1024,512]{1,0:T(8,128)(2,1)} %copy-done, bf16[1024,512]{1,0:T(8,128)(2,1)} %copy-done, ...), custom_call_target="tpu_custom_call" | custom-call | flops 1000 | bytes 1000 | tf_op jit(solution)/shard_map/weight_step/pallas_call | solution.py:339
  96.5 3.4 %collective-permute-start.9 = (bf16[4,2,256,128]{3,2,1,0:T(8,128)(2,1)S(1)}, bf16[4,2,256,128]{3,2,1,0:T(8,128)(2,1)S(1)}, u32[]{:S(2)}, u32[]{:S(2)}) collective-permute-start(bf16[4,2,256,128]{3,2,1,0:T(8,128)(2,1)S(1)} %get-tuple-element.66), channel_id=1, source_target_pairs={{0,96},{4,100},{8,104},{12,108},{16,112},{20,116},{24,120},{28,124... | collective-permute-start | bytes 1572872 | tf_op jit(solution)/shard_map/ppermute | solution.py:480
  100.6 12.8 %collective-permute-done.7.left_ref = bf16[2,160,1024]{2,1,0:T(8,128)(2,1)S(1)} collective-permute-done((bf16[2,160,1024]{2,1,0:T(8,128)(2,1)}, bf16[2,160,1024]{2,1,0:T(8,128)(2,1)S(1)}, u32[]{:S(2)}, u32[]{:S(2)}) %collective-permute-start.7) | collective-permute-done | bytes 655392 | tf_op jit(solution)/shard_map/ppermute | solution.py:554
  114.2 1.2 copy-done.12
  115.4 9.6 %layer_parts.1 = (bf16[256,1024]{1,0:T(8,128)(2,1)S(1)}, bf16[256,1024]{1,0:T(8,128)(2,1)S(1)}, bf16[512,1024]{1,0:T(8,128)(2,1)}, bf16[512,1024]{1,0:T(8,128)(2,1)}, bf16[512,1024]{1,0:T(8,128)(2,1)}) custom-call(s32[4]{0:T(128)S(1)} %pad_add_fusion.1.cols_ref, bf16[512,1024]{1,0:T(8,128)(2,1)S(1)} %copy-done.12, bf16[1024,4096]{1,0:T(8,128)(2,1)} %w_ref.3), custom_call_target="tpu_custom_call" | custom-call | flops 1000 | bytes 1000 | tf_op jit(solution)/shard_map/layer_parts/pallas_call | solution.py:459
  125.9 3.5 %weight_step.6 = (bf16[2,2,512,128]{3,2,1,0:T(8,128)(2,1)S(1)}, bf16[2,2,512,128]{3,2,1,0:T(8,128)(2,1)S(1)}) custom-call(s32[4,16]{1,0:T(4,128)S(1)} %pad_add_fusion.cols_ref, bf16[1024,512]{1,0:T(8,128)(2,1)} %copy-done, bf16[1024,512]{1,0:T(8,128)(2,1)} %copy-done, bf16[1024,512]{1,0:T(8,128)(2,1)} %copy-done, bf16[1024,512]{1,0:T(8,128)(2,1)} %copy-done, ...), custom_call_target="tpu_custom_call" | custom-call | flops 1000 | bytes 1000 | tf_op jit(solution)/shard_map/weight_step/pallas_call | solution.py:339
  129.5 1.4 collective-permute-start.16
  130.8 1.3 collective-permute-start.17
  133.7 10.0 %collective-permute-done.16.refs_16_.refs_17_ = bf16[2,2,512,128]{3,2,1,0:T(8,128)(2,1)S(1)} collective-permute-done((bf16[2,2,512,128]{3,2,1,0:T(8,128)(2,1)S(1)}, bf16[2,2,512,128]{3,2,1,0:T(8,128)(2,1)S(1)}, u32[]{:S(2)}, u32[]{:S(2)}) %collective-permute-start.16) | collective-permute-done | bytes 524320 | tf_op jit(solution)/shard_map/ppermute | solution.py:480
  143.7 2.2 %collective-permute-done.17.refs_18_.refs_19_ = bf16[2,2,512,128]{3,2,1,0:T(8,128)(2,1)S(1)} collective-permute-done((bf16[2,2,512,128]{3,2,1,0:T(8,128)(2,1)S(1)}, bf16[2,2,512,128]{3,2,1,0:T(8,128)(2,1)S(1)}, u32[]{:S(2)}, u32[]{:S(2)}) %collective-permute-start.17) | collective-permute-done | bytes 524320 | tf_op jit(solution)/shard_map/ppermute | solution.py:480
  145.9 2.9 %weight_step.7 = (bf16[1,2,512,128]{3,2,1,0:T(8,128)(2,1)S(1)}, bf16[1,2,512,128]{3,2,1,0:T(8,128)(2,1)S(1)}) custom-call(s32[4,16]{1,0:T(4,128)S(1)} %pad_add_fusion.cols_ref, bf16[1024,512]{1,0:T(8,128)(2,1)} %copy-done, bf16[1024,512]{1,0:T(8,128)(2,1)} %copy-done, bf16[1024,512]{1,0:T(8,128)(2,1)} %copy-done, bf16[1024,512]{1,0:T(8,128)(2,1)} %copy-done, ...), custom_call_target="tpu_custom_call" | custom-call | flops 1000 | bytes 1000 | tf_op jit(solution)/shard_map/weight_step/pallas_call | solution.py:339
  151.0 9.3 %all-to-all-start.1 = ((bf16[32,2,2,1024]{3,2,1,0:T(2,128)(2,1)}), bf16[32,2,2,1024]{3,2,1,0:T(2,128)(2,1)S(1)}, u32[]{:S(2)}, u32[]{:S(2)}) async-start(bf16[32,2,2,1024]{3,2,1,0:T(2,128)(2,1)} %bitcast.7), calls=%async_computation.1 | async-start | bytes 524288 | tf_op jit(solution)/shard_map/all_to_all | solution.py:569
  160.5 3.2 %weight_last.1 = (bf16[1024,128]{1,0:T(8,128)(2,1)S(1)}, f32[1024,128]{1,0:T(8,128)S(1)}) custom-call(s32[5]{0:T(128)S(1)} %pad_add_fusion.2.table_ref, bf16[1024,512]{1,0:T(8,128)(2,1)} %copy-done, bf16[1024,512]{1,0:T(8,128)(2,1)} %copy-done, bf16[1024,512]{1,0:T(8,128)(2,1)} %copy-done, bf16[1024,512]{1,0:T(8,128)(2,1)} %copy-done, ...), custom_call_target="tpu_custom_call" | custom-call | flops 1000 | bytes 1000 | tf_op jit(solution)/shard_map/weight_last/pallas_call | solution.py:395
  163.7 3.4 %collective-permute-start.20 = (bf16[1024,128]{1,0:T(8,128)(2,1)S(1)}, bf16[1024,128]{1,0:T(8,128)(2,1)S(1)}, u32[]{:S(2)}, u32[]{:S(2)}) collective-permute-start(bf16[1024,128]{1,0:T(8,128)(2,1)S(1)} %get-tuple-element.92), channel_id=1, source_target_pairs={{0,4},{4,0},{8,12},{12,8},{16,20},{20,16},{24,28},{28,24},{32,36},... | collective-permute-start | bytes 786440 | tf_op jit(solution)/shard_map/ppermute | solution.py:480
  167.1 4.0 %all-to-all-done.1 = bf16[32,2,2,1024]{3,2,1,0:T(2,128)(2,1)S(1)} async-done(((bf16[32,2,2,1024]{3,2,1,0:T(2,128)(2,1)}), bf16[32,2,2,1024]{3,2,1,0:T(2,128)(2,1)S(1)}, u32[]{:S(2)}, u32[]{:S(2)}) %all-to-all-start.1) | async-done | bytes 262176 | tf_op jit(solution)/shard_map/all_to_all | solution.py:569
  171.9 4.5 %combine.1 = (bf16[512,1024]{1,0:T(8,128)(2,1)}, bf16[512,1024]{1,0:T(8,128)(2,1)}) custom-call(f32[512,1024]{1,0:T(8,128)} %get-tuple-element.83.gk_ref, f32[512,1024]{1,0:T(8,128)} %get-tuple-element.84.gv_ref, bf16[2,160,1024]{2,1,0:T(8,128)(2,1)} %copy-done.18, bf16[2,160,1024]{2,1,0:T(8,128)(2,1)} %collective-permute-done.8.right_ref, ...), custom_call_target="tpu_custom_call" | custom-call | flops 1000 | bytes 1000 | tf_op jit(solution)/shard_map/combine/pallas_call | solution.py:268
  177.4 3.1 %add_convert_fusion = bf16[512,1024]{1,0:T(8,128)(2,1)} fusion(bf16[512,1024]{1,0:T(8,128)(2,1)} %collective-permute-done.15, bf16[512,1024]{1,0:T(8,128)(2,1)} %collective-permute-done.6, bf16[512,1024]{1,0:T(8,128)(2,1)S(1)} %copy-done.17), kind=kLoop, calls=%fused_computation | loop fusion | flops 3145728 | bytes 4194304 | tf_op jit(solution)/shard_map/convert_element_type | solution.py:574
  (96 shorter events, 13.8 us)
Async XLA Ops:
  4.8 40.0 %collective-permute-start = (bf16[2,160,1024]{2,1,0:T(8,128)(2,1)}, bf16[2,160,1024]{2,1,0:T(8,128)(2,1)S(1)}, u32[]{:S(2)}, u32[]{:S(2)}) collective-permute-start(bf16[2,160,1024]{2,1,0:T(8,128)(2,1)} %get-tuple-element.52), channel_id=1, source_target_pairs={{0,4},{4,8},{8,12},{12,16},{16,20},{20,24},{24,28},{28,32},{32,36}... | collective-permute-start | bytes 1966088 | tf_op jit(solution)/shard_map/ppermute | solution.py:516
  10.7 34.1 %collective-permute-start.1 = (bf16[2,160,1024]{2,1,0:T(8,128)(2,1)}, bf16[2,160,1024]{2,1,0:T(8,128)(2,1)S(1)}, u32[]{:S(2)}, u32[]{:S(2)}) collective-permute-start(bf16[2,160,1024]{2,1,0:T(8,128)(2,1)} %get-tuple-element.53), channel_id=1, source_target_pairs={{4,0},{8,4},{12,8},{16,12},{20,16},{24,20},{28,24},{32,28},{36,32}... | collective-permute-start | bytes 1966088 | tf_op jit(solution)/shard_map/ppermute | solution.py:517
  12.0 9.5 %copy-start.19 = (bf16[2,2,1024]{2,1,0:T(2,128)(2,1)S(1)}, bf16[2,2,1024]{2,1,0:T(2,128)(2,1)}, u32[]{:S(2)}) copy-start(bf16[2,2,1024]{2,1,0:T(2,128)(2,1)} %get-tuple-element.55) | copy-start | bytes 24580
  12.0 21.2 %copy-start.20 = (s32[4]{0:T(128)S(1)}, s32[4]{0:T(128)}, u32[]{:S(2)}) copy-start(s32[4]{0:T(128)} %constant.89.clone) | copy-start | bytes 52
  12.0 21.2 %copy-start.21 = (s32[4]{0:T(128)S(1)}, s32[4]{0:T(128)}, u32[]{:S(2)}) copy-start(s32[4]{0:T(128)} %constant.88.clone) | copy-start | bytes 52
  22.3 21.5 %all-to-all-start = ((bf16[32,2,2,1024]{3,2,1,0:T(2,128)(2,1)}), bf16[32,2,2,1024]{3,2,1,0:T(2,128)(2,1)S(1)}, u32[]{:S(2)}, u32[]{:S(2)}) async-start(bf16[32,2,2,1024]{3,2,1,0:T(2,128)(2,1)} %broadcast_in_dim.27), calls=%async_computation | async-start | bytes 524288 | tf_op jit(solution)/shard_map/all_to_all | solution.py:520
  54.7 6.8 %copy-start = (bf16[1024,512]{1,0:T(8,128)(2,1)}, bf16[1024,512]{1,0:T(8,128)(2,1)S(1)}, u32[]{:S(2)}) copy-start(bf16[1024,512]{1,0:T(8,128)(2,1)S(1)} %get-tuple-element.57.refs_0_.refs_1_.refs_2_.refs_3_) | copy-start | bytes 3145732
  54.7 13.0 %copy-start.11 = (bf16[512,1024]{1,0:T(8,128)(2,1)}, bf16[512,1024]{1,0:T(8,128)(2,1)S(1)}, u32[]{:S(2)}) copy-start(bf16[512,1024]{1,0:T(8,128)(2,1)S(1)} %get-tuple-element.70.att_ref) | copy-start | bytes 3145732
  54.7 13.0 %copy-start.13 = (bf16[512,1024]{1,0:T(8,128)(2,1)S(1)}, bf16[512,1024]{1,0:T(8,128)(2,1)}, u32[]{:S(2)}) copy-start(bf16[512,1024]{1,0:T(8,128)(2,1)} %project.1.do_ref) | copy-start | bytes 3145732
  61.5 25.9 %collective-permute-start.2 = (bf16[8,2,256,128]{3,2,1,0:T(8,128)(2,1)S(1)}, bf16[8,2,256,128]{3,2,1,0:T(8,128)(2,1)S(1)}, u32[]{:S(2)}, u32[]{:S(2)}) collective-permute-start(bf16[8,2,256,128]{3,2,1,0:T(8,128)(2,1)S(1)} %get-tuple-element.58), channel_id=1, source_target_pairs={{0,32},{4,36},{8,40},{12,44},{16,48},{20,52},{24,56},{28,60},{32,0... | collective-permute-start | bytes 3145736 | tf_op jit(solution)/shard_map/ppermute | solution.py:480
  64.1 26.0 %collective-permute-start.3 = (bf16[8,2,256,128]{3,2,1,0:T(8,128)(2,1)S(1)}, bf16[8,2,256,128]{3,2,1,0:T(8,128)(2,1)S(1)}, u32[]{:S(2)}, u32[]{:S(2)}) collective-permute-start(bf16[8,2,256,128]{3,2,1,0:T(8,128)(2,1)S(1)} %get-tuple-element.59), channel_id=1, source_target_pairs={{0,96},{4,100},{8,104},{12,108},{16,112},{20,116},{24,120},{28,124... | collective-permute-start | bytes 3145736 | tf_op jit(solution)/shard_map/ppermute | solution.py:480
  66.2 24.5 %collective-permute-start.4 = (bf16[8,2,256,128]{3,2,1,0:T(8,128)(2,1)S(1)}, bf16[8,2,256,128]{3,2,1,0:T(8,128)(2,1)S(1)}, u32[]{:S(2)}, u32[]{:S(2)}) collective-permute-start(bf16[8,2,256,128]{3,2,1,0:T(8,128)(2,1)S(1)} %get-tuple-element.60), channel_id=1, source_target_pairs={{0,8},{4,12},{8,0},{12,4},{16,24},{20,28},{24,16},{28,20},{32,40},... | collective-permute-start | bytes 3145736 | tf_op jit(solution)/shard_map/ppermute | solution.py:480
  66.2 25.7 %collective-permute-start.5 = (bf16[8,2,256,128]{3,2,1,0:T(8,128)(2,1)S(1)}, bf16[8,2,256,128]{3,2,1,0:T(8,128)(2,1)S(1)}, u32[]{:S(2)}, u32[]{:S(2)}) collective-permute-start(bf16[8,2,256,128]{3,2,1,0:T(8,128)(2,1)S(1)} %get-tuple-element.61), channel_id=1, source_target_pairs={{0,24},{4,28},{8,16},{12,20},{16,8},{20,12},{24,0},{28,4},{32,56},... | collective-permute-start | bytes 3145736 | tf_op jit(solution)/shard_map/ppermute | solution.py:480
  82.1 31.2 %collective-permute-start.7 = (bf16[2,160,1024]{2,1,0:T(8,128)(2,1)}, bf16[2,160,1024]{2,1,0:T(8,128)(2,1)S(1)}, u32[]{:S(2)}, u32[]{:S(2)}) collective-permute-start(bf16[2,160,1024]{2,1,0:T(8,128)(2,1)} %get-tuple-element.75), channel_id=1, source_target_pairs={{0,4},{4,8},{8,12},{12,16},{16,20},{20,24},{24,28},{28,32},{32,36}... | collective-permute-start | bytes 1966088 | tf_op jit(solution)/shard_map/ppermute | solution.py:554
  87.4 9.0 %copy-start.1 = (bf16[8,2,256,128]{3,2,1,0:T(8,128)(2,1)}, bf16[8,2,256,128]{3,2,1,0:T(8,128)(2,1)S(1)}, u32[]{:S(2)}) copy-start(bf16[8,2,256,128]{3,2,1,0:T(8,128)(2,1)S(1)} %collective-permute-done.2.refs_12_.refs_8_) | copy-start | bytes 3145732
  87.4 37.6 %collective-permute-start.8 = (bf16[2,160,1024]{2,1,0:T(8,128)(2,1)}, bf16[2,160,1024]{2,1,0:T(8,128)(2,1)}, u32[]{:S(2)}, u32[]{:S(2)}) collective-permute-start(bf16[2,160,1024]{2,1,0:T(8,128)(2,1)} %get-tuple-element.76), channel_id=1, source_target_pairs={{4,0},{8,4},{12,8},{16,12},{20,16},{24,20},{28,24},{32,28},{36,32}... | collective-permute-start | bytes 1966088 | tf_op jit(solution)/shard_map/ppermute | solution.py:555
  96.5 28.6 %collective-permute-start.9 = (bf16[4,2,256,128]{3,2,1,0:T(8,128)(2,1)S(1)}, bf16[4,2,256,128]{3,2,1,0:T(8,128)(2,1)S(1)}, u32[]{:S(2)}, u32[]{:S(2)}) collective-permute-start(bf16[4,2,256,128]{3,2,1,0:T(8,128)(2,1)S(1)} %get-tuple-element.66), channel_id=1, source_target_pairs={{0,96},{4,100},{8,104},{12,108},{16,112},{20,116},{24,120},{28,124... | collective-permute-start | bytes 1572872 | tf_op jit(solution)/shard_map/ppermute | solution.py:480
  100.0 25.6 %collective-permute-start.10 = (bf16[4,2,256,128]{3,2,1,0:T(8,128)(2,1)S(1)}, bf16[4,2,256,128]{3,2,1,0:T(8,128)(2,1)S(1)}, u32[]{:S(2)}, u32[]{:S(2)}) collective-permute-start(bf16[4,2,256,128]{3,2,1,0:T(8,128)(2,1)S(1)} %get-tuple-element.67), channel_id=1, source_target_pairs={{0,32},{4,36},{8,40},{12,44},{16,48},{20,52},{24,56},{28,60},{32,0... | collective-permute-start | bytes 1572872 | tf_op jit(solution)/shard_map/ppermute | solution.py:480
  100.0 25.9 %collective-permute-start.11 = (bf16[4,2,256,128]{3,2,1,0:T(8,128)(2,1)S(1)}, bf16[4,2,256,128]{3,2,1,0:T(8,128)(2,1)S(1)}, u32[]{:S(2)}, u32[]{:S(2)}) collective-permute-start(bf16[4,2,256,128]{3,2,1,0:T(8,128)(2,1)S(1)} %get-tuple-element.68), channel_id=1, source_target_pairs={{0,24},{4,28},{8,16},{12,20},{16,8},{20,12},{24,0},{28,4},{32,56},... | collective-permute-start | bytes 1572872 | tf_op jit(solution)/shard_map/ppermute | solution.py:480
  113.4 11.7 %copy-start.18 = (bf16[2,160,1024]{2,1,0:T(8,128)(2,1)}, bf16[2,160,1024]{2,1,0:T(8,128)(2,1)S(1)}, u32[]{:S(2)}) copy-start(bf16[2,160,1024]{2,1,0:T(8,128)(2,1)S(1)} %collective-permute-done.7.left_ref) | copy-start | bytes 1966084
  113.4 12.5 %collective-permute-start.12 = (bf16[4,2,256,128]{3,2,1,0:T(8,128)(2,1)S(1)}, bf16[4,2,256,128]{3,2,1,0:T(8,128)(2,1)S(1)}, u32[]{:S(2)}, u32[]{:S(2)}) collective-permute-start(bf16[4,2,256,128]{3,2,1,0:T(8,128)(2,1)S(1)} %get-tuple-element.69), channel_id=1, source_target_pairs={{0,8},{4,12},{8,0},{12,4},{16,24},{20,28},{24,16},{28,20},{32,40},... | collective-permute-start | bytes 1572872 | tf_op jit(solution)/shard_map/ppermute | solution.py:480
  125.0 7.1 %collective-permute-start.14 = (bf16[256,1024]{1,0:T(8,128)(2,1)S(1)}, bf16[256,1024]{1,0:T(8,128)(2,1)S(1)}, u32[]{:S(2)}, u32[]{:S(2)}) collective-permute-start(bf16[256,1024]{1,0:T(8,128)(2,1)S(1)} %get-tuple-element.81), channel_id=1, source_target_pairs={{0,1},{1,0},{2,3},{3,2},{4,5},{5,4},{6,7},{7,6},{8,9},{9,8},{10,11... | collective-permute-start | bytes 1572872 | tf_op jit(solution)/shard_map/ppermute | solution.py:480
  125.1 7.1 %collective-permute-start.13 = (bf16[256,1024]{1,0:T(8,128)(2,1)S(1)}, bf16[256,1024]{1,0:T(8,128)(2,1)S(1)}, u32[]{:S(2)}, u32[]{:S(2)}) collective-permute-start(bf16[256,1024]{1,0:T(8,128)(2,1)S(1)} %get-tuple-element.74), channel_id=1, source_target_pairs={{0,1},{1,0},{2,3},{3,2},{4,5},{5,4},{6,7},{7,6},{8,9},{9,8},{10,11... | collective-permute-start | bytes 1572872 | tf_op jit(solution)/shard_map/ppermute | solution.py:480
  125.6 6.6 %copy-start.16 = (bf16[512,1024]{1,0:T(8,128)(2,1)S(1)}, bf16[512,1024]{1,0:T(8,128)(2,1)}, u32[]{:S(2)}) copy-start(bf16[512,1024]{1,0:T(8,128)(2,1)} %get-tuple-element.80) | copy-start | bytes 3145732
  125.6 51.8 %collective-permute-start.6 = (bf16[512,1024]{1,0:T(8,128)(2,1)}, bf16[512,1024]{1,0:T(8,128)(2,1)}, u32[]{:S(2)}, u32[]{:S(2)}) collective-permute-start(bf16[512,1024]{1,0:T(8,128)(2,1)} %get-tuple-element.72), channel_id=1, source_target_pairs={{0,1},{1,0},{2,3},{3,2},{4,5},{5,4},{6,7},{7,6},{8,9},{9,8},{10,11... | collective-permute-start | bytes 3145736 | tf_op jit(solution)/shard_map/ppermute | solution.py:480
  129.5 14.2 %collective-permute-start.16 = (bf16[2,2,512,128]{3,2,1,0:T(8,128)(2,1)S(1)}, bf16[2,2,512,128]{3,2,1,0:T(8,128)(2,1)S(1)}, u32[]{:S(2)}, u32[]{:S(2)}) collective-permute-start(bf16[2,2,512,128]{3,2,1,0:T(8,128)(2,1)S(1)} %get-tuple-element.78), channel_id=1, source_target_pairs={{0,8},{4,12},{8,0},{12,4},{16,24},{20,28},{24,16},{28,20},{32,40},... | collective-permute-start | bytes 1572872 | tf_op jit(solution)/shard_map/ppermute | solution.py:480
  130.8 15.1 %collective-permute-start.17 = (bf16[2,2,512,128]{3,2,1,0:T(8,128)(2,1)S(1)}, bf16[2,2,512,128]{3,2,1,0:T(8,128)(2,1)S(1)}, u32[]{:S(2)}, u32[]{:S(2)}) collective-permute-start(bf16[2,2,512,128]{3,2,1,0:T(8,128)(2,1)S(1)} %get-tuple-element.79), channel_id=1, source_target_pairs={{0,96},{4,100},{8,104},{12,108},{16,112},{20,116},{24,120},{28,124... | collective-permute-start | bytes 1572872 | tf_op jit(solution)/shard_map/ppermute | solution.py:480
  132.6 44.8 %collective-permute-start.15 = (bf16[512,1024]{1,0:T(8,128)(2,1)S(1)}, bf16[512,1024]{1,0:T(8,128)(2,1)}, u32[]{:S(2)}, u32[]{:S(2)}) collective-permute-start(bf16[512,1024]{1,0:T(8,128)(2,1)S(1)} %add_convert_fusion.1), channel_id=1, source_target_pairs={{0,2},{1,3},{2,0},{3,1},{4,6},{5,7},{6,4},{7,5},{8,10},{9,11},{10,... | collective-permute-start | bytes 3145736 | tf_op jit(solution)/shard_map/ppermute | solution.py:480
  148.8 11.7 %collective-permute-start.18 = (bf16[1,2,512,128]{3,2,1,0:T(8,128)(2,1)S(1)}, bf16[1,2,512,128]{3,2,1,0:T(8,128)(2,1)S(1)}, u32[]{:S(2)}, u32[]{:S(2)}) collective-permute-start(bf16[1,2,512,128]{3,2,1,0:T(8,128)(2,1)S(1)} %get-tuple-element.89), channel_id=1, source_target_pairs={{0,24},{4,28},{8,16},{12,20},{16,8},{20,12},{24,0},{28,4},{32,56},... | collective-permute-start | bytes 786440 | tf_op jit(solution)/shard_map/ppermute | solution.py:480
  150.0 10.5 %collective-permute-start.19 = (bf16[1,2,512,128]{3,2,1,0:T(8,128)(2,1)S(1)}, bf16[1,2,512,128]{3,2,1,0:T(8,128)(2,1)S(1)}, u32[]{:S(2)}, u32[]{:S(2)}) collective-permute-start(bf16[1,2,512,128]{3,2,1,0:T(8,128)(2,1)S(1)} %get-tuple-element.90), channel_id=1, source_target_pairs={{0,32},{4,36},{8,40},{12,44},{16,48},{20,52},{24,56},{28,60},{32,0... | collective-permute-start | bytes 786440 | tf_op jit(solution)/shard_map/ppermute | solution.py:480
  151.0 20.1 %all-to-all-start.1 = ((bf16[32,2,2,1024]{3,2,1,0:T(2,128)(2,1)}), bf16[32,2,2,1024]{3,2,1,0:T(2,128)(2,1)S(1)}, u32[]{:S(2)}, u32[]{:S(2)}) async-start(bf16[32,2,2,1024]{3,2,1,0:T(2,128)(2,1)} %bitcast.7), calls=%async_computation.1 | async-start | bytes 524288 | tf_op jit(solution)/shard_map/all_to_all | solution.py:569
  163.7 12.7 %collective-permute-start.20 = (bf16[1024,128]{1,0:T(8,128)(2,1)S(1)}, bf16[1024,128]{1,0:T(8,128)(2,1)S(1)}, u32[]{:S(2)}, u32[]{:S(2)}) collective-permute-start(bf16[1024,128]{1,0:T(8,128)(2,1)S(1)} %get-tuple-element.92), channel_id=1, source_target_pairs={{0,4},{4,0},{8,12},{12,8},{16,20},{20,16},{24,28},{28,24},{32,36},... | collective-permute-start | bytes 786440 | tf_op jit(solution)/shard_map/ppermute | solution.py:480
  (13 other events, 48.8 us)

commit v5 on v4

--- a/solution.py
+++ b/solution.py
@@ -193,7 +193,7 @@
             ],
         ),
         out_shape=[
-            jax.ShapeDtypeStruct((tokens, feats), BF),
+            pltpu.HBM((tokens, feats), BF),
             jax.ShapeDtypeStruct((feats, tokens), BF),
             jax.ShapeDtypeStruct((heads, 1, tokens), F32),
         ],
@@ -239,7 +239,7 @@
         compiler_params=params(BIG),
         cost_estimate=SMALL,
         name="attend_grad",
-    )(pos, *pinned(q, k, v, left, right, near, far, bias), do, att, lse)
+    )(pos, *pinned(q, k, v, left, right, near, far, bias, do, att), lse)
 
 
 def combine_kernel(gk_ref, gv_ref, left_ref, right_ref, far_ref, ok_ref, ov_ref):
@@ -472,7 +472,7 @@
         compiler_params=params(BIG),
         cost_estimate=SMALL,
         name="layer_parts",
-    )(cols, att, *pinned(w))
+    )(cols, *pinned(att, w))
 
 
 def swap(x, axis, bits):
@@ -553,16 +553,16 @@
     )
     back_left = lax.ppermute(sr, "seq", right_perm)
     back_right = lax.ppermute(sl, "seq", left_perm)
-    out = first_axis(1, [gfar])
-
     c, zl = tp & 1, tp >> 1
     lwidth = width // tp_count
     lcols = jnp.stack([zl ^ 1, zl]) * 2
     lorder = jnp.concatenate([lcols + (c ^ 1), lcols + c])
-    top_send, bottom_send, own_send, far_keep, own_keep = layer_parts(lorder, after(att, *out), out_weight, lwidth)
+    top_send, bottom_send, own_send, far_keep, own_keep = layer_parts(lorder, after(att, gfar), out_weight, lwidth)
     far_got = jnp.concatenate([swap(top_send, "tp", 1), swap(bottom_send, "tp", 1)])
     own_got = swap(own_send, "tp", 1)
-    out = second_axis(0, [top_send, back_left, back_right])
+    out = first_axis(1, [top_send])
+
+    out = second_axis(0, [*out, back_left, back_right])
     lsend2 = add(after(far_keep, *out), far_got)
     lgot2 = swap(lsend2, "tp", 2)
     far_parts = jnp.moveaxis(after(gfar, *out).reshape(2, seq_count, -1, feats), 1, 0)

time: 181 us -> 177 us (0.978)
  waiting for transfers between devices: 42.7 us -> 36.9 us
    ppermute x1, waiting for transfers between devices: 12.8 us -> 2.62 us  [shards(): back_left = lax.ppermute(sr, 'seq', right_perm)]
    ppermute x17, waiting for transfers between devices: 15.9 us -> 20.2 us  [swap(): return lax.ppermute(x, axis, [(i, i ^ bits) for i in range(n)])]
  transfers between devices with their start and end apart: 23 -> 23, of which waited for: 9 -> 10; matrix products, arithmetic and copies ran while one was open for 3% -> 3% of each run, Pallas kernels for 29% -> 30%
where the time goes in v5:
time: 177 us; the launch traced here: 176 us
  Pallas kernels  73.2 us (41%)
  starting transfers between devices  54.6 us (31%)
  waiting for transfers between devices  36.9 us (21%)
  other arithmetic  5.62 us (3%)
  local copies, waits for them, and re-layouts  4.61 us (3%)
    ppermute x17, starting transfers between devices, swap(): return lax.ppermute(x, axis, [(i, i ^ bits) for i in range(n)])  20.9 us
    ppermute x17, waiting for transfers between devices, swap(): return lax.ppermute(x, axis, [(i, i ^ bits) for i in range(n)])  20.2 us
    pallas_call x4, Pallas kernels, weight_step(): pl.pallas_call(functools.partial(weight_kernel, n, per, len(recvs) * n, p...  18.2 us
    pallas_call x1, Pallas kernels, backward(): pl.pallas_call(functools.partial(bwd_kernel, seq_count), grid_spec=pltpu....  14.5 us
    all_to_all x1, starting transfers between devices, shards(): far_all = lax.all_to_all(far_all, 'seq', 0, 0, tiled=True)  10.9 us
    all_to_all x1, waiting for transfers between devices, shards(): far_all = lax.all_to_all(far_all, 'seq', 0, 0, tiled=True)  10 us
    pallas_call x1, Pallas kernels, layer_parts(): pl.pallas_call(layer_kernel, grid_spec=pltpu.PrefetchScalarGridSpec(num_s...  9.86 us
    all_to_all x1, starting transfers between devices, shards(): lax.all_to_all(far_parts, 'seq', 0, 0, tiled=True).astype(F32).sum(axis=0)  9.47 us
  transfers between devices with their start and end apart: 23, of which 10 were waited for; matrix products, arithmetic and copies ran while one was open for 3% of the time, Pallas kernels for 30%

profile of v5, /device:TPU:0, one launch (start us, length us, event | category | flops | bytes accessed | tf_op | source)
XLA Modules:
  0.0 175.9 jit_solution(14800148744600810704)
XLA Ops:
  0.6 4.1 %pool.1 = (bf16[2,32,1024]{2,1,0:T(8,128)(2,1)}, bf16[2,2,1024]{2,1,0:T(2,128)(2,1)}, bf16[2,160,1024]{2,1,0:T(8,128)(2,1)}, bf16[2,160,1024]{2,1,0:T(8,128)(2,1)}) custom-call(bf16[512,1024]{1,0:T(8,128)(2,1)} %k_ref.5, bf16[512,1024]{1,0:T(8,128)(2,1)} %v_ref.5), custom_call_target="tpu_custom_call" | custom-call | flops 1000 | bytes 1000 | tf_op jit(solution)/shard_map/pool/pallas_call | solution.py:59
  4.8 5.9 %collective-permute-start = (bf16[2,160,1024]{2,1,0:T(8,128)(2,1)}, bf16[2,160,1024]{2,1,0:T(8,128)(2,1)S(1)}, u32[]{:S(2)}, u32[]{:S(2)}) collective-permute-start(bf16[2,160,1024]{2,1,0:T(8,128)(2,1)} %get-tuple-element.52), channel_id=1, source_target_pairs={{0,4},{4,8},{8,12},{12,16},{16,20},{20,24},{24,28},{28,32},{32,36}... | collective-permute-start | bytes 1966088 | tf_op jit(solution)/shard_map/ppermute | solution.py:516
  10.7 1.3 collective-permute-start.1
  12.0 9.4 %project.1.do_ref = bf16[512,1024]{1,0:T(8,128)(2,1)} custom-call(bf16[512,4096]{1,0:T(8,128)(2,1)} %refs_7_.9, bf16[1024,4096]{1,0:T(8,128)(2,1)} %w_ref.3), custom_call_target="tpu_custom_call" | custom-call | flops 1000 | bytes 1000 | tf_op jit(solution)/shard_map/project/pallas_call | solution.py:425
  22.3 10.9 %all-to-all-start = ((bf16[32,2,2,1024]{3,2,1,0:T(2,128)(2,1)}), bf16[32,2,2,1024]{3,2,1,0:T(2,128)(2,1)S(1)}, u32[]{:S(2)}, u32[]{:S(2)}) async-start(bf16[32,2,2,1024]{3,2,1,0:T(2,128)(2,1)} %broadcast_in_dim.27), calls=%async_computation | async-start | bytes 524288 | tf_op jit(solution)/shard_map/all_to_all | solution.py:520
  33.8 10.0 %all-to-all-done = bf16[32,2,2,1024]{3,2,1,0:T(2,128)(2,1)S(1)} async-done(((bf16[32,2,2,1024]{3,2,1,0:T(2,128)(2,1)}), bf16[32,2,2,1024]{3,2,1,0:T(2,128)(2,1)S(1)}, u32[]{:S(2)}, u32[]{:S(2)}) %all-to-all-start) | async-done | bytes 262176 | tf_op jit(solution)/shard_map/all_to_all | solution.py:520
  46.0 9.4 %attend.1 = (bf16[512,1024]{1,0:T(8,128)(2,1)}, bf16[1024,512]{1,0:T(8,128)(2,1)S(1)}, f32[8,1,512]{2,1,0:T(1,128)S(1)}) custom-call(s32[1]{0:T(128)} %bitcast.2.pos_ref, bf16[512,1024]{1,0:T(8,128)(2,1)} %q_ref.1, bf16[512,1024]{1,0:T(8,128)(2,1)} %k_ref.5, bf16[512,1024]{1,0:T(8,128)(2,1)} %v_ref.5, bf16[2,160,1024]{2,1,0:T(8,128)(2,1)} %copy-done.10, ...), custom_call_target="tpu_custom_call" | custom-call | flops 1000 | bytes 1000 | tf_op jit(solution)/shard_map/attend/pallas_call | solution.py:183
  55.4 7.2 %weight_step.4 = (bf16[8,2,256,128]{3,2,1,0:T(8,128)(2,1)}, bf16[8,2,256,128]{3,2,1,0:T(8,128)(2,1)}, bf16[8,2,256,128]{3,2,1,0:T(8,128)(2,1)}, bf16[8,2,256,128]{3,2,1,0:T(8,128)(2,1)}) custom-call(s32[4,16]{1,0:T(4,128)S(1)} %pad_add_fusion.cols_ref, bf16[1024,512]{1,0:T(8,128)(2,1)S(1)} %get-tuple-element.57.refs_0_.refs_1_.refs_2_.refs_3_, ...), custom_call_target="tpu_custom_call" | custom-call | flops 1000 | bytes 1000 | tf_op jit(solution)/shard_map/weight_step/pallas_call | solution.py:339
  62.6 2.6 %collective-permute-start.3 = (bf16[8,2,256,128]{3,2,1,0:T(8,128)(2,1)}, bf16[8,2,256,128]{3,2,1,0:T(8,128)(2,1)S(1)}, u32[]{:S(2)}, u32[]{:S(2)}) collective-permute-start(bf16[8,2,256,128]{3,2,1,0:T(8,128)(2,1)} %get-tuple-element.58), channel_id=1, source_target_pairs={{0,32},{4,36},{8,40},{12,44},{16,48},{20,52},{24,56},{28,60},{32,0... | collective-permute-start | bytes 3145736 | tf_op jit(solution)/shard_map/ppermute | solution.py:480
  65.2 2.1 %collective-permute-start.4 = (bf16[8,2,256,128]{3,2,1,0:T(8,128)(2,1)}, bf16[8,2,256,128]{3,2,1,0:T(8,128)(2,1)S(1)}, u32[]{:S(2)}, u32[]{:S(2)}) collective-permute-start(bf16[8,2,256,128]{3,2,1,0:T(8,128)(2,1)} %get-tuple-element.59), channel_id=1, source_target_pairs={{0,96},{4,100},{8,104},{12,108},{16,112},{20,116},{24,120},{28,124... | collective-permute-start | bytes 3145736 | tf_op jit(solution)/shard_map/ppermute | solution.py:480
  67.3 1.6 collective-permute-start.6
  68.9 14.5 %attend_grad.1 = (bf16[512,1024]{1,0:T(8,128)(2,1)}, f32[512,1024]{1,0:T(8,128)}, f32[512,1024]{1,0:T(8,128)}, bf16[2,160,1024]{2,1,0:T(8,128)(2,1)S(1)}, bf16[2...) custom-call(s32[1]{0:T(128)} %bitcast.2.pos_ref, bf16[512,1024]{1,0:T(8,128)(2,1)} %q_ref.1, ...), custom_call_target="tpu_custom_call" | custom-call | flops 1000 | bytes 1000 | tf_op jit(solution)/shard_map/attend_grad/pallas_call | solution.py:213
  83.4 4.9 %collective-permute-start.7 = (bf16[2,160,1024]{2,1,0:T(8,128)(2,1)S(1)}, bf16[2,160,1024]{2,1,0:T(8,128)(2,1)S(1)}, u32[]{:S(2)}, u32[]{:S(2)}) collective-permute-start(bf16[2,160,1024]{2,1,0:T(8,128)(2,1)S(1)} %get-tuple-element.75), channel_id=1, source_target_pairs={{0,4},{4,8},{8,12},{12,16},{16,20},{20,24},{24,28},{28,32},{32,36}... | collective-permute-start | bytes 1966088 | tf_op jit(solution)/shard_map/ppermute | solution.py:554
  88.8 1.3 collective-permute-start.8
  90.2 9.9 %layer_parts.1 = (bf16[256,1024]{1,0:T(8,128)(2,1)S(1)}, bf16[256,1024]{1,0:T(8,128)(2,1)S(1)}, bf16[512,1024]{1,0:T(8,128)(2,1)}, bf16[512,1024]{1,0:T(8,128)(2,1)}, bf16[512,1024]{1,0:T(8,128)(2,1)}) custom-call(s32[4]{0:T(128)S(1)} %pad_add_fusion.1.cols_ref, bf16[512,1024]{1,0:T(8,128)(2,1)} %get-tuple-element.65.att_ref, bf16[1024,4096]{1,0:T(8,128)(2,1)} %w_ref.3), custom_call_target="tpu_custom_call" | custom-call | flops 1000 | bytes 1000 | tf_op jit(solution)/shard_map/layer_parts/pallas_call | solution.py:459
  100.1 4.6 %weight_step.5 = (bf16[4,2,256,128]{3,2,1,0:T(8,128)(2,1)S(1)}, bf16[4,2,256,128]{3,2,1,0:T(8,128)(2,1)S(1)}, bf16[4,2,256,128]{3,2,1,0:T(8,128)(2,1)S(1)}, bf16[4,2,256,128]{3,2,1,0:T(8,128)(2,1)S(1)}) custom-call(s32[4,16]{1,0:T(4,128)S(1)} %pad_add_fusion.cols_ref, bf16[1024,512]{1,0:T(8,128)(2,1)} %copy-done, bf16[1024,512]{1,0:T(8,128)(2,1)} %copy-done, ...), custom_call_target="tpu_custom_call" | custom-call | flops 1000 | bytes 1000 | tf_op jit(solution)/shard_map/weight_step/pallas_call | solution.py:339
  104.8 6.2 %collective-permute-start.9 = (bf16[4,2,256,128]{3,2,1,0:T(8,128)(2,1)S(1)}, bf16[4,2,256,128]{3,2,1,0:T(8,128)(2,1)S(1)}, u32[]{:S(2)}, u32[]{:S(2)}) collective-permute-start(bf16[4,2,256,128]{3,2,1,0:T(8,128)(2,1)S(1)} %get-tuple-element.71), channel_id=1, source_target_pairs={{0,96},{4,100},{8,104},{12,108},{16,112},{20,116},{24,120},{28,124... | collective-permute-start | bytes 1572872 | tf_op jit(solution)/shard_map/ppermute | solution.py:480
  111.6 2.6 %collective-permute-done.7.left_ref = bf16[2,160,1024]{2,1,0:T(8,128)(2,1)S(1)} collective-permute-done((bf16[2,160,1024]{2,1,0:T(8,128)(2,1)S(1)}, bf16[2,160,1024]{2,1,0:T(8,128)(2,1)S(1)}, u32[]{:S(2)}, u32[]{:S(2)}) %collective-permute-start.7) | collective-permute-done | bytes 655392 | tf_op jit(solution)/shard_map/ppermute | solution.py:554
  114.9 5.9 %collective-permute-done.9.refs_16_.refs_12_ = bf16[4,2,256,128]{3,2,1,0:T(8,128)(2,1)S(1)} collective-permute-done((bf16[4,2,256,128]{3,2,1,0:T(8,128)(2,1)S(1)}, bf16[4,2,256,128]{3,2,1,0:T(8,128)(2,1)S(1)}, u32[]{:S(2)}, u32[]{:S(2)}) %collective-permute-start.9) | collective-permute-done | bytes 524320 | tf_op jit(solution)/shard_map/ppermute | solution.py:480
  120.9 1.5 collective-permute-done.10.refs_17_.refs_13_
  122.4 1.2 collective-permute-done.11.refs_18_.refs_14_
  123.6 1.4 collective-permute-done.12.refs_19_.refs_15_
  125.0 3.5 %weight_step.6 = (bf16[2,2,512,128]{3,2,1,0:T(8,128)(2,1)S(1)}, bf16[2,2,512,128]{3,2,1,0:T(8,128)(2,1)S(1)}) custom-call(s32[4,16]{1,0:T(4,128)S(1)} %pad_add_fusion.cols_ref, bf16[1024,512]{1,0:T(8,128)(2,1)} %copy-done, bf16[1024,512]{1,0:T(8,128)(2,1)} %copy-done, bf16[1024,512]{1,0:T(8,128)(2,1)} %copy-done, bf16[1024,512]{1,0:T(8,128)(2,1)} %copy-done, ...), custom_call_target="tpu_custom_call" | custom-call | flops 1000 | bytes 1000 | tf_op jit(solution)/shard_map/weight_step/pallas_call | solution.py:339
  132.0 8.3 %collective-permute-done.16.refs_16_.refs_17_ = bf16[2,2,512,128]{3,2,1,0:T(8,128)(2,1)S(1)} collective-permute-done((bf16[2,2,512,128]{3,2,1,0:T(8,128)(2,1)S(1)}, bf16[2,2,512,128]{3,2,1,0:T(8,128)(2,1)S(1)}, u32[]{:S(2)}, u32[]{:S(2)}) %collective-permute-start.16) | collective-permute-done | bytes 524320 | tf_op jit(solution)/shard_map/ppermute | solution.py:480
  140.4 1.3 collective-permute-done.17.refs_18_.refs_19_
  141.7 2.9 %weight_step.7 = (bf16[1,2,512,128]{3,2,1,0:T(8,128)(2,1)S(1)}, bf16[1,2,512,128]{3,2,1,0:T(8,128)(2,1)S(1)}) custom-call(s32[4,16]{1,0:T(4,128)S(1)} %pad_add_fusion.cols_ref, bf16[1024,512]{1,0:T(8,128)(2,1)} %copy-done, bf16[1024,512]{1,0:T(8,128)(2,1)} %copy-done, bf16[1024,512]{1,0:T(8,128)(2,1)} %copy-done, bf16[1024,512]{1,0:T(8,128)(2,1)} %copy-done, ...), custom_call_target="tpu_custom_call" | custom-call | flops 1000 | bytes 1000 | tf_op jit(solution)/shard_map/weight_step/pallas_call | solution.py:339
  146.2 9.5 %all-to-all-start.1 = ((bf16[32,2,2,1024]{3,2,1,0:T(2,128)(2,1)}), bf16[32,2,2,1024]{3,2,1,0:T(2,128)(2,1)S(1)}, u32[]{:S(2)}, u32[]{:S(2)}) async-start(bf16[32,2,2,1024]{3,2,1,0:T(2,128)(2,1)} %bitcast.7), calls=%async_computation.1 | async-start | bytes 524288 | tf_op jit(solution)/shard_map/all_to_all | solution.py:569
  155.9 3.2 %weight_last.1 = (bf16[1024,128]{1,0:T(8,128)(2,1)S(1)}, f32[1024,128]{1,0:T(8,128)S(1)}) custom-call(s32[5]{0:T(128)S(1)} %pad_add_fusion.2.table_ref, bf16[1024,512]{1,0:T(8,128)(2,1)} %copy-done, bf16[1024,512]{1,0:T(8,128)(2,1)} %copy-done, bf16[1024,512]{1,0:T(8,128)(2,1)} %copy-done, bf16[1024,512]{1,0:T(8,128)(2,1)} %copy-done, ...), custom_call_target="tpu_custom_call" | custom-call | flops 1000 | bytes 1000 | tf_op jit(solution)/shard_map/weight_last/pallas_call | solution.py:395
  159.1 3.4 %collective-permute-start.20 = (bf16[1024,128]{1,0:T(8,128)(2,1)S(1)}, bf16[1024,128]{1,0:T(8,128)(2,1)S(1)}, u32[]{:S(2)}, u32[]{:S(2)}) collective-permute-start(bf16[1024,128]{1,0:T(8,128)(2,1)S(1)} %get-tuple-element.92), channel_id=1, source_target_pairs={{0,4},{4,0},{8,12},{12,8},{16,20},{20,16},{24,28},{28,24},{32,36},... | collective-permute-start | bytes 786440 | tf_op jit(solution)/shard_map/ppermute | solution.py:480
  162.5 4.0 %all-to-all-done.1 = bf16[32,2,2,1024]{3,2,1,0:T(2,128)(2,1)S(1)} async-done(((bf16[32,2,2,1024]{3,2,1,0:T(2,128)(2,1)}), bf16[32,2,2,1024]{3,2,1,0:T(2,128)(2,1)S(1)}, u32[]{:S(2)}, u32[]{:S(2)}) %all-to-all-start.1) | async-done | bytes 262176 | tf_op jit(solution)/shard_map/all_to_all | solution.py:569
  167.3 4.5 %combine.1 = (bf16[512,1024]{1,0:T(8,128)(2,1)}, bf16[512,1024]{1,0:T(8,128)(2,1)}) custom-call(f32[512,1024]{1,0:T(8,128)} %get-tuple-element.83.gk_ref, f32[512,1024]{1,0:T(8,128)} %get-tuple-element.84.gv_ref, bf16[2,160,1024]{2,1,0:T(8,128)(2,1)} %copy-done.14, bf16[2,160,1024]{2,1,0:T(8,128)(2,1)} %copy-done.15, f32[2,2,1024]{2,1,0:T(2,128)} %convert_reduce_fusion.far_ref), custom_call_target="tpu_custom_call" | custom-call | flops 1000 | bytes 1000 | tf_op jit(solution)/shard_map/combine/pallas_call | solution.py:268
  172.7 3.1 %add_convert_fusion = bf16[512,1024]{1,0:T(8,128)(2,1)} fusion(bf16[512,1024]{1,0:T(8,128)(2,1)} %collective-permute-done.15, bf16[512,1024]{1,0:T(8,128)(2,1)} %collective-permute-done.2, bf16[512,1024]{1,0:T(8,128)(2,1)S(1)} %copy-done.13), kind=kLoop, calls=%fused_computation | loop fusion | flops 3145728 | bytes 4194304 | tf_op jit(solution)/shard_map/convert_element_type | solution.py:574
  (90 shorter events, 12.7 us)
Async XLA Ops:
  4.8 40.0 %collective-permute-start = (bf16[2,160,1024]{2,1,0:T(8,128)(2,1)}, bf16[2,160,1024]{2,1,0:T(8,128)(2,1)S(1)}, u32[]{:S(2)}, u32[]{:S(2)}) collective-permute-start(bf16[2,160,1024]{2,1,0:T(8,128)(2,1)} %get-tuple-element.52), channel_id=1, source_target_pairs={{0,4},{4,8},{8,12},{12,16},{16,20},{20,24},{24,28},{28,32},{32,36}... | collective-permute-start | bytes 1966088 | tf_op jit(solution)/shard_map/ppermute | solution.py:516
  10.7 34.1 %collective-permute-start.1 = (bf16[2,160,1024]{2,1,0:T(8,128)(2,1)}, bf16[2,160,1024]{2,1,0:T(8,128)(2,1)S(1)}, u32[]{:S(2)}, u32[]{:S(2)}) collective-permute-start(bf16[2,160,1024]{2,1,0:T(8,128)(2,1)} %get-tuple-element.53), channel_id=1, source_target_pairs={{4,0},{8,4},{12,8},{16,12},{20,16},{24,20},{28,24},{32,28},{36,32}... | collective-permute-start | bytes 1966088 | tf_op jit(solution)/shard_map/ppermute | solution.py:517
  12.0 9.5 %copy-start.16 = (bf16[2,2,1024]{2,1,0:T(2,128)(2,1)S(1)}, bf16[2,2,1024]{2,1,0:T(2,128)(2,1)}, u32[]{:S(2)}) copy-start(bf16[2,2,1024]{2,1,0:T(2,128)(2,1)} %get-tuple-element.55) | copy-start | bytes 24580
  12.0 21.2 %copy-start.17 = (s32[4]{0:T(128)S(1)}, s32[4]{0:T(128)}, u32[]{:S(2)}) copy-start(s32[4]{0:T(128)} %constant.89.clone) | copy-start | bytes 52
  12.0 21.2 %copy-start.18 = (s32[4]{0:T(128)S(1)}, s32[4]{0:T(128)}, u32[]{:S(2)}) copy-start(s32[4]{0:T(128)} %constant.88.clone) | copy-start | bytes 52
  22.3 21.5 %all-to-all-start = ((bf16[32,2,2,1024]{3,2,1,0:T(2,128)(2,1)}), bf16[32,2,2,1024]{3,2,1,0:T(2,128)(2,1)S(1)}, u32[]{:S(2)}, u32[]{:S(2)}) async-start(bf16[32,2,2,1024]{3,2,1,0:T(2,128)(2,1)} %broadcast_in_dim.27), calls=%async_computation | async-start | bytes 524288 | tf_op jit(solution)/shard_map/all_to_all | solution.py:520
  55.4 7.2 %copy-start = (bf16[1024,512]{1,0:T(8,128)(2,1)}, bf16[1024,512]{1,0:T(8,128)(2,1)S(1)}, u32[]{:S(2)}) copy-start(bf16[1024,512]{1,0:T(8,128)(2,1)S(1)} %get-tuple-element.57.refs_0_.refs_1_.refs_2_.refs_3_) | copy-start | bytes 3145732
  62.6 26.1 %collective-permute-start.3 = (bf16[8,2,256,128]{3,2,1,0:T(8,128)(2,1)}, bf16[8,2,256,128]{3,2,1,0:T(8,128)(2,1)S(1)}, u32[]{:S(2)}, u32[]{:S(2)}) collective-permute-start(bf16[8,2,256,128]{3,2,1,0:T(8,128)(2,1)} %get-tuple-element.58), channel_id=1, source_target_pairs={{0,32},{4,36},{8,40},{12,44},{16,48},{20,52},{24,56},{28,60},{32,0... | collective-permute-start | bytes 3145736 | tf_op jit(solution)/shard_map/ppermute | solution.py:480
  65.2 34.9 %collective-permute-start.4 = (bf16[8,2,256,128]{3,2,1,0:T(8,128)(2,1)}, bf16[8,2,256,128]{3,2,1,0:T(8,128)(2,1)S(1)}, u32[]{:S(2)}, u32[]{:S(2)}) collective-permute-start(bf16[8,2,256,128]{3,2,1,0:T(8,128)(2,1)} %get-tuple-element.59), channel_id=1, source_target_pairs={{0,96},{4,100},{8,104},{12,108},{16,112},{20,116},{24,120},{28,124... | collective-permute-start | bytes 3145736 | tf_op jit(solution)/shard_map/ppermute | solution.py:480
  67.3 32.8 %collective-permute-start.5 = (bf16[8,2,256,128]{3,2,1,0:T(8,128)(2,1)}, bf16[8,2,256,128]{3,2,1,0:T(8,128)(2,1)S(1)}, u32[]{:S(2)}, u32[]{:S(2)}) collective-permute-start(bf16[8,2,256,128]{3,2,1,0:T(8,128)(2,1)} %get-tuple-element.60), channel_id=1, source_target_pairs={{0,8},{4,12},{8,0},{12,4},{16,24},{20,28},{24,16},{28,20},{32,40},... | collective-permute-start | bytes 3145736 | tf_op jit(solution)/shard_map/ppermute | solution.py:480
  67.3 32.8 %collective-permute-start.6 = (bf16[8,2,256,128]{3,2,1,0:T(8,128)(2,1)}, bf16[8,2,256,128]{3,2,1,0:T(8,128)(2,1)}, u32[]{:S(2)}, u32[]{:S(2)}) collective-permute-start(bf16[8,2,256,128]{3,2,1,0:T(8,128)(2,1)} %get-tuple-element.61), channel_id=1, source_target_pairs={{0,24},{4,28},{8,16},{12,20},{16,8},{20,12},{24,0},{28,4},{32,56},... | collective-permute-start | bytes 3145736 | tf_op jit(solution)/shard_map/ppermute | solution.py:480
  83.4 30.9 %collective-permute-start.7 = (bf16[2,160,1024]{2,1,0:T(8,128)(2,1)S(1)}, bf16[2,160,1024]{2,1,0:T(8,128)(2,1)S(1)}, u32[]{:S(2)}, u32[]{:S(2)}) collective-permute-start(bf16[2,160,1024]{2,1,0:T(8,128)(2,1)S(1)} %get-tuple-element.75), channel_id=1, source_target_pairs={{0,4},{4,8},{8,12},{12,16},{16,20},{20,24},{24,28},{28,32},{32,36}... | collective-permute-start | bytes 1966088 | tf_op jit(solution)/shard_map/ppermute | solution.py:554
  88.8 11.3 %copy-start.1 = (bf16[8,2,256,128]{3,2,1,0:T(8,128)(2,1)}, bf16[8,2,256,128]{3,2,1,0:T(8,128)(2,1)S(1)}, u32[]{:S(2)}) copy-start(bf16[8,2,256,128]{3,2,1,0:T(8,128)(2,1)S(1)} %collective-permute-done.3.refs_12_.refs_8_) | copy-start | bytes 3145732
  88.8 26.2 %collective-permute-start.8 = (bf16[2,160,1024]{2,1,0:T(8,128)(2,1)S(1)}, bf16[2,160,1024]{2,1,0:T(8,128)(2,1)S(1)}, u32[]{:S(2)}, u32[]{:S(2)}) collective-permute-start(bf16[2,160,1024]{2,1,0:T(8,128)(2,1)S(1)} %get-tuple-element.76), channel_id=1, source_target_pairs={{4,0},{8,4},{12,8},{16,12},{20,16},{24,20},{28,24},{32,28},{36,32}... | collective-permute-start | bytes 1966088 | tf_op jit(solution)/shard_map/ppermute | solution.py:555
  104.8 16.1 %collective-permute-start.9 = (bf16[4,2,256,128]{3,2,1,0:T(8,128)(2,1)S(1)}, bf16[4,2,256,128]{3,2,1,0:T(8,128)(2,1)S(1)}, u32[]{:S(2)}, u32[]{:S(2)}) collective-permute-start(bf16[4,2,256,128]{3,2,1,0:T(8,128)(2,1)S(1)} %get-tuple-element.71), channel_id=1, source_target_pairs={{0,96},{4,100},{8,104},{12,108},{16,112},{20,116},{24,120},{28,124... | collective-permute-start | bytes 1572872 | tf_op jit(solution)/shard_map/ppermute | solution.py:480
  110.9 11.4 %collective-permute-start.10 = (bf16[4,2,256,128]{3,2,1,0:T(8,128)(2,1)S(1)}, bf16[4,2,256,128]{3,2,1,0:T(8,128)(2,1)S(1)}, u32[]{:S(2)}, u32[]{:S(2)}) collective-permute-start(bf16[4,2,256,128]{3,2,1,0:T(8,128)(2,1)S(1)} %get-tuple-element.72), channel_id=1, source_target_pairs={{0,32},{4,36},{8,40},{12,44},{16,48},{20,52},{24,56},{28,60},{32,0... | collective-permute-start | bytes 1572872 | tf_op jit(solution)/shard_map/ppermute | solution.py:480
  111.1 12.4 %collective-permute-start.11 = (bf16[4,2,256,128]{3,2,1,0:T(8,128)(2,1)S(1)}, bf16[4,2,256,128]{3,2,1,0:T(8,128)(2,1)S(1)}, u32[]{:S(2)}, u32[]{:S(2)}) collective-permute-start(bf16[4,2,256,128]{3,2,1,0:T(8,128)(2,1)S(1)} %get-tuple-element.73), channel_id=1, source_target_pairs={{0,24},{4,28},{8,16},{12,20},{16,8},{20,12},{24,0},{28,4},{32,56},... | collective-permute-start | bytes 1572872 | tf_op jit(solution)/shard_map/ppermute | solution.py:480
  114.3 14.2 %copy-start.14 = (bf16[2,160,1024]{2,1,0:T(8,128)(2,1)}, bf16[2,160,1024]{2,1,0:T(8,128)(2,1)S(1)}, u32[]{:S(2)}) copy-start(bf16[2,160,1024]{2,1,0:T(8,128)(2,1)S(1)} %collective-permute-done.7.left_ref) | copy-start | bytes 1966084
  114.3 10.7 %collective-permute-start.12 = (bf16[4,2,256,128]{3,2,1,0:T(8,128)(2,1)S(1)}, bf16[4,2,256,128]{3,2,1,0:T(8,128)(2,1)S(1)}, u32[]{:S(2)}, u32[]{:S(2)}) collective-permute-start(bf16[4,2,256,128]{3,2,1,0:T(8,128)(2,1)S(1)} %get-tuple-element.74), channel_id=1, source_target_pairs={{0,8},{4,12},{8,0},{12,4},{16,24},{20,28},{24,16},{28,20},{32,40},... | collective-permute-start | bytes 1572872 | tf_op jit(solution)/shard_map/ppermute | solution.py:480
  114.9 13.6 %copy-start.15 = (bf16[2,160,1024]{2,1,0:T(8,128)(2,1)}, bf16[2,160,1024]{2,1,0:T(8,128)(2,1)S(1)}, u32[]{:S(2)}) copy-start(bf16[2,160,1024]{2,1,0:T(8,128)(2,1)S(1)} %collective-permute-done.8.right_ref) | copy-start | bytes 1966084
  114.9 15.5 %collective-permute-start.14 = (bf16[256,1024]{1,0:T(8,128)(2,1)S(1)}, bf16[256,1024]{1,0:T(8,128)(2,1)S(1)}, u32[]{:S(2)}, u32[]{:S(2)}) collective-permute-start(bf16[256,1024]{1,0:T(8,128)(2,1)S(1)} %get-tuple-element.81), channel_id=1, source_target_pairs={{0,1},{1,0},{2,3},{3,2},{4,5},{5,4},{6,7},{7,6},{8,9},{9,8},{10,11... | collective-permute-start | bytes 1572872 | tf_op jit(solution)/shard_map/ppermute | solution.py:480
  120.9 7.6 %copy-start.6 = (bf16[4,2,256,128]{3,2,1,0:T(8,128)(2,1)}, bf16[4,2,256,128]{3,2,1,0:T(8,128)(2,1)S(1)}, u32[]{:S(2)}) copy-start(bf16[4,2,256,128]{3,2,1,0:T(8,128)(2,1)S(1)} %collective-permute-done.9.refs_16_.refs_12_) | copy-start | bytes 1572868
  120.9 9.6 %collective-permute-start.13 = (bf16[256,1024]{1,0:T(8,128)(2,1)S(1)}, bf16[256,1024]{1,0:T(8,128)(2,1)S(1)}, u32[]{:S(2)}, u32[]{:S(2)}) collective-permute-start(bf16[256,1024]{1,0:T(8,128)(2,1)S(1)} %get-tuple-element.69), channel_id=1, source_target_pairs={{0,1},{1,0},{2,3},{3,2},{4,5},{5,4},{6,7},{7,6},{8,9},{9,8},{10,11... | collective-permute-start | bytes 1572872 | tf_op jit(solution)/shard_map/ppermute | solution.py:480
  122.3 8.1 %copy-start.12 = (bf16[512,1024]{1,0:T(8,128)(2,1)S(1)}, bf16[512,1024]{1,0:T(8,128)(2,1)}, u32[]{:S(2)}) copy-start(bf16[512,1024]{1,0:T(8,128)(2,1)} %get-tuple-element.80) | copy-start | bytes 3145732
  122.3 50.4 %collective-permute-start.2 = (bf16[512,1024]{1,0:T(8,128)(2,1)}, bf16[512,1024]{1,0:T(8,128)(2,1)}, u32[]{:S(2)}, u32[]{:S(2)}) collective-permute-start(bf16[512,1024]{1,0:T(8,128)(2,1)} %get-tuple-element.67), channel_id=1, source_target_pairs={{0,1},{1,0},{2,3},{3,2},{4,5},{5,4},{6,7},{7,6},{8,9},{9,8},{10,11... | collective-permute-start | bytes 3145736 | tf_op jit(solution)/shard_map/ppermute | solution.py:480
  128.6 11.8 %collective-permute-start.16 = (bf16[2,2,512,128]{3,2,1,0:T(8,128)(2,1)S(1)}, bf16[2,2,512,128]{3,2,1,0:T(8,128)(2,1)S(1)}, u32[]{:S(2)}, u32[]{:S(2)}) collective-permute-start(bf16[2,2,512,128]{3,2,1,0:T(8,128)(2,1)S(1)} %get-tuple-element.78), channel_id=1, source_target_pairs={{0,8},{4,12},{8,0},{12,4},{16,24},{20,28},{24,16},{28,20},{32,40},... | collective-permute-start | bytes 1572872 | tf_op jit(solution)/shard_map/ppermute | solution.py:480
  129.3 12.3 %collective-permute-start.17 = (bf16[2,2,512,128]{3,2,1,0:T(8,128)(2,1)S(1)}, bf16[2,2,512,128]{3,2,1,0:T(8,128)(2,1)S(1)}, u32[]{:S(2)}, u32[]{:S(2)}) collective-permute-start(bf16[2,2,512,128]{3,2,1,0:T(8,128)(2,1)S(1)} %get-tuple-element.79), channel_id=1, source_target_pairs={{0,96},{4,100},{8,104},{12,108},{16,112},{20,116},{24,120},{28,124... | collective-permute-start | bytes 1572872 | tf_op jit(solution)/shard_map/ppermute | solution.py:480
  130.9 41.8 %collective-permute-start.15 = (bf16[512,1024]{1,0:T(8,128)(2,1)S(1)}, bf16[512,1024]{1,0:T(8,128)(2,1)}, u32[]{:S(2)}, u32[]{:S(2)}) collective-permute-start(bf16[512,1024]{1,0:T(8,128)(2,1)S(1)} %add_convert_fusion.1), channel_id=1, source_target_pairs={{0,2},{1,3},{2,0},{3,1},{4,6},{5,7},{6,4},{7,5},{8,10},{9,11},{10,... | collective-permute-start | bytes 3145736 | tf_op jit(solution)/shard_map/ppermute | solution.py:480
  144.6 11.3 %collective-permute-start.18 = (bf16[1,2,512,128]{3,2,1,0:T(8,128)(2,1)S(1)}, bf16[1,2,512,128]{3,2,1,0:T(8,128)(2,1)S(1)}, u32[]{:S(2)}, u32[]{:S(2)}) collective-permute-start(bf16[1,2,512,128]{3,2,1,0:T(8,128)(2,1)S(1)} %get-tuple-element.89), channel_id=1, source_target_pairs={{0,24},{4,28},{8,16},{12,20},{16,8},{20,12},{24,0},{28,4},{32,56},... | collective-permute-start | bytes 786440 | tf_op jit(solution)/shard_map/ppermute | solution.py:480
  145.3 10.7 %collective-permute-start.19 = (bf16[1,2,512,128]{3,2,1,0:T(8,128)(2,1)S(1)}, bf16[1,2,512,128]{3,2,1,0:T(8,128)(2,1)S(1)}, u32[]{:S(2)}, u32[]{:S(2)}) collective-permute-start(bf16[1,2,512,128]{3,2,1,0:T(8,128)(2,1)S(1)} %get-tuple-element.90), channel_id=1, source_target_pairs={{0,32},{4,36},{8,40},{12,44},{16,48},{20,52},{24,56},{28,60},{32,0... | collective-permute-start | bytes 786440 | tf_op jit(solution)/shard_map/ppermute | solution.py:480
  146.2 20.2 %all-to-all-start.1 = ((bf16[32,2,2,1024]{3,2,1,0:T(2,128)(2,1)}), bf16[32,2,2,1024]{3,2,1,0:T(2,128)(2,1)S(1)}, u32[]{:S(2)}, u32[]{:S(2)}) async-start(bf16[32,2,2,1024]{3,2,1,0:T(2,128)(2,1)} %bitcast.7), calls=%async_computation.1 | async-start | bytes 524288 | tf_op jit(solution)/shard_map/all_to_all | solution.py:569
  159.1 12.8 %collective-permute-start.20 = (bf16[1024,128]{1,0:T(8,128)(2,1)S(1)}, bf16[1024,128]{1,0:T(8,128)(2,1)S(1)}, u32[]{:S(2)}, u32[]{:S(2)}) collective-permute-start(bf16[1024,128]{1,0:T(8,128)(2,1)S(1)} %get-tuple-element.92), channel_id=1, source_target_pairs={{0,4},{4,0},{8,12},{12,8},{16,20},{20,16},{24,28},{28,24},{32,36},... | collective-permute-start | bytes 786440 | tf_op jit(solution)/shard_map/ppermute | solution.py:480
  (10 other events, 38.8 us)

commit v6 on v5

--- a/solution.py
+++ b/solution.py
@@ -531,7 +531,7 @@
     attt = [attt]
 
     def first_axis(step, dep):
-        start, per = (8, 2) if step == 0 else (4, 2)
+        start, per = (8, 4) if step == 0 else (4, 2)
         got = [recv1][:step]
         out = weight_step(after(cols, *dep), attt, out_grad, part, every, start, start, per, got, False)
         for u, x in enumerate(out):

time: 177 us -> 176 us (level)
  no operation moved by 1% of the time
where the time goes in v6:
time: 176 us; the launch traced here: 175 us
  Pallas kernels  72.7 us (41%)
  starting transfers between devices  54.7 us (31%)
  waiting for transfers between devices  36.8 us (21%)
  other arithmetic  5.62 us (3%)
  local copies, waits for them, and re-layouts  4.61 us (3%)
    ppermute x17, starting transfers between devices, swap(): return lax.ppermute(x, axis, [(i, i ^ bits) for i in range(n)])  20.9 us
    ppermute x17, waiting for transfers between devices, swap(): return lax.ppermute(x, axis, [(i, i ^ bits) for i in range(n)])  20.2 us
    pallas_call x4, Pallas kernels, weight_step(): pl.pallas_call(functools.partial(weight_kernel, n, per, len(recvs) * n, p...  17.7 us
    pallas_call x1, Pallas kernels, backward(): pl.pallas_call(functools.partial(bwd_kernel, seq_count), grid_spec=pltpu....  14.5 us
    all_to_all x1, starting transfers between devices, shards(): far_all = lax.all_to_all(far_all, 'seq', 0, 0, tiled=True)  10.9 us
    all_to_all x1, waiting for transfers between devices, shards(): far_all = lax.all_to_all(far_all, 'seq', 0, 0, tiled=True)  10 us
    pallas_call x1, Pallas kernels, layer_parts(): pl.pallas_call(layer_kernel, grid_spec=pltpu.PrefetchScalarGridSpec(num_s...  9.85 us
    all_to_all x1, starting transfers between devices, shards(): lax.all_to_all(far_parts, 'seq', 0, 0, tiled=True).astype(F32).sum(axis=0)  9.51 us
  transfers between devices with their start and end apart: 23, of which 10 were waited for; matrix products, arithmetic and copies ran while one was open for 3% of the time, Pallas kernels for 30%

profile of v6, /device:TPU:0, one launch (start us, length us, event | category | flops | bytes accessed | tf_op | source)
XLA Modules:
  0.0 175.5 jit_solution(11126882906141249079)
XLA Ops:
  0.6 4.1 %pool.1 = (bf16[2,32,1024]{2,1,0:T(8,128)(2,1)}, bf16[2,2,1024]{2,1,0:T(2,128)(2,1)}, bf16[2,160,1024]{2,1,0:T(8,128)(2,1)}, bf16[2,160,1024]{2,1,0:T(8,128)(2,1)}) custom-call(bf16[512,1024]{1,0:T(8,128)(2,1)} %k_ref.5, bf16[512,1024]{1,0:T(8,128)(2,1)} %v_ref.5), custom_call_target="tpu_custom_call" | custom-call | flops 1000 | bytes 1000 | tf_op jit(solution)/shard_map/pool/pallas_call | solution.py:59
  4.8 5.9 %collective-permute-start = (bf16[2,160,1024]{2,1,0:T(8,128)(2,1)}, bf16[2,160,1024]{2,1,0:T(8,128)(2,1)S(1)}, u32[]{:S(2)}, u32[]{:S(2)}) collective-permute-start(bf16[2,160,1024]{2,1,0:T(8,128)(2,1)} %get-tuple-element.52), channel_id=1, source_target_pairs={{0,4},{4,8},{8,12},{12,16},{16,20},{20,24},{24,28},{28,32},{32,36}... | collective-permute-start | bytes 1966088 | tf_op jit(solution)/shard_map/ppermute | solution.py:516
  10.7 1.3 collective-permute-start.1
  12.0 9.4 %project.1.do_ref = bf16[512,1024]{1,0:T(8,128)(2,1)} custom-call(bf16[512,4096]{1,0:T(8,128)(2,1)} %refs_7_.9, bf16[1024,4096]{1,0:T(8,128)(2,1)} %w_ref.3), custom_call_target="tpu_custom_call" | custom-call | flops 1000 | bytes 1000 | tf_op jit(solution)/shard_map/project/pallas_call | solution.py:425
  22.3 10.9 %all-to-all-start = ((bf16[32,2,2,1024]{3,2,1,0:T(2,128)(2,1)}), bf16[32,2,2,1024]{3,2,1,0:T(2,128)(2,1)S(1)}, u32[]{:S(2)}, u32[]{:S(2)}) async-start(bf16[32,2,2,1024]{3,2,1,0:T(2,128)(2,1)} %broadcast_in_dim.27), calls=%async_computation | async-start | bytes 524288 | tf_op jit(solution)/shard_map/all_to_all | solution.py:520
  33.8 10.0 %all-to-all-done = bf16[32,2,2,1024]{3,2,1,0:T(2,128)(2,1)S(1)} async-done(((bf16[32,2,2,1024]{3,2,1,0:T(2,128)(2,1)}), bf16[32,2,2,1024]{3,2,1,0:T(2,128)(2,1)S(1)}, u32[]{:S(2)}, u32[]{:S(2)}) %all-to-all-start) | async-done | bytes 262176 | tf_op jit(solution)/shard_map/all_to_all | solution.py:520
  46.0 9.4 %attend.1 = (bf16[512,1024]{1,0:T(8,128)(2,1)}, bf16[1024,512]{1,0:T(8,128)(2,1)S(1)}, f32[8,1,512]{2,1,0:T(1,128)S(1)}) custom-call(s32[1]{0:T(128)} %bitcast.2.pos_ref, bf16[512,1024]{1,0:T(8,128)(2,1)} %q_ref.1, bf16[512,1024]{1,0:T(8,128)(2,1)} %k_ref.5, bf16[512,1024]{1,0:T(8,128)(2,1)} %v_ref.5, bf16[2,160,1024]{2,1,0:T(8,128)(2,1)} %copy-done.10, ...), custom_call_target="tpu_custom_call" | custom-call | flops 1000 | bytes 1000 | tf_op jit(solution)/shard_map/attend/pallas_call | solution.py:183
  55.4 6.7 %weight_step.4 = (bf16[8,2,256,128]{3,2,1,0:T(8,128)(2,1)}, bf16[8,2,256,128]{3,2,1,0:T(8,128)(2,1)}, bf16[8,2,256,128]{3,2,1,0:T(8,128)(2,1)}, bf16[8,2,256,128]{3,2,1,0:T(8,128)(2,1)}) custom-call(s32[4,16]{1,0:T(4,128)S(1)} %pad_add_fusion.cols_ref, bf16[1024,512]{1,0:T(8,128)(2,1)S(1)} %get-tuple-element.57.refs_0_.refs_1_.refs_2_.refs_3_, ...), custom_call_target="tpu_custom_call" | custom-call | flops 1000 | bytes 1000 | tf_op jit(solution)/shard_map/weight_step/pallas_call | solution.py:339
  62.2 2.6 %collective-permute-start.3 = (bf16[8,2,256,128]{3,2,1,0:T(8,128)(2,1)}, bf16[8,2,256,128]{3,2,1,0:T(8,128)(2,1)S(1)}, u32[]{:S(2)}, u32[]{:S(2)}) collective-permute-start(bf16[8,2,256,128]{3,2,1,0:T(8,128)(2,1)} %get-tuple-element.58), channel_id=1, source_target_pairs={{0,32},{4,36},{8,40},{12,44},{16,48},{20,52},{24,56},{28,60},{32,0... | collective-permute-start | bytes 3145736 | tf_op jit(solution)/shard_map/ppermute | solution.py:480
  64.7 2.1 %collective-permute-start.4 = (bf16[8,2,256,128]{3,2,1,0:T(8,128)(2,1)}, bf16[8,2,256,128]{3,2,1,0:T(8,128)(2,1)S(1)}, u32[]{:S(2)}, u32[]{:S(2)}) collective-permute-start(bf16[8,2,256,128]{3,2,1,0:T(8,128)(2,1)} %get-tuple-element.59), channel_id=1, source_target_pairs={{0,96},{4,100},{8,104},{12,108},{16,112},{20,116},{24,120},{28,124... | collective-permute-start | bytes 3145736 | tf_op jit(solution)/shard_map/ppermute | solution.py:480
  66.8 1.6 collective-permute-start.6
  68.4 14.5 %attend_grad.1 = (bf16[512,1024]{1,0:T(8,128)(2,1)}, f32[512,1024]{1,0:T(8,128)}, f32[512,1024]{1,0:T(8,128)}, bf16[2,160,1024]{2,1,0:T(8,128)(2,1)S(1)}, bf16[2...) custom-call(s32[1]{0:T(128)} %bitcast.2.pos_ref, bf16[512,1024]{1,0:T(8,128)(2,1)} %q_ref.1, ...), custom_call_target="tpu_custom_call" | custom-call | flops 1000 | bytes 1000 | tf_op jit(solution)/shard_map/attend_grad/pallas_call | solution.py:213
  82.9 4.9 %collective-permute-start.7 = (bf16[2,160,1024]{2,1,0:T(8,128)(2,1)S(1)}, bf16[2,160,1024]{2,1,0:T(8,128)(2,1)S(1)}, u32[]{:S(2)}, u32[]{:S(2)}) collective-permute-start(bf16[2,160,1024]{2,1,0:T(8,128)(2,1)S(1)} %get-tuple-element.75), channel_id=1, source_target_pairs={{0,4},{4,8},{8,12},{12,16},{16,20},{20,24},{24,28},{28,32},{32,36}... | collective-permute-start | bytes 1966088 | tf_op jit(solution)/shard_map/ppermute | solution.py:554
  88.3 1.3 collective-permute-start.8
  89.7 9.9 %layer_parts.1 = (bf16[256,1024]{1,0:T(8,128)(2,1)S(1)}, bf16[256,1024]{1,0:T(8,128)(2,1)S(1)}, bf16[512,1024]{1,0:T(8,128)(2,1)}, bf16[512,1024]{1,0:T(8,128)(2,1)}, bf16[512,1024]{1,0:T(8,128)(2,1)}) custom-call(s32[4]{0:T(128)S(1)} %pad_add_fusion.1.cols_ref, bf16[512,1024]{1,0:T(8,128)(2,1)} %get-tuple-element.65.att_ref, bf16[1024,4096]{1,0:T(8,128)(2,1)} %w_ref.3), custom_call_target="tpu_custom_call" | custom-call | flops 1000 | bytes 1000 | tf_op jit(solution)/shard_map/layer_parts/pallas_call | solution.py:459
  99.6 4.6 %weight_step.5 = (bf16[4,2,256,128]{3,2,1,0:T(8,128)(2,1)S(1)}, bf16[4,2,256,128]{3,2,1,0:T(8,128)(2,1)S(1)}, bf16[4,2,256,128]{3,2,1,0:T(8,128)(2,1)S(1)}, bf16[4,2,256,128]{3,2,1,0:T(8,128)(2,1)S(1)}) custom-call(s32[4,16]{1,0:T(4,128)S(1)} %pad_add_fusion.cols_ref, bf16[1024,512]{1,0:T(8,128)(2,1)} %copy-done, bf16[1024,512]{1,0:T(8,128)(2,1)} %copy-done, ...), custom_call_target="tpu_custom_call" | custom-call | flops 1000 | bytes 1000 | tf_op jit(solution)/shard_map/weight_step/pallas_call | solution.py:339
  104.3 6.2 %collective-permute-start.9 = (bf16[4,2,256,128]{3,2,1,0:T(8,128)(2,1)S(1)}, bf16[4,2,256,128]{3,2,1,0:T(8,128)(2,1)S(1)}, u32[]{:S(2)}, u32[]{:S(2)}) collective-permute-start(bf16[4,2,256,128]{3,2,1,0:T(8,128)(2,1)S(1)} %get-tuple-element.71), channel_id=1, source_target_pairs={{0,96},{4,100},{8,104},{12,108},{16,112},{20,116},{24,120},{28,124... | collective-permute-start | bytes 1572872 | tf_op jit(solution)/shard_map/ppermute | solution.py:480
  111.2 2.6 %collective-permute-done.7.left_ref = bf16[2,160,1024]{2,1,0:T(8,128)(2,1)S(1)} collective-permute-done((bf16[2,160,1024]{2,1,0:T(8,128)(2,1)S(1)}, bf16[2,160,1024]{2,1,0:T(8,128)(2,1)S(1)}, u32[]{:S(2)}, u32[]{:S(2)}) %collective-permute-start.7) | collective-permute-done | bytes 655392 | tf_op jit(solution)/shard_map/ppermute | solution.py:554
  114.5 5.9 %collective-permute-done.9.refs_16_.refs_12_ = bf16[4,2,256,128]{3,2,1,0:T(8,128)(2,1)S(1)} collective-permute-done((bf16[4,2,256,128]{3,2,1,0:T(8,128)(2,1)S(1)}, bf16[4,2,256,128]{3,2,1,0:T(8,128)(2,1)S(1)}, u32[]{:S(2)}, u32[]{:S(2)}) %collective-permute-start.9) | collective-permute-done | bytes 524320 | tf_op jit(solution)/shard_map/ppermute | solution.py:480
  120.4 1.5 collective-permute-done.10.refs_17_.refs_13_
  121.9 1.2 collective-permute-done.11.refs_18_.refs_14_
  123.1 1.4 collective-permute-done.12.refs_19_.refs_15_
  124.5 3.5 %weight_step.6 = (bf16[2,2,512,128]{3,2,1,0:T(8,128)(2,1)S(1)}, bf16[2,2,512,128]{3,2,1,0:T(8,128)(2,1)S(1)}) custom-call(s32[4,16]{1,0:T(4,128)S(1)} %pad_add_fusion.cols_ref, bf16[1024,512]{1,0:T(8,128)(2,1)} %copy-done, bf16[1024,512]{1,0:T(8,128)(2,1)} %copy-done, bf16[1024,512]{1,0:T(8,128)(2,1)} %copy-done, bf16[1024,512]{1,0:T(8,128)(2,1)} %copy-done, ...), custom_call_target="tpu_custom_call" | custom-call | flops 1000 | bytes 1000 | tf_op jit(solution)/shard_map/weight_step/pallas_call | solution.py:339
  131.6 8.3 %collective-permute-done.16.refs_16_.refs_17_ = bf16[2,2,512,128]{3,2,1,0:T(8,128)(2,1)S(1)} collective-permute-done((bf16[2,2,512,128]{3,2,1,0:T(8,128)(2,1)S(1)}, bf16[2,2,512,128]{3,2,1,0:T(8,128)(2,1)S(1)}, u32[]{:S(2)}, u32[]{:S(2)}) %collective-permute-start.16) | collective-permute-done | bytes 524320 | tf_op jit(solution)/shard_map/ppermute | solution.py:480
  139.9 1.3 collective-permute-done.17.refs_18_.refs_19_
  141.2 2.9 %weight_step.7 = (bf16[1,2,512,128]{3,2,1,0:T(8,128)(2,1)S(1)}, bf16[1,2,512,128]{3,2,1,0:T(8,128)(2,1)S(1)}) custom-call(s32[4,16]{1,0:T(4,128)S(1)} %pad_add_fusion.cols_ref, bf16[1024,512]{1,0:T(8,128)(2,1)} %copy-done, bf16[1024,512]{1,0:T(8,128)(2,1)} %copy-done, bf16[1024,512]{1,0:T(8,128)(2,1)} %copy-done, bf16[1024,512]{1,0:T(8,128)(2,1)} %copy-done, ...), custom_call_target="tpu_custom_call" | custom-call | flops 1000 | bytes 1000 | tf_op jit(solution)/shard_map/weight_step/pallas_call | solution.py:339
  145.8 9.5 %all-to-all-start.1 = ((bf16[32,2,2,1024]{3,2,1,0:T(2,128)(2,1)}), bf16[32,2,2,1024]{3,2,1,0:T(2,128)(2,1)S(1)}, u32[]{:S(2)}, u32[]{:S(2)}) async-start(bf16[32,2,2,1024]{3,2,1,0:T(2,128)(2,1)} %bitcast.7), calls=%async_computation.1 | async-start | bytes 524288 | tf_op jit(solution)/shard_map/all_to_all | solution.py:569
  155.5 3.2 %weight_last.1 = (bf16[1024,128]{1,0:T(8,128)(2,1)S(1)}, f32[1024,128]{1,0:T(8,128)S(1)}) custom-call(s32[5]{0:T(128)S(1)} %pad_add_fusion.2.table_ref, bf16[1024,512]{1,0:T(8,128)(2,1)} %copy-done, bf16[1024,512]{1,0:T(8,128)(2,1)} %copy-done, bf16[1024,512]{1,0:T(8,128)(2,1)} %copy-done, bf16[1024,512]{1,0:T(8,128)(2,1)} %copy-done, ...), custom_call_target="tpu_custom_call" | custom-call | flops 1000 | bytes 1000 | tf_op jit(solution)/shard_map/weight_last/pallas_call | solution.py:395
  158.7 3.4 %collective-permute-start.20 = (bf16[1024,128]{1,0:T(8,128)(2,1)S(1)}, bf16[1024,128]{1,0:T(8,128)(2,1)S(1)}, u32[]{:S(2)}, u32[]{:S(2)}) collective-permute-start(bf16[1024,128]{1,0:T(8,128)(2,1)S(1)} %get-tuple-element.92), channel_id=1, source_target_pairs={{0,4},{4,0},{8,12},{12,8},{16,20},{20,16},{24,28},{28,24},{32,36},... | collective-permute-start | bytes 786440 | tf_op jit(solution)/shard_map/ppermute | solution.py:480
  162.1 4.0 %all-to-all-done.1 = bf16[32,2,2,1024]{3,2,1,0:T(2,128)(2,1)S(1)} async-done(((bf16[32,2,2,1024]{3,2,1,0:T(2,128)(2,1)}), bf16[32,2,2,1024]{3,2,1,0:T(2,128)(2,1)S(1)}, u32[]{:S(2)}, u32[]{:S(2)}) %all-to-all-start.1) | async-done | bytes 262176 | tf_op jit(solution)/shard_map/all_to_all | solution.py:569
  166.9 4.5 %combine.1 = (bf16[512,1024]{1,0:T(8,128)(2,1)}, bf16[512,1024]{1,0:T(8,128)(2,1)}) custom-call(f32[512,1024]{1,0:T(8,128)} %get-tuple-element.83.gk_ref, f32[512,1024]{1,0:T(8,128)} %get-tuple-element.84.gv_ref, bf16[2,160,1024]{2,1,0:T(8,128)(2,1)} %copy-done.14, bf16[2,160,1024]{2,1,0:T(8,128)(2,1)} %copy-done.15, f32[2,2,1024]{2,1,0:T(2,128)} %convert_reduce_fusion.far_ref), custom_call_target="tpu_custom_call" | custom-call | flops 1000 | bytes 1000 | tf_op jit(solution)/shard_map/combine/pallas_call | solution.py:268
  172.3 3.1 %add_convert_fusion = bf16[512,1024]{1,0:T(8,128)(2,1)} fusion(bf16[512,1024]{1,0:T(8,128)(2,1)} %collective-permute-done.15, bf16[512,1024]{1,0:T(8,128)(2,1)} %collective-permute-done.2, bf16[512,1024]{1,0:T(8,128)(2,1)S(1)} %copy-done.13), kind=kLoop, calls=%fused_computation | loop fusion | flops 3145728 | bytes 4194304 | tf_op jit(solution)/shard_map/convert_element_type | solution.py:574
  (90 shorter events, 12.7 us)
Async XLA Ops:
  4.8 40.0 %collective-permute-start = (bf16[2,160,1024]{2,1,0:T(8,128)(2,1)}, bf16[2,160,1024]{2,1,0:T(8,128)(2,1)S(1)}, u32[]{:S(2)}, u32[]{:S(2)}) collective-permute-start(bf16[2,160,1024]{2,1,0:T(8,128)(2,1)} %get-tuple-element.52), channel_id=1, source_target_pairs={{0,4},{4,8},{8,12},{12,16},{16,20},{20,24},{24,28},{28,32},{32,36}... | collective-permute-start | bytes 1966088 | tf_op jit(solution)/shard_map/ppermute | solution.py:516
  10.7 34.1 %collective-permute-start.1 = (bf16[2,160,1024]{2,1,0:T(8,128)(2,1)}, bf16[2,160,1024]{2,1,0:T(8,128)(2,1)S(1)}, u32[]{:S(2)}, u32[]{:S(2)}) collective-permute-start(bf16[2,160,1024]{2,1,0:T(8,128)(2,1)} %get-tuple-element.53), channel_id=1, source_target_pairs={{4,0},{8,4},{12,8},{16,12},{20,16},{24,20},{28,24},{32,28},{36,32}... | collective-permute-start | bytes 1966088 | tf_op jit(solution)/shard_map/ppermute | solution.py:517
  12.0 9.5 %copy-start.16 = (bf16[2,2,1024]{2,1,0:T(2,128)(2,1)S(1)}, bf16[2,2,1024]{2,1,0:T(2,128)(2,1)}, u32[]{:S(2)}) copy-start(bf16[2,2,1024]{2,1,0:T(2,128)(2,1)} %get-tuple-element.55) | copy-start | bytes 24580
  12.0 21.2 %copy-start.17 = (s32[4]{0:T(128)S(1)}, s32[4]{0:T(128)}, u32[]{:S(2)}) copy-start(s32[4]{0:T(128)} %constant.89.clone) | copy-start | bytes 52
  12.0 21.2 %copy-start.18 = (s32[4]{0:T(128)S(1)}, s32[4]{0:T(128)}, u32[]{:S(2)}) copy-start(s32[4]{0:T(128)} %constant.88.clone) | copy-start | bytes 52
  22.3 21.5 %all-to-all-start = ((bf16[32,2,2,1024]{3,2,1,0:T(2,128)(2,1)}), bf16[32,2,2,1024]{3,2,1,0:T(2,128)(2,1)S(1)}, u32[]{:S(2)}, u32[]{:S(2)}) async-start(bf16[32,2,2,1024]{3,2,1,0:T(2,128)(2,1)} %broadcast_in_dim.27), calls=%async_computation | async-start | bytes 524288 | tf_op jit(solution)/shard_map/all_to_all | solution.py:520
  55.4 6.7 %copy-start = (bf16[1024,512]{1,0:T(8,128)(2,1)}, bf16[1024,512]{1,0:T(8,128)(2,1)S(1)}, u32[]{:S(2)}) copy-start(bf16[1024,512]{1,0:T(8,128)(2,1)S(1)} %get-tuple-element.57.refs_0_.refs_1_.refs_2_.refs_3_) | copy-start | bytes 3145732
  62.2 26.1 %collective-permute-start.3 = (bf16[8,2,256,128]{3,2,1,0:T(8,128)(2,1)}, bf16[8,2,256,128]{3,2,1,0:T(8,128)(2,1)S(1)}, u32[]{:S(2)}, u32[]{:S(2)}) collective-permute-start(bf16[8,2,256,128]{3,2,1,0:T(8,128)(2,1)} %get-tuple-element.58), channel_id=1, source_target_pairs={{0,32},{4,36},{8,40},{12,44},{16,48},{20,52},{24,56},{28,60},{32,0... | collective-permute-start | bytes 3145736 | tf_op jit(solution)/shard_map/ppermute | solution.py:480
  64.7 34.9 %collective-permute-start.4 = (bf16[8,2,256,128]{3,2,1,0:T(8,128)(2,1)}, bf16[8,2,256,128]{3,2,1,0:T(8,128)(2,1)S(1)}, u32[]{:S(2)}, u32[]{:S(2)}) collective-permute-start(bf16[8,2,256,128]{3,2,1,0:T(8,128)(2,1)} %get-tuple-element.59), channel_id=1, source_target_pairs={{0,96},{4,100},{8,104},{12,108},{16,112},{20,116},{24,120},{28,124... | collective-permute-start | bytes 3145736 | tf_op jit(solution)/shard_map/ppermute | solution.py:480
  66.8 32.8 %collective-permute-start.5 = (bf16[8,2,256,128]{3,2,1,0:T(8,128)(2,1)}, bf16[8,2,256,128]{3,2,1,0:T(8,128)(2,1)S(1)}, u32[]{:S(2)}, u32[]{:S(2)}) collective-permute-start(bf16[8,2,256,128]{3,2,1,0:T(8,128)(2,1)} %get-tuple-element.60), channel_id=1, source_target_pairs={{0,8},{4,12},{8,0},{12,4},{16,24},{20,28},{24,16},{28,20},{32,40},... | collective-permute-start | bytes 3145736 | tf_op jit(solution)/shard_map/ppermute | solution.py:480
  66.8 32.8 %collective-permute-start.6 = (bf16[8,2,256,128]{3,2,1,0:T(8,128)(2,1)}, bf16[8,2,256,128]{3,2,1,0:T(8,128)(2,1)}, u32[]{:S(2)}, u32[]{:S(2)}) collective-permute-start(bf16[8,2,256,128]{3,2,1,0:T(8,128)(2,1)} %get-tuple-element.61), channel_id=1, source_target_pairs={{0,24},{4,28},{8,16},{12,20},{16,8},{20,12},{24,0},{28,4},{32,56},... | collective-permute-start | bytes 3145736 | tf_op jit(solution)/shard_map/ppermute | solution.py:480
  82.9 30.9 %collective-permute-start.7 = (bf16[2,160,1024]{2,1,0:T(8,128)(2,1)S(1)}, bf16[2,160,1024]{2,1,0:T(8,128)(2,1)S(1)}, u32[]{:S(2)}, u32[]{:S(2)}) collective-permute-start(bf16[2,160,1024]{2,1,0:T(8,128)(2,1)S(1)} %get-tuple-element.75), channel_id=1, source_target_pairs={{0,4},{4,8},{8,12},{12,16},{16,20},{20,24},{24,28},{28,32},{32,36}... | collective-permute-start | bytes 1966088 | tf_op jit(solution)/shard_map/ppermute | solution.py:554
  88.3 11.3 %copy-start.1 = (bf16[8,2,256,128]{3,2,1,0:T(8,128)(2,1)}, bf16[8,2,256,128]{3,2,1,0:T(8,128)(2,1)S(1)}, u32[]{:S(2)}) copy-start(bf16[8,2,256,128]{3,2,1,0:T(8,128)(2,1)S(1)} %collective-permute-done.3.refs_12_.refs_8_) | copy-start | bytes 3145732
  88.3 26.2 %collective-permute-start.8 = (bf16[2,160,1024]{2,1,0:T(8,128)(2,1)S(1)}, bf16[2,160,1024]{2,1,0:T(8,128)(2,1)S(1)}, u32[]{:S(2)}, u32[]{:S(2)}) collective-permute-start(bf16[2,160,1024]{2,1,0:T(8,128)(2,1)S(1)} %get-tuple-element.76), channel_id=1, source_target_pairs={{4,0},{8,4},{12,8},{16,12},{20,16},{24,20},{28,24},{32,28},{36,32}... | collective-permute-start | bytes 1966088 | tf_op jit(solution)/shard_map/ppermute | solution.py:555
  104.3 16.1 %collective-permute-start.9 = (bf16[4,2,256,128]{3,2,1,0:T(8,128)(2,1)S(1)}, bf16[4,2,256,128]{3,2,1,0:T(8,128)(2,1)S(1)}, u32[]{:S(2)}, u32[]{:S(2)}) collective-permute-start(bf16[4,2,256,128]{3,2,1,0:T(8,128)(2,1)S(1)} %get-tuple-element.71), channel_id=1, source_target_pairs={{0,96},{4,100},{8,104},{12,108},{16,112},{20,116},{24,120},{28,124... | collective-permute-start | bytes 1572872 | tf_op jit(solution)/shard_map/ppermute | solution.py:480
  110.5 11.4 %collective-permute-start.10 = (bf16[4,2,256,128]{3,2,1,0:T(8,128)(2,1)S(1)}, bf16[4,2,256,128]{3,2,1,0:T(8,128)(2,1)S(1)}, u32[]{:S(2)}, u32[]{:S(2)}) collective-permute-start(bf16[4,2,256,128]{3,2,1,0:T(8,128)(2,1)S(1)} %get-tuple-element.72), channel_id=1, source_target_pairs={{0,32},{4,36},{8,40},{12,44},{16,48},{20,52},{24,56},{28,60},{32,0... | collective-permute-start | bytes 1572872 | tf_op jit(solution)/shard_map/ppermute | solution.py:480
  110.6 12.4 %collective-permute-start.11 = (bf16[4,2,256,128]{3,2,1,0:T(8,128)(2,1)S(1)}, bf16[4,2,256,128]{3,2,1,0:T(8,128)(2,1)S(1)}, u32[]{:S(2)}, u32[]{:S(2)}) collective-permute-start(bf16[4,2,256,128]{3,2,1,0:T(8,128)(2,1)S(1)} %get-tuple-element.73), channel_id=1, source_target_pairs={{0,24},{4,28},{8,16},{12,20},{16,8},{20,12},{24,0},{28,4},{32,56},... | collective-permute-start | bytes 1572872 | tf_op jit(solution)/shard_map/ppermute | solution.py:480
  113.8 14.2 %copy-start.14 = (bf16[2,160,1024]{2,1,0:T(8,128)(2,1)}, bf16[2,160,1024]{2,1,0:T(8,128)(2,1)S(1)}, u32[]{:S(2)}) copy-start(bf16[2,160,1024]{2,1,0:T(8,128)(2,1)S(1)} %collective-permute-done.7.left_ref) | copy-start | bytes 1966084
  113.8 10.7 %collective-permute-start.12 = (bf16[4,2,256,128]{3,2,1,0:T(8,128)(2,1)S(1)}, bf16[4,2,256,128]{3,2,1,0:T(8,128)(2,1)S(1)}, u32[]{:S(2)}, u32[]{:S(2)}) collective-permute-start(bf16[4,2,256,128]{3,2,1,0:T(8,128)(2,1)S(1)} %get-tuple-element.74), channel_id=1, source_target_pairs={{0,8},{4,12},{8,0},{12,4},{16,24},{20,28},{24,16},{28,20},{32,40},... | collective-permute-start | bytes 1572872 | tf_op jit(solution)/shard_map/ppermute | solution.py:480
  114.5 13.6 %copy-start.15 = (bf16[2,160,1024]{2,1,0:T(8,128)(2,1)}, bf16[2,160,1024]{2,1,0:T(8,128)(2,1)S(1)}, u32[]{:S(2)}) copy-start(bf16[2,160,1024]{2,1,0:T(8,128)(2,1)S(1)} %collective-permute-done.8.right_ref) | copy-start | bytes 1966084
  114.5 15.5 %collective-permute-start.14 = (bf16[256,1024]{1,0:T(8,128)(2,1)S(1)}, bf16[256,1024]{1,0:T(8,128)(2,1)S(1)}, u32[]{:S(2)}, u32[]{:S(2)}) collective-permute-start(bf16[256,1024]{1,0:T(8,128)(2,1)S(1)} %get-tuple-element.81), channel_id=1, source_target_pairs={{0,1},{1,0},{2,3},{3,2},{4,5},{5,4},{6,7},{7,6},{8,9},{9,8},{10,11... | collective-permute-start | bytes 1572872 | tf_op jit(solution)/shard_map/ppermute | solution.py:480
  120.4 7.6 %copy-start.6 = (bf16[4,2,256,128]{3,2,1,0:T(8,128)(2,1)}, bf16[4,2,256,128]{3,2,1,0:T(8,128)(2,1)S(1)}, u32[]{:S(2)}) copy-start(bf16[4,2,256,128]{3,2,1,0:T(8,128)(2,1)S(1)} %collective-permute-done.9.refs_16_.refs_12_) | copy-start | bytes 1572868
  120.4 9.6 %collective-permute-start.13 = (bf16[256,1024]{1,0:T(8,128)(2,1)S(1)}, bf16[256,1024]{1,0:T(8,128)(2,1)S(1)}, u32[]{:S(2)}, u32[]{:S(2)}) collective-permute-start(bf16[256,1024]{1,0:T(8,128)(2,1)S(1)} %get-tuple-element.69), channel_id=1, source_target_pairs={{0,1},{1,0},{2,3},{3,2},{4,5},{5,4},{6,7},{7,6},{8,9},{9,8},{10,11... | collective-permute-start | bytes 1572872 | tf_op jit(solution)/shard_map/ppermute | solution.py:480
  121.9 8.1 %copy-start.12 = (bf16[512,1024]{1,0:T(8,128)(2,1)S(1)}, bf16[512,1024]{1,0:T(8,128)(2,1)}, u32[]{:S(2)}) copy-start(bf16[512,1024]{1,0:T(8,128)(2,1)} %get-tuple-element.80) | copy-start | bytes 3145732
  121.9 50.4 %collective-permute-start.2 = (bf16[512,1024]{1,0:T(8,128)(2,1)}, bf16[512,1024]{1,0:T(8,128)(2,1)}, u32[]{:S(2)}, u32[]{:S(2)}) collective-permute-start(bf16[512,1024]{1,0:T(8,128)(2,1)} %get-tuple-element.67), channel_id=1, source_target_pairs={{0,1},{1,0},{2,3},{3,2},{4,5},{5,4},{6,7},{7,6},{8,9},{9,8},{10,11... | collective-permute-start | bytes 3145736 | tf_op jit(solution)/shard_map/ppermute | solution.py:480
  128.1 11.8 %collective-permute-start.16 = (bf16[2,2,512,128]{3,2,1,0:T(8,128)(2,1)S(1)}, bf16[2,2,512,128]{3,2,1,0:T(8,128)(2,1)S(1)}, u32[]{:S(2)}, u32[]{:S(2)}) collective-permute-start(bf16[2,2,512,128]{3,2,1,0:T(8,128)(2,1)S(1)} %get-tuple-element.78), channel_id=1, source_target_pairs={{0,8},{4,12},{8,0},{12,4},{16,24},{20,28},{24,16},{28,20},{32,40},... | collective-permute-start | bytes 1572872 | tf_op jit(solution)/shard_map/ppermute | solution.py:480
  128.9 12.3 %collective-permute-start.17 = (bf16[2,2,512,128]{3,2,1,0:T(8,128)(2,1)S(1)}, bf16[2,2,512,128]{3,2,1,0:T(8,128)(2,1)S(1)}, u32[]{:S(2)}, u32[]{:S(2)}) collective-permute-start(bf16[2,2,512,128]{3,2,1,0:T(8,128)(2,1)S(1)} %get-tuple-element.79), channel_id=1, source_target_pairs={{0,96},{4,100},{8,104},{12,108},{16,112},{20,116},{24,120},{28,124... | collective-permute-start | bytes 1572872 | tf_op jit(solution)/shard_map/ppermute | solution.py:480
  130.4 41.9 %collective-permute-start.15 = (bf16[512,1024]{1,0:T(8,128)(2,1)S(1)}, bf16[512,1024]{1,0:T(8,128)(2,1)}, u32[]{:S(2)}, u32[]{:S(2)}) collective-permute-start(bf16[512,1024]{1,0:T(8,128)(2,1)S(1)} %add_convert_fusion.1), channel_id=1, source_target_pairs={{0,2},{1,3},{2,0},{3,1},{4,6},{5,7},{6,4},{7,5},{8,10},{9,11},{10,... | collective-permute-start | bytes 3145736 | tf_op jit(solution)/shard_map/ppermute | solution.py:480
  144.1 11.4 %collective-permute-start.18 = (bf16[1,2,512,128]{3,2,1,0:T(8,128)(2,1)S(1)}, bf16[1,2,512,128]{3,2,1,0:T(8,128)(2,1)S(1)}, u32[]{:S(2)}, u32[]{:S(2)}) collective-permute-start(bf16[1,2,512,128]{3,2,1,0:T(8,128)(2,1)S(1)} %get-tuple-element.89), channel_id=1, source_target_pairs={{0,24},{4,28},{8,16},{12,20},{16,8},{20,12},{24,0},{28,4},{32,56},... | collective-permute-start | bytes 786440 | tf_op jit(solution)/shard_map/ppermute | solution.py:480
  144.8 10.7 %collective-permute-start.19 = (bf16[1,2,512,128]{3,2,1,0:T(8,128)(2,1)S(1)}, bf16[1,2,512,128]{3,2,1,0:T(8,128)(2,1)S(1)}, u32[]{:S(2)}, u32[]{:S(2)}) collective-permute-start(bf16[1,2,512,128]{3,2,1,0:T(8,128)(2,1)S(1)} %get-tuple-element.90), channel_id=1, source_target_pairs={{0,32},{4,36},{8,40},{12,44},{16,48},{20,52},{24,56},{28,60},{32,0... | collective-permute-start | bytes 786440 | tf_op jit(solution)/shard_map/ppermute | solution.py:480
  145.8 20.3 %all-to-all-start.1 = ((bf16[32,2,2,1024]{3,2,1,0:T(2,128)(2,1)}), bf16[32,2,2,1024]{3,2,1,0:T(2,128)(2,1)S(1)}, u32[]{:S(2)}, u32[]{:S(2)}) async-start(bf16[32,2,2,1024]{3,2,1,0:T(2,128)(2,1)} %bitcast.7), calls=%async_computation.1 | async-start | bytes 524288 | tf_op jit(solution)/shard_map/all_to_all | solution.py:569
  158.7 12.8 %collective-permute-start.20 = (bf16[1024,128]{1,0:T(8,128)(2,1)S(1)}, bf16[1024,128]{1,0:T(8,128)(2,1)S(1)}, u32[]{:S(2)}, u32[]{:S(2)}) collective-permute-start(bf16[1024,128]{1,0:T(8,128)(2,1)S(1)} %get-tuple-element.92), channel_id=1, source_target_pairs={{0,4},{4,0},{8,12},{12,8},{16,20},{20,16},{24,28},{28,24},{32,36},... | collective-permute-start | bytes 786440 | tf_op jit(solution)/shard_map/ppermute | solution.py:480
  (10 other events, 38.8 us)
